TPU v7x, 128 devices: a whole 4x4x4 slice. The times are simulated.
128 devices in a mesh: row: 8 (over z, y_hi), col: 16 (over x, y_lo, core).
Axes of the slice: x: 4, y: 4 (y_hi: 2, y_lo: 2; y = y_hi * 2 + y_lo), z: 4, core: 2. Of those that a mesh axis runs over, the one named last changes fastest.
Arguments:
- rhs: float32 [4096, 128], P(('row', 'col')), may hold values from -8 to 8
- diag_vals: float32 [4096, 128], P(('row', 'col')), may hold values from 2 to 6
- tiles: float32 [128, 16, 4, 128, 128], P(('row', 'col')), may hold values from -0.1875 to 0.1875
- tile_row: int32 [128, 16, 4], P(('row', 'col')), may hold values from 0 to 31
- tile_col: int32 [128, 16, 4], P(('row', 'col')), may hold values from 0 to 255
Outputs:
- pressure: float32 [4096, 128], P(('row', 'col'))
- residual: float32 [4096, 128], P(('row', 'col'))
All inputs are finite; a program needn't handle non-finite values.
Results may differ from a plain program's by a relative error of at most 0.0001.
Values sent between devices are 32-bit elements; how exact they have to be, the bound alone decides.
No kernel may reach another device: no remote copies, remote signals or barrier semaphores. Data moves between devices by JAX's collectives and lax.ppermute only.
A program may use at most 64 MiB of HBM per device.

v0:
```python
import jax
import jax.numpy as jnp
from jax import lax
from jax.sharding import PartitionSpec as P

ITERS = 16


centre = 4.0
half_width = 3.96


def in_order(parts, dim):
    parts = jnp.moveaxis(parts, 0, dim)
    shape = parts.shape
    return parts.reshape(*shape[:dim], shape[dim] * shape[dim + 1], *shape[dim + 2 :])


def sent_to_all(x, axis):
    size = lax.axis_size(axis)
    return lax.all_to_all(jnp.broadcast_to(x[None], (size, *x.shape)), axis, 0, 0, tiled=True)


def gathered_copies(x, axis, dim):
    return in_order(sent_to_all(x, axis), dim)


def in_blocks(x, dim, size):
    before, after = (x.shape[:dim], x.shape[dim + 1 :])
    return jnp.moveaxis(x.reshape(*before, size, -1, *after), dim, 0)


def sent_and_summed(x, axis, dim):
    size = lax.axis_size(axis)
    parts = lax.all_to_all(in_blocks(x, dim, size), axis, 0, 0, tiled=True)
    return jnp.sum(parts, axis=0)


def local_product(tile_block, row_local, col_local, vec, out_rows):
    order = tile_block.shape[-1]
    flat = tile_block.reshape(-1, order, order)
    picked = vec[col_local.reshape(-1)]
    prod = jnp.einsum("tij,tj->ti", flat, picked, precision=lax.Precision.HIGHEST)
    target = row_local.reshape(-1)
    onehot = (jnp.arange(out_rows, dtype=jnp.int32)[:, None] == target[None, :]).astype(jnp.float32)
    return jnp.dot(onehot, prod, precision=lax.Precision.HIGHEST)


def per_device(rhs, diag_vals, tiles, tile_row, tile_col):
    width = lax.axis_size("col")
    owned = rhs.shape[0]
    moved = lax.all_to_all(tiles[0], "col", split_axis=0, concat_axis=0, tiled=True)
    pattern = jnp.stack([tile_row[0], tile_col[0]], 0)
    moved_pattern = lax.all_to_all(pattern, "col", split_axis=1, concat_axis=1, tiled=True)
    row_local = moved_pattern[0] + (jnp.arange(width, dtype=jnp.int32) * owned)[:, None]
    col_local = moved_pattern[1]

    def off_apply(vec):
        column = gathered_copies(vec, "row", 0)
        partial_rows = local_product(moved, row_local, col_local, column, width * owned)
        return sent_and_summed(partial_rows, "col", 0)

    def operate(vec):
        return diag_vals * vec - off_apply(vec)

    sigma = centre / half_width

    def advance(index, carry):
        pressure, residual, direction, rho = carry
        pressure = pressure + direction
        residual = residual - operate(direction)
        rho_new = 1.0 / (2.0 * sigma - rho)
        direction = rho_new * rho * direction + 2.0 * rho_new / half_width * residual
        return (pressure, residual, direction, rho_new)

    start = (jnp.zeros_like(rhs), rhs, rhs / centre, jnp.asarray(1.0 / sigma, dtype=jnp.float32))
    pressure, residual, direction, rho = lax.fori_loop(0, ITERS, advance, start)
    return (pressure, residual)


def solution(mesh):
    return jax.shard_map(
        per_device,
        mesh=mesh,
        in_specs=(
            P(("row", "col"), None),
            P(("row", "col"), None),
            P(("row", "col"), None, None, None, None),
            P(("row", "col"), None, None),
            P(("row", "col"), None, None),
        ),
        out_specs=(P(("row", "col"), None), P(("row", "col"), None)),
        check_vma=False,
    )
```

profile of v0, /device:TPU:1, one launch (start us, length us, event | category | flops | bytes accessed | tf_op | source)
XLA Modules:
  0.0 616.1 jit_solution(6213167487070188003)
XLA Ops:
  2.1 12.4 %all_to_all.32 = s32[2,16,4]{2,0,1:T(2,128)S(1)} all-to-all(s32[2,16,4]{2,0,1:T(2,128)S(1)} %copy.15), channel_id=1, replica_groups=mesh['row'=8,'col'=16] {'col'}, dimensions={1} | all-to-all | bytes 1024 | tf_op jit(solution)/shard_map/all_to_all | solution.py:54
  19.8 52.2 %all-to-all-done.3 = f32[16,4,128,128]{3,2,1,0:T(8,128)} async-done(((f32[16,4,128,128]{3,2,1,0:T(8,128)}), f32[16,4,128,128]{3,2,1,0:T(8,128)}, u32[]{:S(2)}, u32[]{:S(2)}) %all-to-all-start.3) | async-done | bytes 4194336 | tf_op jit(solution)/shard_map/all_to_all | solution.py:52
  72.0 543.4 %while.20 = (s32[]{:T(128)}, f32[32,128]{1,0:T(8,128)S(1)}, f32[32,128]{1,0:T(8,128)S(1)}, f32[32,128]{1,0:T(8,128)S(1)}, f32[]{:T(128)}, /*index=5*/f32[32,128]...) while((s32[]{:T(128)}, f32[32,128]{1,0:T(8,128)S(1)}, ...), condition=%wide.wide.region_2.0_spmd.clone, body=%wide.wide.region_0.0_spmd.clone.sunk | while | flops 63042756 | bytes 6362667 | solution.py:77
  72.7 7.4 %all-to-all-start = ((f32[8,32,128]{2,1,0:T(8,128)}), f32[8,32,128]{2,1,0:T(8,128)S(1)}, u32[]{:S(2)}, u32[]{:S(2)}) async-start(f32[8,32,128]{2,1,0:T(8,128)} %broadcast_in_dim.19), calls=%async_computation | async-start | bytes 262144 | tf_op jit(solution)/shard_map/while/body/eval_jaxpr/all_to_all | solution.py:21
  80.1 7.4 %all-to-all-done = f32[8,32,128]{2,1,0:T(8,128)S(1)} async-done(((f32[8,32,128]{2,1,0:T(8,128)}), f32[8,32,128]{2,1,0:T(8,128)S(1)}, u32[]{:S(2)}, u32[]{:S(2)}) %all-to-all-start) | async-done | bytes 131104 | tf_op jit(solution)/shard_map/while/body/eval_jaxpr/all_to_all | solution.py:21
  88.1 8.3 %fusion.24 = f32[64,1,128]{2,1,0:T(1,128)S(1)} fusion(f32[64,128,1]{1,2,0:T(1,128)S(1)} %bitcast.46, f32[64,128,128]{2,1,0:T(8,128)} %bitcast.41), kind=kOutput, calls=%fused_computation.15.clone.clone.1 | convolution fusion | flops 12582912 | bytes 4259840 | tf_op jit(solution)/shard_map/while/body/eval_jaxpr/tij,tj->ti/dot_general | solution.py:43
  97.4 11.5 %all-to-all-start.1 = ((f32[16,32,128]{2,1,0:T(8,128)}), f32[16,32,128]{2,1,0:T(8,128)S(1)}, u32[]{:S(2)}, u32[]{:S(2)}) async-start(f32[16,32,128]{2,1,0:T(8,128)} %bitcast.43), calls=%async_computation.1 | async-start | bytes 524288 | tf_op jit(solution)/shard_map/while/body/eval_jaxpr/all_to_all | solution.py:35
  108.9 7.3 %all-to-all-done.1 = f32[16,32,128]{2,1,0:T(8,128)S(1)} async-done(((f32[16,32,128]{2,1,0:T(8,128)}), f32[16,32,128]{2,1,0:T(8,128)S(1)}, u32[]{:S(2)}, u32[]{:S(2)}) %all-to-all-start.1) | async-done | bytes 262176 | tf_op jit(solution)/shard_map/while/body/eval_jaxpr/all_to_all | solution.py:35
  120.3 7.0 %all-to-all-done = f32[8,32,128]{2,1,0:T(8,128)S(1)} async-done(((f32[8,32,128]{2,1,0:T(8,128)}), f32[8,32,128]{2,1,0:T(8,128)S(1)}, u32[]{:S(2)}, u32[]{:S(2)}) %all-to-all-start) | async-done | bytes 131104 | tf_op jit(solution)/shard_map/while/body/eval_jaxpr/all_to_all | solution.py:21
  127.9 8.3 %fusion.24 = f32[64,1,128]{2,1,0:T(1,128)S(1)} fusion(f32[64,128,1]{1,2,0:T(1,128)S(1)} %bitcast.46, f32[64,128,128]{2,1,0:T(8,128)} %bitcast.41), kind=kOutput, calls=%fused_computation.15.clone.clone.1 | convolution fusion | flops 12582912 | bytes 4259840 | tf_op jit(solution)/shard_map/while/body/eval_jaxpr/tij,tj->ti/dot_general | solution.py:43
  142.1 7.4 %all-to-all-done.1 = f32[16,32,128]{2,1,0:T(8,128)S(1)} async-done(((f32[16,32,128]{2,1,0:T(8,128)}), f32[16,32,128]{2,1,0:T(8,128)S(1)}, u32[]{:S(2)}, u32[]{:S(2)}) %all-to-all-start.1) | async-done | bytes 262176 | tf_op jit(solution)/shard_map/while/body/eval_jaxpr/all_to_all | solution.py:35
  153.6 7.0 %all-to-all-done = f32[8,32,128]{2,1,0:T(8,128)S(1)} async-done(((f32[8,32,128]{2,1,0:T(8,128)}), f32[8,32,128]{2,1,0:T(8,128)S(1)}, u32[]{:S(2)}, u32[]{:S(2)}) %all-to-all-start) | async-done | bytes 131104 | tf_op jit(solution)/shard_map/while/body/eval_jaxpr/all_to_all | solution.py:21
  161.1 8.3 %fusion.24 = f32[64,1,128]{2,1,0:T(1,128)S(1)} fusion(f32[64,128,1]{1,2,0:T(1,128)S(1)} %bitcast.46, f32[64,128,128]{2,1,0:T(8,128)} %bitcast.41), kind=kOutput, calls=%fused_computation.15.clone.clone.1 | convolution fusion | flops 12582912 | bytes 4259840 | tf_op jit(solution)/shard_map/while/body/eval_jaxpr/tij,tj->ti/dot_general | solution.py:43
  170.4 4.9 all-to-all-start.1
  175.3 7.4 %all-to-all-done.1 = f32[16,32,128]{2,1,0:T(8,128)S(1)} async-done(((f32[16,32,128]{2,1,0:T(8,128)}), f32[16,32,128]{2,1,0:T(8,128)S(1)}, u32[]{:S(2)}, u32[]{:S(2)}) %all-to-all-start.1) | async-done | bytes 262176 | tf_op jit(solution)/shard_map/while/body/eval_jaxpr/all_to_all | solution.py:35
  186.9 7.0 %all-to-all-done = f32[8,32,128]{2,1,0:T(8,128)S(1)} async-done(((f32[8,32,128]{2,1,0:T(8,128)}), f32[8,32,128]{2,1,0:T(8,128)S(1)}, u32[]{:S(2)}, u32[]{:S(2)}) %all-to-all-start) | async-done | bytes 131104 | tf_op jit(solution)/shard_map/while/body/eval_jaxpr/all_to_all | solution.py:21
  194.4 8.3 %fusion.24 = f32[64,1,128]{2,1,0:T(1,128)S(1)} fusion(f32[64,128,1]{1,2,0:T(1,128)S(1)} %bitcast.46, f32[64,128,128]{2,1,0:T(8,128)} %bitcast.41), kind=kOutput, calls=%fused_computation.15.clone.clone.1 | convolution fusion | flops 12582912 | bytes 4259840 | tf_op jit(solution)/shard_map/while/body/eval_jaxpr/tij,tj->ti/dot_general | solution.py:43
  203.7 4.9 all-to-all-start.1
  208.6 7.4 %all-to-all-done.1 = f32[16,32,128]{2,1,0:T(8,128)S(1)} async-done(((f32[16,32,128]{2,1,0:T(8,128)}), f32[16,32,128]{2,1,0:T(8,128)S(1)}, u32[]{:S(2)}, u32[]{:S(2)}) %all-to-all-start.1) | async-done | bytes 262176 | tf_op jit(solution)/shard_map/while/body/eval_jaxpr/all_to_all | solution.py:35
  220.1 7.0 %all-to-all-done = f32[8,32,128]{2,1,0:T(8,128)S(1)} async-done(((f32[8,32,128]{2,1,0:T(8,128)}), f32[8,32,128]{2,1,0:T(8,128)S(1)}, u32[]{:S(2)}, u32[]{:S(2)}) %all-to-all-start) | async-done | bytes 131104 | tf_op jit(solution)/shard_map/while/body/eval_jaxpr/all_to_all | solution.py:21
  227.7 8.3 %fusion.24 = f32[64,1,128]{2,1,0:T(1,128)S(1)} fusion(f32[64,128,1]{1,2,0:T(1,128)S(1)} %bitcast.46, f32[64,128,128]{2,1,0:T(8,128)} %bitcast.41), kind=kOutput, calls=%fused_computation.15.clone.clone.1 | convolution fusion | flops 12582912 | bytes 4259840 | tf_op jit(solution)/shard_map/while/body/eval_jaxpr/tij,tj->ti/dot_general | solution.py:43
  237.0 4.9 all-to-all-start.1
  241.9 7.4 %all-to-all-done.1 = f32[16,32,128]{2,1,0:T(8,128)S(1)} async-done(((f32[16,32,128]{2,1,0:T(8,128)}), f32[16,32,128]{2,1,0:T(8,128)S(1)}, u32[]{:S(2)}, u32[]{:S(2)}) %all-to-all-start.1) | async-done | bytes 262176 | tf_op jit(solution)/shard_map/while/body/eval_jaxpr/all_to_all | solution.py:35
  253.4 7.0 %all-to-all-done = f32[8,32,128]{2,1,0:T(8,128)S(1)} async-done(((f32[8,32,128]{2,1,0:T(8,128)}), f32[8,32,128]{2,1,0:T(8,128)S(1)}, u32[]{:S(2)}, u32[]{:S(2)}) %all-to-all-start) | async-done | bytes 131104 | tf_op jit(solution)/shard_map/while/body/eval_jaxpr/all_to_all | solution.py:21
  261.0 8.3 %fusion.24 = f32[64,1,128]{2,1,0:T(1,128)S(1)} fusion(f32[64,128,1]{1,2,0:T(1,128)S(1)} %bitcast.46, f32[64,128,128]{2,1,0:T(8,128)} %bitcast.41), kind=kOutput, calls=%fused_computation.15.clone.clone.1 | convolution fusion | flops 12582912 | bytes 4259840 | tf_op jit(solution)/shard_map/while/body/eval_jaxpr/tij,tj->ti/dot_general | solution.py:43
  275.2 7.4 %all-to-all-done.1 = f32[16,32,128]{2,1,0:T(8,128)S(1)} async-done(((f32[16,32,128]{2,1,0:T(8,128)}), f32[16,32,128]{2,1,0:T(8,128)S(1)}, u32[]{:S(2)}, u32[]{:S(2)}) %all-to-all-start.1) | async-done | bytes 262176 | tf_op jit(solution)/shard_map/while/body/eval_jaxpr/all_to_all | solution.py:35
  286.7 7.0 %all-to-all-done = f32[8,32,128]{2,1,0:T(8,128)S(1)} async-done(((f32[8,32,128]{2,1,0:T(8,128)}), f32[8,32,128]{2,1,0:T(8,128)S(1)}, u32[]{:S(2)}, u32[]{:S(2)}) %all-to-all-start) | async-done | bytes 131104 | tf_op jit(solution)/shard_map/while/body/eval_jaxpr/all_to_all | solution.py:21
  294.2 8.3 %fusion.24 = f32[64,1,128]{2,1,0:T(1,128)S(1)} fusion(f32[64,128,1]{1,2,0:T(1,128)S(1)} %bitcast.46, f32[64,128,128]{2,1,0:T(8,128)} %bitcast.41), kind=kOutput, calls=%fused_computation.15.clone.clone.1 | convolution fusion | flops 12582912 | bytes 4259840 | tf_op jit(solution)/shard_map/while/body/eval_jaxpr/tij,tj->ti/dot_general | solution.py:43
  303.5 4.9 all-to-all-start.1
  308.5 7.4 %all-to-all-done.1 = f32[16,32,128]{2,1,0:T(8,128)S(1)} async-done(((f32[16,32,128]{2,1,0:T(8,128)}), f32[16,32,128]{2,1,0:T(8,128)S(1)}, u32[]{:S(2)}, u32[]{:S(2)}) %all-to-all-start.1) | async-done | bytes 262176 | tf_op jit(solution)/shard_map/while/body/eval_jaxpr/all_to_all | solution.py:35
  320.0 7.0 %all-to-all-done = f32[8,32,128]{2,1,0:T(8,128)S(1)} async-done(((f32[8,32,128]{2,1,0:T(8,128)}), f32[8,32,128]{2,1,0:T(8,128)S(1)}, u32[]{:S(2)}, u32[]{:S(2)}) %all-to-all-start) | async-done | bytes 131104 | tf_op jit(solution)/shard_map/while/body/eval_jaxpr/all_to_all | solution.py:21
  327.5 8.3 %fusion.24 = f32[64,1,128]{2,1,0:T(1,128)S(1)} fusion(f32[64,128,1]{1,2,0:T(1,128)S(1)} %bitcast.46, f32[64,128,128]{2,1,0:T(8,128)} %bitcast.41), kind=kOutput, calls=%fused_computation.15.clone.clone.1 | convolution fusion | flops 12582912 | bytes 4259840 | tf_op jit(solution)/shard_map/while/body/eval_jaxpr/tij,tj->ti/dot_general | solution.py:43
  336.8 4.9 all-to-all-start.1
  341.8 7.4 %all-to-all-done.1 = f32[16,32,128]{2,1,0:T(8,128)S(1)} async-done(((f32[16,32,128]{2,1,0:T(8,128)}), f32[16,32,128]{2,1,0:T(8,128)S(1)}, u32[]{:S(2)}, u32[]{:S(2)}) %all-to-all-start.1) | async-done | bytes 262176 | tf_op jit(solution)/shard_map/while/body/eval_jaxpr/all_to_all | solution.py:35
  353.3 7.0 %all-to-all-done = f32[8,32,128]{2,1,0:T(8,128)S(1)} async-done(((f32[8,32,128]{2,1,0:T(8,128)}), f32[8,32,128]{2,1,0:T(8,128)S(1)}, u32[]{:S(2)}, u32[]{:S(2)}) %all-to-all-start) | async-done | bytes 131104 | tf_op jit(solution)/shard_map/while/body/eval_jaxpr/all_to_all | solution.py:21
  360.8 8.3 %fusion.24 = f32[64,1,128]{2,1,0:T(1,128)S(1)} fusion(f32[64,128,1]{1,2,0:T(1,128)S(1)} %bitcast.46, f32[64,128,128]{2,1,0:T(8,128)} %bitcast.41), kind=kOutput, calls=%fused_computation.15.clone.clone.1 | convolution fusion | flops 12582912 | bytes 4259840 | tf_op jit(solution)/shard_map/while/body/eval_jaxpr/tij,tj->ti/dot_general | solution.py:43
  375.0 7.4 %all-to-all-done.1 = f32[16,32,128]{2,1,0:T(8,128)S(1)} async-done(((f32[16,32,128]{2,1,0:T(8,128)}), f32[16,32,128]{2,1,0:T(8,128)S(1)}, u32[]{:S(2)}, u32[]{:S(2)}) %all-to-all-start.1) | async-done | bytes 262176 | tf_op jit(solution)/shard_map/while/body/eval_jaxpr/all_to_all | solution.py:35
  386.5 7.0 %all-to-all-done = f32[8,32,128]{2,1,0:T(8,128)S(1)} async-done(((f32[8,32,128]{2,1,0:T(8,128)}), f32[8,32,128]{2,1,0:T(8,128)S(1)}, u32[]{:S(2)}, u32[]{:S(2)}) %all-to-all-start) | async-done | bytes 131104 | tf_op jit(solution)/shard_map/while/body/eval_jaxpr/all_to_all | solution.py:21
  394.1 8.3 %fusion.24 = f32[64,1,128]{2,1,0:T(1,128)S(1)} fusion(f32[64,128,1]{1,2,0:T(1,128)S(1)} %bitcast.46, f32[64,128,128]{2,1,0:T(8,128)} %bitcast.41), kind=kOutput, calls=%fused_computation.15.clone.clone.1 | convolution fusion | flops 12582912 | bytes 4259840 | tf_op jit(solution)/shard_map/while/body/eval_jaxpr/tij,tj->ti/dot_general | solution.py:43
  403.4 4.9 all-to-all-start.1
  408.3 7.4 %all-to-all-done.1 = f32[16,32,128]{2,1,0:T(8,128)S(1)} async-done(((f32[16,32,128]{2,1,0:T(8,128)}), f32[16,32,128]{2,1,0:T(8,128)S(1)}, u32[]{:S(2)}, u32[]{:S(2)}) %all-to-all-start.1) | async-done | bytes 262176 | tf_op jit(solution)/shard_map/while/body/eval_jaxpr/all_to_all | solution.py:35
  419.8 7.0 %all-to-all-done = f32[8,32,128]{2,1,0:T(8,128)S(1)} async-done(((f32[8,32,128]{2,1,0:T(8,128)}), f32[8,32,128]{2,1,0:T(8,128)S(1)}, u32[]{:S(2)}, u32[]{:S(2)}) %all-to-all-start) | async-done | bytes 131104 | tf_op jit(solution)/shard_map/while/body/eval_jaxpr/all_to_all | solution.py:21
  427.4 8.3 %fusion.24 = f32[64,1,128]{2,1,0:T(1,128)S(1)} fusion(f32[64,128,1]{1,2,0:T(1,128)S(1)} %bitcast.46, f32[64,128,128]{2,1,0:T(8,128)} %bitcast.41), kind=kOutput, calls=%fused_computation.15.clone.clone.1 | convolution fusion | flops 12582912 | bytes 4259840 | tf_op jit(solution)/shard_map/while/body/eval_jaxpr/tij,tj->ti/dot_general | solution.py:43
  436.7 4.9 all-to-all-start.1
  441.6 7.4 %all-to-all-done.1 = f32[16,32,128]{2,1,0:T(8,128)S(1)} async-done(((f32[16,32,128]{2,1,0:T(8,128)}), f32[16,32,128]{2,1,0:T(8,128)S(1)}, u32[]{:S(2)}, u32[]{:S(2)}) %all-to-all-start.1) | async-done | bytes 262176 | tf_op jit(solution)/shard_map/while/body/eval_jaxpr/all_to_all | solution.py:35
  453.1 7.0 %all-to-all-done = f32[8,32,128]{2,1,0:T(8,128)S(1)} async-done(((f32[8,32,128]{2,1,0:T(8,128)}), f32[8,32,128]{2,1,0:T(8,128)S(1)}, u32[]{:S(2)}, u32[]{:S(2)}) %all-to-all-start) | async-done | bytes 131104 | tf_op jit(solution)/shard_map/while/body/eval_jaxpr/all_to_all | solution.py:21
  460.7 8.3 %fusion.24 = f32[64,1,128]{2,1,0:T(1,128)S(1)} fusion(f32[64,128,1]{1,2,0:T(1,128)S(1)} %bitcast.46, f32[64,128,128]{2,1,0:T(8,128)} %bitcast.41), kind=kOutput, calls=%fused_computation.15.clone.clone.1 | convolution fusion | flops 12582912 | bytes 4259840 | tf_op jit(solution)/shard_map/while/body/eval_jaxpr/tij,tj->ti/dot_general | solution.py:43
  469.9 4.9 all-to-all-start.1
  474.9 7.4 %all-to-all-done.1 = f32[16,32,128]{2,1,0:T(8,128)S(1)} async-done(((f32[16,32,128]{2,1,0:T(8,128)}), f32[16,32,128]{2,1,0:T(8,128)S(1)}, u32[]{:S(2)}, u32[]{:S(2)}) %all-to-all-start.1) | async-done | bytes 262176 | tf_op jit(solution)/shard_map/while/body/eval_jaxpr/all_to_all | solution.py:35
  486.4 7.0 %all-to-all-done = f32[8,32,128]{2,1,0:T(8,128)S(1)} async-done(((f32[8,32,128]{2,1,0:T(8,128)}), f32[8,32,128]{2,1,0:T(8,128)S(1)}, u32[]{:S(2)}, u32[]{:S(2)}) %all-to-all-start) | async-done | bytes 131104 | tf_op jit(solution)/shard_map/while/body/eval_jaxpr/all_to_all | solution.py:21
  493.9 8.3 %fusion.24 = f32[64,1,128]{2,1,0:T(1,128)S(1)} fusion(f32[64,128,1]{1,2,0:T(1,128)S(1)} %bitcast.46, f32[64,128,128]{2,1,0:T(8,128)} %bitcast.41), kind=kOutput, calls=%fused_computation.15.clone.clone.1 | convolution fusion | flops 12582912 | bytes 4259840 | tf_op jit(solution)/shard_map/while/body/eval_jaxpr/tij,tj->ti/dot_general | solution.py:43
  503.2 4.9 all-to-all-start.1
  508.2 7.4 %all-to-all-done.1 = f32[16,32,128]{2,1,0:T(8,128)S(1)} async-done(((f32[16,32,128]{2,1,0:T(8,128)}), f32[16,32,128]{2,1,0:T(8,128)S(1)}, u32[]{:S(2)}, u32[]{:S(2)}) %all-to-all-start.1) | async-done | bytes 262176 | tf_op jit(solution)/shard_map/while/body/eval_jaxpr/all_to_all | solution.py:35
  519.7 7.0 %all-to-all-done = f32[8,32,128]{2,1,0:T(8,128)S(1)} async-done(((f32[8,32,128]{2,1,0:T(8,128)}), f32[8,32,128]{2,1,0:T(8,128)S(1)}, u32[]{:S(2)}, u32[]{:S(2)}) %all-to-all-start) | async-done | bytes 131104 | tf_op jit(solution)/shard_map/while/body/eval_jaxpr/all_to_all | solution.py:21
  527.2 8.3 %fusion.24 = f32[64,1,128]{2,1,0:T(1,128)S(1)} fusion(f32[64,128,1]{1,2,0:T(1,128)S(1)} %bitcast.46, f32[64,128,128]{2,1,0:T(8,128)} %bitcast.41), kind=kOutput, calls=%fused_computation.15.clone.clone.1 | convolution fusion | flops 12582912 | bytes 4259840 | tf_op jit(solution)/shard_map/while/body/eval_jaxpr/tij,tj->ti/dot_general | solution.py:43
  536.5 4.9 all-to-all-start.1
  541.5 7.4 %all-to-all-done.1 = f32[16,32,128]{2,1,0:T(8,128)S(1)} async-done(((f32[16,32,128]{2,1,0:T(8,128)}), f32[16,32,128]{2,1,0:T(8,128)S(1)}, u32[]{:S(2)}, u32[]{:S(2)}) %all-to-all-start.1) | async-done | bytes 262176 | tf_op jit(solution)/shard_map/while/body/eval_jaxpr/all_to_all | solution.py:35
  553.0 7.0 %all-to-all-done = f32[8,32,128]{2,1,0:T(8,128)S(1)} async-done(((f32[8,32,128]{2,1,0:T(8,128)}), f32[8,32,128]{2,1,0:T(8,128)S(1)}, u32[]{:S(2)}, u32[]{:S(2)}) %all-to-all-start) | async-done | bytes 131104 | tf_op jit(solution)/shard_map/while/body/eval_jaxpr/all_to_all | solution.py:21
  560.5 8.3 %fusion.24 = f32[64,1,128]{2,1,0:T(1,128)S(1)} fusion(f32[64,128,1]{1,2,0:T(1,128)S(1)} %bitcast.46, f32[64,128,128]{2,1,0:T(8,128)} %bitcast.41), kind=kOutput, calls=%fused_computation.15.clone.clone.1 | convolution fusion | flops 12582912 | bytes 4259840 | tf_op jit(solution)/shard_map/while/body/eval_jaxpr/tij,tj->ti/dot_general | solution.py:43
  569.8 4.9 all-to-all-start.1
  574.7 7.4 %all-to-all-done.1 = f32[16,32,128]{2,1,0:T(8,128)S(1)} async-done(((f32[16,32,128]{2,1,0:T(8,128)}), f32[16,32,128]{2,1,0:T(8,128)S(1)}, u32[]{:S(2)}, u32[]{:S(2)}) %all-to-all-start.1) | async-done | bytes 262176 | tf_op jit(solution)/shard_map/while/body/eval_jaxpr/all_to_all | solution.py:35
  586.2 7.0 %all-to-all-done = f32[8,32,128]{2,1,0:T(8,128)S(1)} async-done(((f32[8,32,128]{2,1,0:T(8,128)}), f32[8,32,128]{2,1,0:T(8,128)S(1)}, u32[]{:S(2)}, u32[]{:S(2)}) %all-to-all-start) | async-done | bytes 131104 | tf_op jit(solution)/shard_map/while/body/eval_jaxpr/all_to_all | solution.py:21
  593.8 8.3 %fusion.24 = f32[64,1,128]{2,1,0:T(1,128)S(1)} fusion(f32[64,128,1]{1,2,0:T(1,128)S(1)} %bitcast.46, f32[64,128,128]{2,1,0:T(8,128)} %bitcast.41), kind=kOutput, calls=%fused_computation.15.clone.clone.1 | convolution fusion | flops 12582912 | bytes 4259840 | tf_op jit(solution)/shard_map/while/body/eval_jaxpr/tij,tj->ti/dot_general | solution.py:43
  608.0 7.4 %all-to-all-done.1 = f32[16,32,128]{2,1,0:T(8,128)S(1)} async-done(((f32[16,32,128]{2,1,0:T(8,128)}), f32[16,32,128]{2,1,0:T(8,128)S(1)}, u32[]{:S(2)}, u32[]{:S(2)}) %all-to-all-start.1) | async-done | bytes 262176 | tf_op jit(solution)/shard_map/while/body/eval_jaxpr/all_to_all | solution.py:35
  (154 shorter events, 113.9 us)
Async XLA Ops:
  14.5 57.4 %copy-start.1 = (f32[32,128]{1,0:T(8,128)S(1)}, f32[32,128]{1,0:T(8,128)}, u32[]{:S(2)}) copy-start(f32[32,128]{1,0:T(8,128)} %param.8) | copy-start | bytes 49156
  14.5 57.4 %all-to-all-start.3 = ((f32[16,4,128,128]{3,2,1,0:T(8,128)}), f32[16,4,128,128]{3,2,1,0:T(8,128)}, u32[]{:S(2)}, u32[]{:S(2)}) async-start(f32[16,4,128,128]{3,2,1,0:T(8,128)} %bitcast.45), calls=%async_computation.3 | async-start | bytes 8388608 | tf_op jit(solution)/shard_map/all_to_all | solution.py:52
  19.4 52.6 %copy-start.4 = (s32[1,16,4]{2,0,1:T(1,128)}, s32[1,16,4]{2,0,1:T(1,128)S(1)}, u32[]{:S(2)}) copy-start(s32[1,16,4]{2,0,1:T(1,128)S(1)} %get-tuple-element.196) | copy-start | bytes 772
  19.6 52.4 %copy-start.3 = (s32[16,4]{1,0:T(8,128)}, s32[16,4]{1,0:T(8,128)S(1)}, u32[]{:S(2)}) copy-start(s32[16,4]{1,0:T(8,128)S(1)} %copy.17) | copy-start | bytes 772
  72.7 14.8 %all-to-all-start = ((f32[8,32,128]{2,1,0:T(8,128)}), f32[8,32,128]{2,1,0:T(8,128)S(1)}, u32[]{:S(2)}, u32[]{:S(2)}) async-start(f32[8,32,128]{2,1,0:T(8,128)} %broadcast_in_dim.19), calls=%async_computation | async-start | bytes 262144 | tf_op jit(solution)/shard_map/while/body/eval_jaxpr/all_to_all | solution.py:21
  97.4 18.8 %all-to-all-start.1 = ((f32[16,32,128]{2,1,0:T(8,128)}), f32[16,32,128]{2,1,0:T(8,128)S(1)}, u32[]{:S(2)}, u32[]{:S(2)}) async-start(f32[16,32,128]{2,1,0:T(8,128)} %bitcast.43), calls=%async_computation.1 | async-start | bytes 524288 | tf_op jit(solution)/shard_map/while/body/eval_jaxpr/all_to_all | solution.py:35
  116.9 10.4 %all-to-all-start = ((f32[8,32,128]{2,1,0:T(8,128)}), f32[8,32,128]{2,1,0:T(8,128)S(1)}, u32[]{:S(2)}, u32[]{:S(2)}) async-start(f32[8,32,128]{2,1,0:T(8,128)} %broadcast_in_dim.19), calls=%async_computation | async-start | bytes 262144 | tf_op jit(solution)/shard_map/while/body/eval_jaxpr/all_to_all | solution.py:21
  137.1 12.3 %all-to-all-start.1 = ((f32[16,32,128]{2,1,0:T(8,128)}), f32[16,32,128]{2,1,0:T(8,128)S(1)}, u32[]{:S(2)}, u32[]{:S(2)}) async-start(f32[16,32,128]{2,1,0:T(8,128)} %bitcast.43), calls=%async_computation.1 | async-start | bytes 524288 | tf_op jit(solution)/shard_map/while/body/eval_jaxpr/all_to_all | solution.py:35
  150.2 10.4 %all-to-all-start = ((f32[8,32,128]{2,1,0:T(8,128)}), f32[8,32,128]{2,1,0:T(8,128)S(1)}, u32[]{:S(2)}, u32[]{:S(2)}) async-start(f32[8,32,128]{2,1,0:T(8,128)} %broadcast_in_dim.19), calls=%async_computation | async-start | bytes 262144 | tf_op jit(solution)/shard_map/while/body/eval_jaxpr/all_to_all | solution.py:21
  170.4 12.3 %all-to-all-start.1 = ((f32[16,32,128]{2,1,0:T(8,128)}), f32[16,32,128]{2,1,0:T(8,128)S(1)}, u32[]{:S(2)}, u32[]{:S(2)}) async-start(f32[16,32,128]{2,1,0:T(8,128)} %bitcast.43), calls=%async_computation.1 | async-start | bytes 524288 | tf_op jit(solution)/shard_map/while/body/eval_jaxpr/all_to_all | solution.py:35
  183.4 10.4 %all-to-all-start = ((f32[8,32,128]{2,1,0:T(8,128)}), f32[8,32,128]{2,1,0:T(8,128)S(1)}, u32[]{:S(2)}, u32[]{:S(2)}) async-start(f32[8,32,128]{2,1,0:T(8,128)} %broadcast_in_dim.19), calls=%async_computation | async-start | bytes 262144 | tf_op jit(solution)/shard_map/while/body/eval_jaxpr/all_to_all | solution.py:21
  203.7 12.3 %all-to-all-start.1 = ((f32[16,32,128]{2,1,0:T(8,128)}), f32[16,32,128]{2,1,0:T(8,128)S(1)}, u32[]{:S(2)}, u32[]{:S(2)}) async-start(f32[16,32,128]{2,1,0:T(8,128)} %bitcast.43), calls=%async_computation.1 | async-start | bytes 524288 | tf_op jit(solution)/shard_map/while/body/eval_jaxpr/all_to_all | solution.py:35
  216.7 10.4 %all-to-all-start = ((f32[8,32,128]{2,1,0:T(8,128)}), f32[8,32,128]{2,1,0:T(8,128)S(1)}, u32[]{:S(2)}, u32[]{:S(2)}) async-start(f32[8,32,128]{2,1,0:T(8,128)} %broadcast_in_dim.19), calls=%async_computation | async-start | bytes 262144 | tf_op jit(solution)/shard_map/while/body/eval_jaxpr/all_to_all | solution.py:21
  237.0 12.3 %all-to-all-start.1 = ((f32[16,32,128]{2,1,0:T(8,128)}), f32[16,32,128]{2,1,0:T(8,128)S(1)}, u32[]{:S(2)}, u32[]{:S(2)}) async-start(f32[16,32,128]{2,1,0:T(8,128)} %bitcast.43), calls=%async_computation.1 | async-start | bytes 524288 | tf_op jit(solution)/shard_map/while/body/eval_jaxpr/all_to_all | solution.py:35
  250.0 10.4 %all-to-all-start = ((f32[8,32,128]{2,1,0:T(8,128)}), f32[8,32,128]{2,1,0:T(8,128)S(1)}, u32[]{:S(2)}, u32[]{:S(2)}) async-start(f32[8,32,128]{2,1,0:T(8,128)} %broadcast_in_dim.19), calls=%async_computation | async-start | bytes 262144 | tf_op jit(solution)/shard_map/while/body/eval_jaxpr/all_to_all | solution.py:21
  270.2 12.3 %all-to-all-start.1 = ((f32[16,32,128]{2,1,0:T(8,128)}), f32[16,32,128]{2,1,0:T(8,128)S(1)}, u32[]{:S(2)}, u32[]{:S(2)}) async-start(f32[16,32,128]{2,1,0:T(8,128)} %bitcast.43), calls=%async_computation.1 | async-start | bytes 524288 | tf_op jit(solution)/shard_map/while/body/eval_jaxpr/all_to_all | solution.py:35
  283.3 10.4 %all-to-all-start = ((f32[8,32,128]{2,1,0:T(8,128)}), f32[8,32,128]{2,1,0:T(8,128)S(1)}, u32[]{:S(2)}, u32[]{:S(2)}) async-start(f32[8,32,128]{2,1,0:T(8,128)} %broadcast_in_dim.19), calls=%async_computation | async-start | bytes 262144 | tf_op jit(solution)/shard_map/while/body/eval_jaxpr/all_to_all | solution.py:21
  303.5 12.3 %all-to-all-start.1 = ((f32[16,32,128]{2,1,0:T(8,128)}), f32[16,32,128]{2,1,0:T(8,128)S(1)}, u32[]{:S(2)}, u32[]{:S(2)}) async-start(f32[16,32,128]{2,1,0:T(8,128)} %bitcast.43), calls=%async_computation.1 | async-start | bytes 524288 | tf_op jit(solution)/shard_map/while/body/eval_jaxpr/all_to_all | solution.py:35
  316.6 10.4 %all-to-all-start = ((f32[8,32,128]{2,1,0:T(8,128)}), f32[8,32,128]{2,1,0:T(8,128)S(1)}, u32[]{:S(2)}, u32[]{:S(2)}) async-start(f32[8,32,128]{2,1,0:T(8,128)} %broadcast_in_dim.19), calls=%async_computation | async-start | bytes 262144 | tf_op jit(solution)/shard_map/while/body/eval_jaxpr/all_to_all | solution.py:21
  336.8 12.3 %all-to-all-start.1 = ((f32[16,32,128]{2,1,0:T(8,128)}), f32[16,32,128]{2,1,0:T(8,128)S(1)}, u32[]{:S(2)}, u32[]{:S(2)}) async-start(f32[16,32,128]{2,1,0:T(8,128)} %bitcast.43), calls=%async_computation.1 | async-start | bytes 524288 | tf_op jit(solution)/shard_map/while/body/eval_jaxpr/all_to_all | solution.py:35
  349.9 10.4 %all-to-all-start = ((f32[8,32,128]{2,1,0:T(8,128)}), f32[8,32,128]{2,1,0:T(8,128)S(1)}, u32[]{:S(2)}, u32[]{:S(2)}) async-start(f32[8,32,128]{2,1,0:T(8,128)} %broadcast_in_dim.19), calls=%async_computation | async-start | bytes 262144 | tf_op jit(solution)/shard_map/while/body/eval_jaxpr/all_to_all | solution.py:21
  370.1 12.3 %all-to-all-start.1 = ((f32[16,32,128]{2,1,0:T(8,128)}), f32[16,32,128]{2,1,0:T(8,128)S(1)}, u32[]{:S(2)}, u32[]{:S(2)}) async-start(f32[16,32,128]{2,1,0:T(8,128)} %bitcast.43), calls=%async_computation.1 | async-start | bytes 524288 | tf_op jit(solution)/shard_map/while/body/eval_jaxpr/all_to_all | solution.py:35
  383.1 10.4 %all-to-all-start = ((f32[8,32,128]{2,1,0:T(8,128)}), f32[8,32,128]{2,1,0:T(8,128)S(1)}, u32[]{:S(2)}, u32[]{:S(2)}) async-start(f32[8,32,128]{2,1,0:T(8,128)} %broadcast_in_dim.19), calls=%async_computation | async-start | bytes 262144 | tf_op jit(solution)/shard_map/while/body/eval_jaxpr/all_to_all | solution.py:21
  403.4 12.3 %all-to-all-start.1 = ((f32[16,32,128]{2,1,0:T(8,128)}), f32[16,32,128]{2,1,0:T(8,128)S(1)}, u32[]{:S(2)}, u32[]{:S(2)}) async-start(f32[16,32,128]{2,1,0:T(8,128)} %bitcast.43), calls=%async_computation.1 | async-start | bytes 524288 | tf_op jit(solution)/shard_map/while/body/eval_jaxpr/all_to_all | solution.py:35
  416.4 10.4 %all-to-all-start = ((f32[8,32,128]{2,1,0:T(8,128)}), f32[8,32,128]{2,1,0:T(8,128)S(1)}, u32[]{:S(2)}, u32[]{:S(2)}) async-start(f32[8,32,128]{2,1,0:T(8,128)} %broadcast_in_dim.19), calls=%async_computation | async-start | bytes 262144 | tf_op jit(solution)/shard_map/while/body/eval_jaxpr/all_to_all | solution.py:21
  436.7 12.3 %all-to-all-start.1 = ((f32[16,32,128]{2,1,0:T(8,128)}), f32[16,32,128]{2,1,0:T(8,128)S(1)}, u32[]{:S(2)}, u32[]{:S(2)}) async-start(f32[16,32,128]{2,1,0:T(8,128)} %bitcast.43), calls=%async_computation.1 | async-start | bytes 524288 | tf_op jit(solution)/shard_map/while/body/eval_jaxpr/all_to_all | solution.py:35
  449.7 10.4 %all-to-all-start = ((f32[8,32,128]{2,1,0:T(8,128)}), f32[8,32,128]{2,1,0:T(8,128)S(1)}, u32[]{:S(2)}, u32[]{:S(2)}) async-start(f32[8,32,128]{2,1,0:T(8,128)} %broadcast_in_dim.19), calls=%async_computation | async-start | bytes 262144 | tf_op jit(solution)/shard_map/while/body/eval_jaxpr/all_to_all | solution.py:21
  469.9 12.3 %all-to-all-start.1 = ((f32[16,32,128]{2,1,0:T(8,128)}), f32[16,32,128]{2,1,0:T(8,128)S(1)}, u32[]{:S(2)}, u32[]{:S(2)}) async-start(f32[16,32,128]{2,1,0:T(8,128)} %bitcast.43), calls=%async_computation.1 | async-start | bytes 524288 | tf_op jit(solution)/shard_map/while/body/eval_jaxpr/all_to_all | solution.py:35
  483.0 10.4 %all-to-all-start = ((f32[8,32,128]{2,1,0:T(8,128)}), f32[8,32,128]{2,1,0:T(8,128)S(1)}, u32[]{:S(2)}, u32[]{:S(2)}) async-start(f32[8,32,128]{2,1,0:T(8,128)} %broadcast_in_dim.19), calls=%async_computation | async-start | bytes 262144 | tf_op jit(solution)/shard_map/while/body/eval_jaxpr/all_to_all | solution.py:21
  503.2 12.3 %all-to-all-start.1 = ((f32[16,32,128]{2,1,0:T(8,128)}), f32[16,32,128]{2,1,0:T(8,128)S(1)}, u32[]{:S(2)}, u32[]{:S(2)}) async-start(f32[16,32,128]{2,1,0:T(8,128)} %bitcast.43), calls=%async_computation.1 | async-start | bytes 524288 | tf_op jit(solution)/shard_map/while/body/eval_jaxpr/all_to_all | solution.py:35
  516.3 10.4 %all-to-all-start = ((f32[8,32,128]{2,1,0:T(8,128)}), f32[8,32,128]{2,1,0:T(8,128)S(1)}, u32[]{:S(2)}, u32[]{:S(2)}) async-start(f32[8,32,128]{2,1,0:T(8,128)} %broadcast_in_dim.19), calls=%async_computation | async-start | bytes 262144 | tf_op jit(solution)/shard_map/while/body/eval_jaxpr/all_to_all | solution.py:21
  536.5 12.3 %all-to-all-start.1 = ((f32[16,32,128]{2,1,0:T(8,128)}), f32[16,32,128]{2,1,0:T(8,128)S(1)}, u32[]{:S(2)}, u32[]{:S(2)}) async-start(f32[16,32,128]{2,1,0:T(8,128)} %bitcast.43), calls=%async_computation.1 | async-start | bytes 524288 | tf_op jit(solution)/shard_map/while/body/eval_jaxpr/all_to_all | solution.py:35
  549.6 10.4 %all-to-all-start = ((f32[8,32,128]{2,1,0:T(8,128)}), f32[8,32,128]{2,1,0:T(8,128)S(1)}, u32[]{:S(2)}, u32[]{:S(2)}) async-start(f32[8,32,128]{2,1,0:T(8,128)} %broadcast_in_dim.19), calls=%async_computation | async-start | bytes 262144 | tf_op jit(solution)/shard_map/while/body/eval_jaxpr/all_to_all | solution.py:21
  569.8 12.3 %all-to-all-start.1 = ((f32[16,32,128]{2,1,0:T(8,128)}), f32[16,32,128]{2,1,0:T(8,128)S(1)}, u32[]{:S(2)}, u32[]{:S(2)}) async-start(f32[16,32,128]{2,1,0:T(8,128)} %bitcast.43), calls=%async_computation.1 | async-start | bytes 524288 | tf_op jit(solution)/shard_map/while/body/eval_jaxpr/all_to_all | solution.py:35
  582.8 10.4 %all-to-all-start = ((f32[8,32,128]{2,1,0:T(8,128)}), f32[8,32,128]{2,1,0:T(8,128)S(1)}, u32[]{:S(2)}, u32[]{:S(2)}) async-start(f32[8,32,128]{2,1,0:T(8,128)} %broadcast_in_dim.19), calls=%async_computation | async-start | bytes 262144 | tf_op jit(solution)/shard_map/while/body/eval_jaxpr/all_to_all | solution.py:21
  603.1 12.3 %all-to-all-start.1 = ((f32[16,32,128]{2,1,0:T(8,128)}), f32[16,32,128]{2,1,0:T(8,128)S(1)}, u32[]{:S(2)}, u32[]{:S(2)}) async-start(f32[16,32,128]{2,1,0:T(8,128)} %bitcast.43), calls=%async_computation.1 | async-start | bytes 524288 | tf_op jit(solution)/shard_map/while/body/eval_jaxpr/all_to_all | solution.py:35
  615.5 0.6 copy-start
  615.5 0.6 copy-start.2
where the time goes:
time: 621 us; the launch traced here: 616 us
  waiting for transfers between devices  282 us (45%)
  matrix products  149 us (24%)
  starting transfers between devices  148 us (24%)
  local copies, waits for them, and re-layouts  21.9 us (4%)
  blocking collectives  12.4 us (2%)
    dot_general x16, matrix products, local_product(): jnp.einsum('tij,tj->ti', flat, picked, precision=lax.Precision.HIGHEST)  133 us
    all_to_all x16, waiting for transfers between devices, sent_and_summed(): parts = lax.all_to_all(in_blocks(x, dim, size), axis, 0, 0, tiled=True)  118 us
    all_to_all x16, waiting for transfers between devices, sent_to_all(): lax.all_to_all(jnp.broadcast_to(x[None], (size, *x.shape)), axis, 0, 0, t...  112 us
    all_to_all x16, starting transfers between devices, sent_and_summed(): parts = lax.all_to_all(in_blocks(x, dim, size), axis, 0, 0, tiled=True)  84.8 us
    all_to_all x16, starting transfers between devices, sent_to_all(): lax.all_to_all(jnp.broadcast_to(x[None], (size, *x.shape)), axis, 0, 0, t...  57.9 us
    all_to_all x1, waiting for transfers between devices, per_device(): lax.all_to_all(tiles[0], 'col', split_axis=0, concat_axis=0, tiled=True)  52.2 us
    dot_general x16, matrix products, local_product(): return jnp.dot(onehot, prod, precision=lax.Precision.HIGHEST)  15.6 us
  transfers between devices with their start and end apart: 33, of which 33 were waited for; matrix products, arithmetic and copies ran while one was open for 0% of the time, Pallas kernels for 0%

commit v1 on v0

v1 whole, which is shorter than its diff:
```python
import functools

import jax
import jax.numpy as jnp
import numpy as np
from jax import lax
from jax.experimental import pallas as pl
from jax.experimental.pallas import tpu as pltpu
from jax.sharding import PartitionSpec as P

ITERS = 16

centre = 4.0
half_width = 3.96

BOTH = ("row", "col")
VMEM = pl.BlockSpec(memory_space=pltpu.VMEM)
MIB = 1 << 20


def steps():
    sigma = np.float32(2.0 * (centre / half_width))
    rho = np.float32(1.0 / (centre / half_width))
    pairs = []
    for _ in range(ITERS):
        rho_new = np.float32(1.0) / (sigma - rho)
        pairs.append((float(rho_new * rho), float(np.float32(2.0) * rho_new / np.float32(half_width))))
        rho = rho_new
    return pairs


def three_parts(x):
    high = x.astype(jnp.bfloat16)
    rest = x - high.astype(jnp.float32)
    middle = rest.astype(jnp.bfloat16)
    low = (rest - middle.astype(jnp.float32)).astype(jnp.bfloat16)
    return [high, middle, low]


def to_send(pick, direction):
    parts = three_parts(direction)
    parts.append(jnp.zeros_like(parts[0]))
    return jnp.dot(pick, jnp.concatenate(parts, axis=0), preferred_element_type=jnp.float32)


def tile_kernel(tile_ref, held_ref):
    for pair in range(held_ref.shape[0]):
        for end in range(2):
            flipped = tile_ref[2 * pair + end].T
            high = flipped.astype(jnp.bfloat16)
            low = (flipped - high.astype(jnp.float32)).astype(jnp.bfloat16)
            order = flipped.shape[0]
            held_ref[pair, :order, end * order : (end + 1) * order] = high
            held_ref[pair, order:, end * order : (end + 1) * order] = low


def start_kernel(want_ref, mine_ref, rhs_ref, pick_ref, send_ref, direction_ref):
    pick = jnp.where(want_ref[...] == mine_ref[...], 1.0, 0.0).astype(jnp.bfloat16)
    pick_ref[...] = pick
    direction = rhs_ref[...] * (1.0 / centre)
    direction_ref[...] = direction
    send_ref[...] = to_send(pick, direction)


def step_kernel(keep, gain, last, got_ref, held_ref, place_ref, pick_ref, diag_ref, pressure_ref, residual_ref, direction_ref, *out_refs):
    senders, wanted, order = got_ref.shape
    vec = got_ref[0]
    for sender in range(1, senders):
        vec = vec + got_ref[sender]
    high = vec.astype(jnp.bfloat16).astype(jnp.float32)
    low = vec - high
    lane_row = lax.broadcasted_iota(jnp.int32, (8, order), 0)
    products = []
    for block in range(wanted // 8):
        rows = slice(8 * block, 8 * block + 8)
        left = jnp.concatenate([high[rows], low[rows]], axis=0).astype(jnp.bfloat16)
        left = jnp.concatenate([left, left], axis=1)
        total = jnp.zeros((8, order), jnp.float32)
        for pair in range(4):
            out = jnp.dot(left, held_ref[4 * block + pair], preferred_element_type=jnp.float32)
            both = out[:8] + out[8:]
            for end in range(2):
                total = jnp.where(lane_row == 2 * pair + end, both[:, end * order : (end + 1) * order], total)
        products.append(total)
    products = jnp.concatenate(products, axis=0)
    off = jnp.dot(place_ref[...], jnp.concatenate(three_parts(products), axis=0), preferred_element_type=jnp.float32)
    direction = direction_ref[...]
    residual = residual_ref[...] - (diag_ref[...] * direction - off)
    out_refs[0][...] = pressure_ref[...] + direction
    out_refs[1][...] = residual
    if not last:
        direction = keep * direction + gain * residual
        out_refs[2][...] = direction
        out_refs[3][...] = to_send(pick_ref[...], direction)


def per_device(rhs, diag_vals, tiles, tile_row, tile_col):
    owned, order = rhs.shape
    _, groups, slots = tile_col.shape
    devices = lax.axis_size(BOTH)
    senders = devices // groups
    wanted = groups * slots
    f32 = jnp.float32

    asked = jnp.broadcast_to(tile_col[0][None, :, :, None], (senders, groups, slots, order)).reshape(devices, slots, order)
    want = lax.all_to_all(asked, BOTH, 0, 0, tiled=True).reshape(devices * slots, order)

    held = pl.pallas_call(
        tile_kernel,
        grid=(8,),
        in_specs=[pl.BlockSpec((wanted // 8, order, order), lambda i: (i, 0, 0))],
        out_specs=pl.BlockSpec((wanted // 16, 2 * order, 2 * order), lambda i: (i, 0, 0)),
        out_shape=jax.ShapeDtypeStruct((wanted // 2, 2 * order, 2 * order), jnp.bfloat16),
        compiler_params=pltpu.CompilerParams(vmem_limit_bytes=8 * MIB),
    )(tiles.reshape(wanted, order, order))

    targets = jnp.tile(tile_row.reshape(wanted), 3)
    place = (jnp.arange(owned, dtype=jnp.int32)[:, None] == targets[None, :]).astype(jnp.bfloat16)

    lane = jnp.arange(order, dtype=jnp.int32)
    mine = jnp.where(lane < 3 * owned, lax.axis_index("row") * owned + lane % owned, -1)[None, :]
    pick, send, direction = pl.pallas_call(
        start_kernel,
        in_specs=[VMEM] * 3,
        out_specs=[VMEM] * 3,
        out_shape=[
            jax.ShapeDtypeStruct((devices * slots, order), jnp.bfloat16),
            jax.ShapeDtypeStruct((devices * slots, order), f32),
            jax.ShapeDtypeStruct((owned, order), f32),
        ],
        compiler_params=pltpu.CompilerParams(vmem_limit_bytes=8 * MIB),
    )(want, mine, rhs)

    small = jax.ShapeDtypeStruct((owned, order), f32)
    pressure, residual = jnp.zeros_like(rhs), rhs
    for index, (keep, gain) in enumerate(steps()):
        last = index == ITERS - 1
        got = lax.all_to_all(send.reshape(devices, slots, order), BOTH, 0, 0, tiled=True)
        outs = pl.pallas_call(
            functools.partial(step_kernel, keep, gain, last),
            in_specs=[VMEM] * 8,
            out_specs=[VMEM] * (2 if last else 4),
            out_shape=[small, small] if last else [small, small, small, jax.ShapeDtypeStruct((devices * slots, order), f32)],
            compiler_params=pltpu.CompilerParams(vmem_limit_bytes=16 * MIB),
        )(got.reshape(senders, wanted, order), held, place, pick, diag_vals, pressure, residual, direction)
        pressure, residual = outs[:2]
        if not last:
            direction, send = outs[2:]
    return (pressure, residual)


def solution(mesh):
    return jax.shard_map(
        per_device,
        mesh=mesh,
        in_specs=(
            P(("row", "col"), None),
            P(("row", "col"), None),
            P(("row", "col"), None, None, None, None),
            P(("row", "col"), None, None),
            P(("row", "col"), None, None),
        ),
        out_specs=(P(("row", "col"), None), P(("row", "col"), None)),
        check_vma=False,
    )
```

time: 621 us -> 289 us (0.47)
  waiting for transfers between devices: 282 us -> 16 us
  blocking collectives: 12.4 us -> 228 us
  matrix products: 149 us -> 0 us
  starting transfers between devices: 148 us -> 15.4 us
  Pallas kernels: 0 us -> 18.6 us
  local copies, waits for them, and re-layouts: 21.9 us -> 9.63 us
    all_to_all x33 -> x2, waiting for transfers between devices: 282 us -> 16 us  [the longest x1 11.4 us: per_device(): lax.all_to_all(asked, BOTH, 0, 0, tiled=True)]
    all_to_all x1 -> x15, blocking collectives: 12.4 us -> 228 us  [per_device(): lax.all_to_all(send.reshape(devices, slots, order), BOTH, 0, 0, tiled=True)]
    dot_general x32 -> x0, matrix products: 149 us -> none  [the longest x16 133 us: local_product(): jnp.einsum('tij,tj->ti', flat, picked, precision=lax.Precision.HIGHEST)]
    all_to_all x33 -> x2, starting transfers between devices: 148 us -> 15.4 us  [the longest x1 11.5 us: per_device(): lax.all_to_all(asked, BOTH, 0, 0, tiled=True)]
    pallas_call x0 -> x18, Pallas kernels: none -> 18.6 us  [the longest x16 16 us: per_device(): pl.pallas_call(functools.partial(step_kernel, keep, gain, last), in_specs...]
    gather x16 -> x0, local copies, waits for them, and re-layouts: 9.54 us -> none  [local_product(): picked = vec[col_local.reshape(-1)]]
    broadcast_in_dim x16 -> x4, local copies, waits for them, and re-layouts: 10.6 us -> 1.67 us  [the longest x3 1.67 us: per_device(): jnp.broadcast_to(tile_col[0][None, :, :, None], (senders, groups, slots,...]
    unnamed x12 -> x15, local copies, waits for them, and re-layouts: 1.42 us -> 7.79 us
  transfers between devices with their start and end apart: 33 -> 2, of which waited for: 33 -> 2; matrix products, arithmetic and copies ran while one was open for 0% -> 0% of each run, Pallas kernels for 0% -> 1%
where the time goes in v1:
time: 289 us
  blocking collectives  228 us (79%)
  Pallas kernels  18.6 us (6%)
  waiting for transfers between devices  16 us (6%)
  starting transfers between devices  15.4 us (5%)
  local copies, waits for them, and re-layouts  9.63 us (3%)
    all_to_all x15, blocking collectives, per_device(): lax.all_to_all(send.reshape(devices, slots, order), BOTH, 0, 0, tiled=True)  228 us
    pallas_call x16, Pallas kernels, per_device(): pl.pallas_call(functools.partial(step_kernel, keep, gain, last), in_specs...  16 us
    all_to_all x1, starting transfers between devices, per_device(): lax.all_to_all(asked, BOTH, 0, 0, tiled=True)  11.5 us
    all_to_all x1, waiting for transfers between devices, per_device(): lax.all_to_all(asked, BOTH, 0, 0, tiled=True)  11.4 us
    unnamed x15, local copies, waits for them, and re-layouts  7.79 us
  transfers between devices with their start and end apart: 2, of which 2 were waited for; matrix products, arithmetic and copies ran while one was open for 0% of the time, Pallas kernels for 1%

profile of v1, /device:TPU:1, one launch (start us, length us, event | category | flops | bytes accessed | tf_op | source)
XLA Modules:
  0.0 288.8 jit_solution(4447163326799638230)
XLA Ops:
  0.6 0.8 copy.9
  1.4 0.9 broadcast_in_dim.23
  2.3 11.5 %all-to-all-start = ((s32[128,4,128]{2,1,0:T(4,128)}), s32[128,4,128]{2,1,0:T(4,128)S(1)}, u32[]{:S(2)}, u32[]{:S(2)}) async-start(s32[128,4,128]{2,1,0:T(4,128)} %broadcast_in_dim.23), calls=%async_computation | async-start | bytes 524288 | tf_op jit(solution)/shard_map/all_to_all | solution.py:106
  13.8 11.4 %all-to-all-done = s32[128,4,128]{2,1,0:T(4,128)S(1)} async-done(((s32[128,4,128]{2,1,0:T(4,128)}), s32[128,4,128]{2,1,0:T(4,128)S(1)}, u32[]{:S(2)}, u32[]{:S(2)}) %all-to-all-start) | async-done | bytes 262176 | tf_op jit(solution)/shard_map/all_to_all | solution.py:106
  25.2 0.0 copy-start.5
  25.2 0.7 copy-done.5
  25.9 0.9 shard_map.68
  26.8 3.9 %all-to-all-start.1 = ((f32[128,4,128]{2,1,0:T(4,128)}), f32[128,4,128]{2,1,0:T(4,128)S(1)}, u32[]{:S(2)}, u32[]{:S(2)}) async-start(f32[128,4,128]{2,1,0:T(4,128)} %bitcast.3), calls=%async_computation.1 | async-start | bytes 524288 | tf_op jit(solution)/shard_map/all_to_all | solution.py:138
  30.7 0.8 copy.10
  31.5 0.1 tile.7
  31.6 0.1 eq.18
  31.7 0.0 copy-start.4
  31.7 2.2 copy-done.4
  33.9 0.0 copy-start.3
  33.9 0.0 copy-start.6
  33.9 1.7 shard_map.69.held_ref
  35.6 0.0 copy-start
  35.6 1.9 copy-done
  37.5 4.6 %all-to-all-done.1 = f32[128,4,128]{2,1,0:T(4,128)S(1)} async-done(((f32[128,4,128]{2,1,0:T(4,128)}), f32[128,4,128]{2,1,0:T(4,128)S(1)}, u32[]{:S(2)}, u32[]{:S(2)}) %all-to-all-start.1) | async-done | bytes 262176 | tf_op jit(solution)/shard_map/all_to_all | solution.py:138
  42.1 0.0 copy-done.3
  42.1 0.0 copy-done.6
  42.2 0.0 copy-start.1
  42.2 2.2 copy-done.1
  44.3 0.0 copy-start.2
  44.3 1.0 shard_map.70
  45.3 16.4 %all_to_all.85 = f32[128,4,128]{2,1,0:T(4,128)S(1)} all-to-all(f32[128,4,128]{2,1,0:T(4,128)S(1)} %bitcast.68), channel_id=1, replica_groups=mesh['row'=8,'col'=16] {'row','col'}, dimensions={0} | all-to-all | bytes 524288 | tf_op jit(solution)/shard_map/all_to_all | solution.py:138
  61.7 0.0 copy-done.2
  61.7 1.0 shard_map.71
  62.7 15.1 %all_to_all.86 = f32[128,4,128]{2,1,0:T(4,128)S(1)} all-to-all(f32[128,4,128]{2,1,0:T(4,128)S(1)} %bitcast.54), channel_id=1, replica_groups=mesh['row'=8,'col'=16] {'row','col'}, dimensions={0} | all-to-all | bytes 524288 | tf_op jit(solution)/shard_map/all_to_all | solution.py:138
  77.8 1.0 shard_map.72
  78.8 15.1 %all_to_all.87 = f32[128,4,128]{2,1,0:T(4,128)S(1)} all-to-all(f32[128,4,128]{2,1,0:T(4,128)S(1)} %bitcast.55), channel_id=1, replica_groups=mesh['row'=8,'col'=16] {'row','col'}, dimensions={0} | all-to-all | bytes 524288 | tf_op jit(solution)/shard_map/all_to_all | solution.py:138
  94.0 1.0 shard_map.73
  94.9 15.1 %all_to_all.88 = f32[128,4,128]{2,1,0:T(4,128)S(1)} all-to-all(f32[128,4,128]{2,1,0:T(4,128)S(1)} %bitcast.56), channel_id=1, replica_groups=mesh['row'=8,'col'=16] {'row','col'}, dimensions={0} | all-to-all | bytes 524288 | tf_op jit(solution)/shard_map/all_to_all | solution.py:138
  110.1 1.0 shard_map.74
  111.1 15.1 %all_to_all.89 = f32[128,4,128]{2,1,0:T(4,128)S(1)} all-to-all(f32[128,4,128]{2,1,0:T(4,128)S(1)} %bitcast.57), channel_id=1, replica_groups=mesh['row'=8,'col'=16] {'row','col'}, dimensions={0} | all-to-all | bytes 524288 | tf_op jit(solution)/shard_map/all_to_all | solution.py:138
  126.2 1.0 shard_map.75
  127.2 15.1 %all_to_all.90 = f32[128,4,128]{2,1,0:T(4,128)S(1)} all-to-all(f32[128,4,128]{2,1,0:T(4,128)S(1)} %bitcast.58), channel_id=1, replica_groups=mesh['row'=8,'col'=16] {'row','col'}, dimensions={0} | all-to-all | bytes 524288 | tf_op jit(solution)/shard_map/all_to_all | solution.py:138
  142.3 1.0 shard_map.76
  143.3 15.1 %all_to_all.91 = f32[128,4,128]{2,1,0:T(4,128)S(1)} all-to-all(f32[128,4,128]{2,1,0:T(4,128)S(1)} %bitcast.59), channel_id=1, replica_groups=mesh['row'=8,'col'=16] {'row','col'}, dimensions={0} | all-to-all | bytes 524288 | tf_op jit(solution)/shard_map/all_to_all | solution.py:138
  158.4 1.0 shard_map.77
  159.4 15.1 %all_to_all.92 = f32[128,4,128]{2,1,0:T(4,128)S(1)} all-to-all(f32[128,4,128]{2,1,0:T(4,128)S(1)} %bitcast.60), channel_id=1, replica_groups=mesh['row'=8,'col'=16] {'row','col'}, dimensions={0} | all-to-all | bytes 524288 | tf_op jit(solution)/shard_map/all_to_all | solution.py:138
  174.5 1.0 shard_map.78
  175.5 15.1 %all_to_all.93 = f32[128,4,128]{2,1,0:T(4,128)S(1)} all-to-all(f32[128,4,128]{2,1,0:T(4,128)S(1)} %bitcast.61), channel_id=1, replica_groups=mesh['row'=8,'col'=16] {'row','col'}, dimensions={0} | all-to-all | bytes 524288 | tf_op jit(solution)/shard_map/all_to_all | solution.py:138
  190.7 1.0 shard_map.79
  191.6 15.1 %all_to_all.94 = f32[128,4,128]{2,1,0:T(4,128)S(1)} all-to-all(f32[128,4,128]{2,1,0:T(4,128)S(1)} %bitcast.62), channel_id=1, replica_groups=mesh['row'=8,'col'=16] {'row','col'}, dimensions={0} | all-to-all | bytes 524288 | tf_op jit(solution)/shard_map/all_to_all | solution.py:138
  206.8 1.0 shard_map.80
  207.8 15.1 %all_to_all.95 = f32[128,4,128]{2,1,0:T(4,128)S(1)} all-to-all(f32[128,4,128]{2,1,0:T(4,128)S(1)} %bitcast.63), channel_id=1, replica_groups=mesh['row'=8,'col'=16] {'row','col'}, dimensions={0} | all-to-all | bytes 524288 | tf_op jit(solution)/shard_map/all_to_all | solution.py:138
  222.9 1.0 shard_map.81
  223.9 15.1 %all_to_all.96 = f32[128,4,128]{2,1,0:T(4,128)S(1)} all-to-all(f32[128,4,128]{2,1,0:T(4,128)S(1)} %bitcast.64), channel_id=1, replica_groups=mesh['row'=8,'col'=16] {'row','col'}, dimensions={0} | all-to-all | bytes 524288 | tf_op jit(solution)/shard_map/all_to_all | solution.py:138
  239.0 1.0 shard_map.82
  240.0 15.1 %all_to_all.97 = f32[128,4,128]{2,1,0:T(4,128)S(1)} all-to-all(f32[128,4,128]{2,1,0:T(4,128)S(1)} %bitcast.65), channel_id=1, replica_groups=mesh['row'=8,'col'=16] {'row','col'}, dimensions={0} | all-to-all | bytes 524288 | tf_op jit(solution)/shard_map/all_to_all | solution.py:138
  255.1 1.0 shard_map.83
  256.1 15.1 %all_to_all.98 = f32[128,4,128]{2,1,0:T(4,128)S(1)} all-to-all(f32[128,4,128]{2,1,0:T(4,128)S(1)} %bitcast.66), channel_id=1, replica_groups=mesh['row'=8,'col'=16] {'row','col'}, dimensions={0} | all-to-all | bytes 524288 | tf_op jit(solution)/shard_map/all_to_all | solution.py:138
  271.2 1.0 shard_map.84
  272.2 15.1 %all_to_all.99 = f32[128,4,128]{2,1,0:T(4,128)S(1)} all-to-all(f32[128,4,128]{2,1,0:T(4,128)S(1)} %bitcast.67), channel_id=1, replica_groups=mesh['row'=8,'col'=16] {'row','col'}, dimensions={0} | all-to-all | bytes 524288 | tf_op jit(solution)/shard_map/all_to_all | solution.py:138
  287.4 1.4 shard_map.85
  (5 shorter events, 0.0 us)
Async XLA Ops:
  2.3 22.9 %all-to-all-start = ((s32[128,4,128]{2,1,0:T(4,128)}), s32[128,4,128]{2,1,0:T(4,128)S(1)}, u32[]{:S(2)}, u32[]{:S(2)}) async-start(s32[128,4,128]{2,1,0:T(4,128)} %broadcast_in_dim.23), calls=%async_computation | async-start | bytes 524288 | tf_op jit(solution)/shard_map/all_to_all | solution.py:106
  25.2 0.7 copy-start.5
  26.8 15.3 %all-to-all-start.1 = ((f32[128,4,128]{2,1,0:T(4,128)}), f32[128,4,128]{2,1,0:T(4,128)S(1)}, u32[]{:S(2)}, u32[]{:S(2)}) async-start(f32[128,4,128]{2,1,0:T(4,128)} %bitcast.3), calls=%async_computation.1 | async-start | bytes 524288 | tf_op jit(solution)/shard_map/all_to_all | solution.py:138
  31.7 2.2 copy-start.4
  33.9 8.3 %copy-start.3 = (f32[32,128]{1,0:T(8,128)S(1)}, f32[32,128]{1,0:T(8,128)}, u32[]{:S(2)}) copy-start(f32[32,128]{1,0:T(8,128)} %diag_ref.31) | copy-start | bytes 49156
  33.9 8.3 %copy-start.6 = (f32[32,128]{1,0:T(8,128)S(1)}, f32[32,128]{1,0:T(8,128)}, u32[]{:S(2)}) copy-start(f32[32,128]{1,0:T(8,128)} %residual_ref.1) | copy-start | bytes 49156
  35.6 1.9 copy-start
  42.2 2.2 copy-start.1
  44.3 17.4 %copy-start.2 = (bf16[32,256,256]{2,1,0:T(8,128)(2,1)S(1)}, bf16[32,256,256]{2,1,0:T(8,128)(2,1)}, u32[]{:S(2)}) copy-start(bf16[32,256,256]{2,1,0:T(8,128)(2,1)} %copy-done) | copy-start | bytes 12582916

commit v2 on v1

v2 whole, which is shorter than its diff:
```python
import functools

import jax
import jax.numpy as jnp
import numpy as np
from jax import lax
from jax.experimental import pallas as pl
from jax.experimental.pallas import tpu as pltpu
from jax.sharding import PartitionSpec as P

ITERS = 16

centre = 4.0
half_width = 3.96

BOTH = ("row", "col")
VMEM = pl.BlockSpec(memory_space=pltpu.VMEM)
MIB = 1 << 20


def steps():
    sigma = np.float32(2.0 * (centre / half_width))
    rho = np.float32(1.0 / (centre / half_width))
    pairs = []
    for _ in range(ITERS):
        rho_new = np.float32(1.0) / (sigma - rho)
        pairs.append((float(rho_new * rho), float(np.float32(2.0) * rho_new / np.float32(half_width))))
        rho = rho_new
    return pairs


def three_parts(x):
    high = x.astype(jnp.bfloat16)
    rest = x - high.astype(jnp.float32)
    middle = rest.astype(jnp.bfloat16)
    low = (rest - middle.astype(jnp.float32)).astype(jnp.bfloat16)
    return [high, middle, low]


def to_send(pick, direction):
    parts = three_parts(direction)
    parts.append(jnp.zeros_like(parts[0]))
    return jnp.dot(pick, jnp.concatenate(parts, axis=0), preferred_element_type=jnp.float32)


def ask_kernel(col_ref, ask_ref):
    slots, groups = col_ref.shape
    devices, lanes = ask_ref.shape
    wide = jnp.concatenate([col_ref[...], jnp.zeros((slots, lanes - groups), jnp.int32)], axis=1)
    wide = jnp.concatenate([wide, jnp.zeros((lanes - slots, lanes), jnp.int32)], axis=0)
    rows = wide.T[:groups]
    for first in range(0, devices, groups):
        ask_ref[first : first + groups] = rows


def tile_kernel(tile_ref, place_ref, mine_ref, held_ref):
    for tile in range(held_ref.shape[0]):
        flipped = tile_ref[tile].T
        order = flipped.shape[0]
        high = flipped.astype(jnp.bfloat16)
        held_ref[tile, :order] = high
        held_ref[tile, order:] = (flipped - high.astype(jnp.float32)).astype(jnp.bfloat16)


def begin_kernel(rhs_ref, held_ref, direction_ref):
    direction_ref[...] = rhs_ref[...] * (1.0 / centre)


def start_kernel(want_ref, mine_ref, direction_ref, pick_ref, send_ref, spread_ref):
    devices, lanes = want_ref.shape
    slots = spread_ref.shape[0] // devices
    mine = mine_ref[...]
    for slot in range(slots):
        asked = jnp.broadcast_to(want_ref[:, slot : slot + 1], (devices, lanes))
        spread_ref[pl.ds(slot, devices, stride=slots), :] = jnp.where(asked == mine, 1.0, 0.0)
    pick = spread_ref[...].astype(jnp.bfloat16)
    pick_ref[...] = pick
    send_ref[...] = to_send(pick, direction_ref[...])


def step_kernel(keep, gain, first, last, *refs):
    got_ref, held_ref, place_ref, pick_ref, diag_ref, direction_ref, residual_ref = refs[:7]
    out_refs = refs[7:] if first else refs[8:]
    senders, wanted, order = got_ref.shape
    vec = got_ref[0]
    for sender in range(1, senders):
        vec = vec + got_ref[sender]
    high = vec.astype(jnp.bfloat16).astype(jnp.float32)
    low = vec - high
    lane_row = lax.broadcasted_iota(jnp.int32, (8, order), 0)
    products = []
    for block in range(wanted // 8):
        rows = slice(8 * block, 8 * block + 8)
        left = jnp.concatenate([high[rows], low[rows]], axis=0).astype(jnp.bfloat16)
        left = jnp.concatenate([left, left], axis=1)
        total = jnp.zeros((8, order), jnp.float32)
        for slot in range(8):
            out = jnp.dot(left, held_ref[8 * block + slot], preferred_element_type=jnp.float32)
            total = jnp.where(lane_row == slot, out[:8] + out[8:], total)
        products.append(total)
    products = jnp.concatenate(products, axis=0)
    off = jnp.dot(place_ref[...], jnp.concatenate(three_parts(products), axis=0), preferred_element_type=jnp.float32)
    direction = direction_ref[...]
    residual = residual_ref[...] - (diag_ref[...] * direction - off)
    out_refs[0][...] = direction if first else refs[7][...] + direction
    out_refs[1][...] = residual
    if not last:
        direction = keep * direction + gain * residual
        out_refs[2][...] = direction
        out_refs[3][...] = to_send(pick_ref[...], direction)


def per_device(rhs, diag_vals, tiles, tile_row, tile_col):
    owned, order = rhs.shape
    _, groups, slots = tile_col.shape
    devices = lax.axis_size(BOTH)
    senders = devices // groups
    wanted = groups * slots
    f32 = jnp.float32

    asked = pl.pallas_call(
        ask_kernel,
        in_specs=[VMEM],
        out_specs=VMEM,
        out_shape=jax.ShapeDtypeStruct((devices, order), jnp.int32),
        compiler_params=pltpu.CompilerParams(vmem_limit_bytes=4 * MIB),
    )(tile_col[0].T)
    want = lax.all_to_all(asked[:, None], BOTH, 0, 0, tiled=True)[:, 0]

    targets = jnp.tile(tile_row.reshape(wanted), 3)
    place = (jnp.arange(owned, dtype=jnp.int32)[:, None] == targets[None, :]).astype(jnp.bfloat16)
    lane = jnp.arange(order, dtype=jnp.int32)
    mine = jnp.where(lane < 3 * owned, lax.axis_index("row") * owned + lane % owned, -1)[None, :]

    chunk = wanted // 8
    held = pl.pallas_call(
        tile_kernel,
        grid=(8,),
        in_specs=[
            pl.BlockSpec((chunk, order, order), lambda i: (i, 0, 0)),
            pl.BlockSpec(place.shape, lambda i: (0, 0)),
            pl.BlockSpec(mine.shape, lambda i: (0, 0)),
        ],
        out_specs=pl.BlockSpec((chunk, 2 * order, order), lambda i: (i, 0, 0)),
        out_shape=jax.ShapeDtypeStruct((wanted, 2 * order, order), jnp.bfloat16),
        compiler_params=pltpu.CompilerParams(vmem_limit_bytes=8 * MIB),
    )(tiles.reshape(wanted, order, order), place, mine)

    small = jax.ShapeDtypeStruct((owned, order), f32)
    direction = pl.pallas_call(
        begin_kernel,
        in_specs=[VMEM] * 2,
        out_specs=VMEM,
        out_shape=small,
        compiler_params=pltpu.CompilerParams(vmem_limit_bytes=8 * MIB),
    )(rhs, held)

    pick, send = pl.pallas_call(
        start_kernel,
        in_specs=[VMEM] * 3,
        out_specs=[VMEM] * 2,
        out_shape=[
            jax.ShapeDtypeStruct((devices * slots, order), jnp.bfloat16),
            jax.ShapeDtypeStruct((devices * slots, order), f32),
        ],
        scratch_shapes=[pltpu.VMEM((devices * slots, order), f32)],
        cost_estimate=pl.CostEstimate(flops=10**10, transcendentals=0, bytes_accessed=4 * 10**7),
        compiler_params=pltpu.CompilerParams(vmem_limit_bytes=16 * MIB),
    )(want, mine, direction)

    pressure, residual = [], rhs
    for index, (keep, gain) in enumerate(steps()):
        first, last = index == 0, index == ITERS - 1
        got = lax.all_to_all(send.reshape(devices, slots, order), BOTH, 0, 0, tiled=True)
        outs = pl.pallas_call(
            functools.partial(step_kernel, keep, gain, first, last),
            in_specs=[VMEM] * (7 if first else 8),
            out_specs=[VMEM] * (2 if last else 4),
            out_shape=[small, small] if last else [small, small, small, jax.ShapeDtypeStruct((devices * slots, order), f32)],
            compiler_params=pltpu.CompilerParams(vmem_limit_bytes=16 * MIB),
        )(got.reshape(senders, wanted, order), held, place, pick, diag_vals, direction, residual, *pressure)
        pressure, residual = [outs[0]], outs[1]
        if not last:
            direction, send = outs[2:]
    return (pressure[0], residual)


def solution(mesh):
    return jax.shard_map(
        per_device,
        mesh=mesh,
        in_specs=(
            P(("row", "col"), None),
            P(("row", "col"), None),
            P(("row", "col"), None, None, None, None),
            P(("row", "col"), None, None),
            P(("row", "col"), None, None),
        ),
        out_specs=(P(("row", "col"), None), P(("row", "col"), None)),
        check_vma=False,
    )
```

time: 289 us -> 285 us (0.986)
  blocking collectives: 228 us -> 245 us
  waiting for transfers between devices: 16 us -> 3 us
  local copies, waits for them, and re-layouts: 9.63 us -> 5.73 us
  starting transfers between devices: 15.4 us -> 11.5 us
    all_to_all x15 -> x16, blocking collectives: 228 us -> 245 us  [per_device(): lax.all_to_all(send.reshape(devices, slots, order), BOTH, 0, 0, tiled=True)]
    all_to_all x2 -> x1, waiting for transfers between devices: 16 us -> 3 us  [per_device(): want = lax.all_to_all(asked[:, None], BOTH, 0, 0, tiled=True)[:, 0]]
    all_to_all x2 -> x1, starting transfers between devices: 15.4 us -> 11.5 us  [per_device(): want = lax.all_to_all(asked[:, None], BOTH, 0, 0, tiled=True)[:, 0]]
    unnamed x15 -> x13, local copies, waits for them, and re-layouts: 7.79 us -> 5.56 us
    pallas_call x18 -> x20, Pallas kernels: 18.6 us -> 18.8 us  [the longest x16 16.1 us: per_device(): pl.pallas_call(functools.partial(step_kernel, keep, gain, first, last), i...]
  transfers between devices with their start and end apart: 2 -> 1, of which waited for: 2 -> 1; matrix products, arithmetic and copies ran while one was open for 0% -> 0% of each run, Pallas kernels for 1% -> 1%
where the time goes in v2:
time: 285 us
  blocking collectives  245 us (86%)
  Pallas kernels  18.8 us (7%)
  starting transfers between devices  11.5 us (4%)
  local copies, waits for them, and re-layouts  5.73 us (2%)
  waiting for transfers between devices  3 us (1%)
    all_to_all x16, blocking collectives, per_device(): lax.all_to_all(send.reshape(devices, slots, order), BOTH, 0, 0, tiled=True)  245 us
    pallas_call x16, Pallas kernels, per_device(): pl.pallas_call(functools.partial(step_kernel, keep, gain, first, last), i...  16.1 us
    all_to_all x1, starting transfers between devices, per_device(): want = lax.all_to_all(asked[:, None], BOTH, 0, 0, tiled=True)[:, 0]  11.5 us
  transfers between devices with their start and end apart: 1, of which 1 were waited for; matrix products, arithmetic and copies ran while one was open for 0% of the time, Pallas kernels for 1%

profile of v2, /device:TPU:1, one launch (start us, length us, event | category | flops | bytes accessed | tf_op | source)
XLA Modules:
  0.0 284.8 jit_solution(18107727594904809119)
XLA Ops:
  0.6 0.0 copy-start.5
  0.6 0.7 copy-done.5
  1.3 0.7 shard_map.68
  2.0 11.5 %all-to-all-start = ((s32[128,1,128]{2,1,0:T(1,128)}), s32[128,1,128]{2,1,0:T(1,128)S(1)}, u32[]{:S(2)}, u32[]{:S(2)}) async-start(s32[128,1,128]{2,1,0:T(1,128)} %bitcast.3), calls=%async_computation | async-start | bytes 131072 | tf_op jit(solution)/shard_map/all_to_all | solution.py:128
  13.5 0.8 copy.10
  14.3 0.1 tile.7
  14.4 0.1 eq.18
  14.5 0.0 copy-start.3
  14.5 2.2 copy-done.3
  16.7 0.0 copy-start.4
  16.7 1.7 shard_map.69.held_ref.refs_1_
  18.4 0.0 copy-done.4
  18.4 0.0 copy-start
  18.4 1.9 copy-done
  20.3 3.0 %all-to-all-done = s32[128,1,128]{2,1,0:T(1,128)S(1)} async-done(((s32[128,1,128]{2,1,0:T(1,128)}), s32[128,1,128]{2,1,0:T(1,128)S(1)}, u32[]{:S(2)}, u32[]{:S(2)}) %all-to-all-start) | async-done | bytes 65568 | tf_op jit(solution)/shard_map/all_to_all | solution.py:128
  23.3 0.0 copy-start.1
  23.3 0.0 copy-start.2
  23.3 0.3 shard_map.71
  23.6 18.0 %all_to_all.85 = f32[128,4,128]{2,1,0:T(4,128)S(1)} all-to-all(f32[128,4,128]{2,1,0:T(4,128)S(1)} %bitcast.72), channel_id=1, replica_groups=mesh['row'=8,'col'=16] {'row','col'}, dimensions={0} | all-to-all | bytes 524288 | tf_op jit(solution)/shard_map/all_to_all | solution.py:174
  41.6 0.0 copy-done.1
  41.6 0.0 copy-done.2
  41.6 1.0 shard_map.72
  42.6 15.1 %all_to_all.86 = f32[128,4,128]{2,1,0:T(4,128)S(1)} all-to-all(f32[128,4,128]{2,1,0:T(4,128)S(1)} %bitcast.71), channel_id=1, replica_groups=mesh['row'=8,'col'=16] {'row','col'}, dimensions={0} | all-to-all | bytes 524288 | tf_op jit(solution)/shard_map/all_to_all | solution.py:174
  57.7 1.0 shard_map.73
  58.7 15.1 %all_to_all.87 = f32[128,4,128]{2,1,0:T(4,128)S(1)} all-to-all(f32[128,4,128]{2,1,0:T(4,128)S(1)} %bitcast.57), channel_id=1, replica_groups=mesh['row'=8,'col'=16] {'row','col'}, dimensions={0} | all-to-all | bytes 524288 | tf_op jit(solution)/shard_map/all_to_all | solution.py:174
  73.9 1.0 shard_map.74
  74.8 15.1 %all_to_all.88 = f32[128,4,128]{2,1,0:T(4,128)S(1)} all-to-all(f32[128,4,128]{2,1,0:T(4,128)S(1)} %bitcast.58), channel_id=1, replica_groups=mesh['row'=8,'col'=16] {'row','col'}, dimensions={0} | all-to-all | bytes 524288 | tf_op jit(solution)/shard_map/all_to_all | solution.py:174
  90.0 1.0 shard_map.75
  91.0 15.1 %all_to_all.89 = f32[128,4,128]{2,1,0:T(4,128)S(1)} all-to-all(f32[128,4,128]{2,1,0:T(4,128)S(1)} %bitcast.59), channel_id=1, replica_groups=mesh['row'=8,'col'=16] {'row','col'}, dimensions={0} | all-to-all | bytes 524288 | tf_op jit(solution)/shard_map/all_to_all | solution.py:174
  106.1 1.0 shard_map.76
  107.1 15.1 %all_to_all.90 = f32[128,4,128]{2,1,0:T(4,128)S(1)} all-to-all(f32[128,4,128]{2,1,0:T(4,128)S(1)} %bitcast.60), channel_id=1, replica_groups=mesh['row'=8,'col'=16] {'row','col'}, dimensions={0} | all-to-all | bytes 524288 | tf_op jit(solution)/shard_map/all_to_all | solution.py:174
  122.2 1.0 shard_map.77
  123.2 15.1 %all_to_all.91 = f32[128,4,128]{2,1,0:T(4,128)S(1)} all-to-all(f32[128,4,128]{2,1,0:T(4,128)S(1)} %bitcast.61), channel_id=1, replica_groups=mesh['row'=8,'col'=16] {'row','col'}, dimensions={0} | all-to-all | bytes 524288 | tf_op jit(solution)/shard_map/all_to_all | solution.py:174
  138.3 1.0 shard_map.78
  139.3 15.1 %all_to_all.92 = f32[128,4,128]{2,1,0:T(4,128)S(1)} all-to-all(f32[128,4,128]{2,1,0:T(4,128)S(1)} %bitcast.62), channel_id=1, replica_groups=mesh['row'=8,'col'=16] {'row','col'}, dimensions={0} | all-to-all | bytes 524288 | tf_op jit(solution)/shard_map/all_to_all | solution.py:174
  154.4 1.0 shard_map.79
  155.4 15.1 %all_to_all.93 = f32[128,4,128]{2,1,0:T(4,128)S(1)} all-to-all(f32[128,4,128]{2,1,0:T(4,128)S(1)} %bitcast.63), channel_id=1, replica_groups=mesh['row'=8,'col'=16] {'row','col'}, dimensions={0} | all-to-all | bytes 524288 | tf_op jit(solution)/shard_map/all_to_all | solution.py:174
  170.6 1.0 shard_map.80
  171.6 15.1 %all_to_all.94 = f32[128,4,128]{2,1,0:T(4,128)S(1)} all-to-all(f32[128,4,128]{2,1,0:T(4,128)S(1)} %bitcast.64), channel_id=1, replica_groups=mesh['row'=8,'col'=16] {'row','col'}, dimensions={0} | all-to-all | bytes 524288 | tf_op jit(solution)/shard_map/all_to_all | solution.py:174
  186.7 1.0 shard_map.81
  187.7 15.1 %all_to_all.95 = f32[128,4,128]{2,1,0:T(4,128)S(1)} all-to-all(f32[128,4,128]{2,1,0:T(4,128)S(1)} %bitcast.65), channel_id=1, replica_groups=mesh['row'=8,'col'=16] {'row','col'}, dimensions={0} | all-to-all | bytes 524288 | tf_op jit(solution)/shard_map/all_to_all | solution.py:174
  202.8 1.0 shard_map.82
  203.8 15.1 %all_to_all.96 = f32[128,4,128]{2,1,0:T(4,128)S(1)} all-to-all(f32[128,4,128]{2,1,0:T(4,128)S(1)} %bitcast.66), channel_id=1, replica_groups=mesh['row'=8,'col'=16] {'row','col'}, dimensions={0} | all-to-all | bytes 524288 | tf_op jit(solution)/shard_map/all_to_all | solution.py:174
  218.9 1.0 shard_map.83
  219.9 15.1 %all_to_all.97 = f32[128,4,128]{2,1,0:T(4,128)S(1)} all-to-all(f32[128,4,128]{2,1,0:T(4,128)S(1)} %bitcast.67), channel_id=1, replica_groups=mesh['row'=8,'col'=16] {'row','col'}, dimensions={0} | all-to-all | bytes 524288 | tf_op jit(solution)/shard_map/all_to_all | solution.py:174
  235.0 1.0 shard_map.84
  236.0 15.1 %all_to_all.98 = f32[128,4,128]{2,1,0:T(4,128)S(1)} all-to-all(f32[128,4,128]{2,1,0:T(4,128)S(1)} %bitcast.68), channel_id=1, replica_groups=mesh['row'=8,'col'=16] {'row','col'}, dimensions={0} | all-to-all | bytes 524288 | tf_op jit(solution)/shard_map/all_to_all | solution.py:174
  251.2 1.0 shard_map.85
  252.1 15.1 %all_to_all.99 = f32[128,4,128]{2,1,0:T(4,128)S(1)} all-to-all(f32[128,4,128]{2,1,0:T(4,128)S(1)} %bitcast.69), channel_id=1, replica_groups=mesh['row'=8,'col'=16] {'row','col'}, dimensions={0} | all-to-all | bytes 524288 | tf_op jit(solution)/shard_map/all_to_all | solution.py:174
  267.3 1.0 shard_map.86
  268.3 15.1 %all_to_all.100 = f32[128,4,128]{2,1,0:T(4,128)S(1)} all-to-all(f32[128,4,128]{2,1,0:T(4,128)S(1)} %bitcast.70), channel_id=1, replica_groups=mesh['row'=8,'col'=16] {'row','col'}, dimensions={0} | all-to-all | bytes 524288 | tf_op jit(solution)/shard_map/all_to_all | solution.py:174
  283.4 1.4 shard_map.87
  (4 shorter events, 0.0 us)
Async XLA Ops:
  0.6 0.7 copy-start.5
  2.0 21.3 %all-to-all-start = ((s32[128,1,128]{2,1,0:T(1,128)}), s32[128,1,128]{2,1,0:T(1,128)S(1)}, u32[]{:S(2)}, u32[]{:S(2)}) async-start(s32[128,1,128]{2,1,0:T(1,128)} %bitcast.3), calls=%async_computation | async-start | bytes 131072 | tf_op jit(solution)/shard_map/all_to_all | solution.py:128
  14.5 2.2 copy-start.3
  16.7 1.7 copy-start.4
  18.4 1.9 copy-start
  23.3 18.3 %copy-start.1 = (bf16[64,256,128]{2,1,0:T(8,128)(2,1)S(1)}, bf16[64,256,128]{2,1,0:T(8,128)(2,1)}, u32[]{:S(2)}) copy-start(bf16[64,256,128]{2,1,0:T(8,128)(2,1)} %copy-done) | copy-start | bytes 12582916
  23.3 18.3 %copy-start.2 = (f32[32,128]{1,0:T(8,128)S(1)}, f32[32,128]{1,0:T(8,128)}, u32[]{:S(2)}) copy-start(f32[32,128]{1,0:T(8,128)} %refs_4_.31) | copy-start | bytes 49156

commit v3 on v2

--- a/solution.py
+++ b/solution.py
@@ -53,17 +53,38 @@
         ask_ref[first : first + groups] = rows
 
 
-def tile_kernel(tile_ref, place_ref, mine_ref, held_ref):
-    for tile in range(held_ref.shape[0]):
-        flipped = tile_ref[tile].T
-        order = flipped.shape[0]
-        high = flipped.astype(jnp.bfloat16)
-        held_ref[tile, :order] = high
-        held_ref[tile, order:] = (flipped - high.astype(jnp.float32)).astype(jnp.bfloat16)
-
-
-def begin_kernel(rhs_ref, held_ref, direction_ref):
+def tile_kernel(tile_hbm, row_ref, rhs_ref, mine_ref, held_hbm, place_ref, direction_ref, tile_buf, held_buf, in_sem, out_sem):
+    chunks = in_sem.shape[0]
+    size = tile_hbm.shape[0] // chunks
+    order = tile_hbm.shape[-1]
+    fetches = [pltpu.make_async_copy(tile_hbm.at[pl.ds(c * size, size)], tile_buf.at[pl.ds(c * size, size)], in_sem.at[c]) for c in range(chunks)]
+    stores = [pltpu.make_async_copy(held_buf.at[pl.ds(c * size, size)], held_hbm.at[pl.ds(c * size, size)], out_sem.at[c]) for c in range(chunks)]
+    for fetch in fetches:
+        fetch.start()
     direction_ref[...] = rhs_ref[...] * (1.0 / centre)
+    slots, groups = row_ref.shape
+    owned, spread = place_ref.shape
+    wanted = slots * groups
+    source = lax.broadcasted_iota(jnp.int32, (groups, spread), 0)
+    target = lax.broadcasted_iota(jnp.int32, (groups, spread), 1) % wanted
+    targets = jnp.zeros((8, spread), jnp.float32)
+    rows = row_ref[...].astype(jnp.float32)
+    for slot in range(slots):
+        expand = jnp.where(target == source * slots + slot, 1.0, 0.0).astype(jnp.bfloat16)
+        line = jnp.broadcast_to(rows[slot : slot + 1], (8, groups)).astype(jnp.bfloat16)
+        targets = targets + jnp.dot(line, expand, preferred_element_type=jnp.float32)
+    block = lax.broadcasted_iota(jnp.int32, (owned, spread), 0)
+    place_ref[...] = jnp.where(block == targets[:1].astype(jnp.int32), 1.0, 0.0).astype(jnp.bfloat16)
+    for c in range(chunks):
+        fetches[c].wait()
+        for tile in range(c * size, (c + 1) * size):
+            flipped = tile_buf[tile].T
+            high = flipped.astype(jnp.bfloat16)
+            held_buf[tile, :order] = high
+            held_buf[tile, order:] = (flipped - high.astype(jnp.float32)).astype(jnp.bfloat16)
+        stores[c].start()
+    for store in stores:
+        store.wait()
 
 
 def start_kernel(want_ref, mine_ref, direction_ref, pick_ref, send_ref, spread_ref):
@@ -127,33 +148,28 @@
     )(tile_col[0].T)
     want = lax.all_to_all(asked[:, None], BOTH, 0, 0, tiled=True)[:, 0]
 
-    targets = jnp.tile(tile_row.reshape(wanted), 3)
-    place = (jnp.arange(owned, dtype=jnp.int32)[:, None] == targets[None, :]).astype(jnp.bfloat16)
     lane = jnp.arange(order, dtype=jnp.int32)
     mine = jnp.where(lane < 3 * owned, lax.axis_index("row") * owned + lane % owned, -1)[None, :]
 
-    chunk = wanted // 8
-    held = pl.pallas_call(
+    chunks = 8
+    small = jax.ShapeDtypeStruct((owned, order), f32)
+    held, place, direction = pl.pallas_call(
         tile_kernel,
-        grid=(8,),
-        in_specs=[
-            pl.BlockSpec((chunk, order, order), lambda i: (i, 0, 0)),
-            pl.BlockSpec(place.shape, lambda i: (0, 0)),
-            pl.BlockSpec(mine.shape, lambda i: (0, 0)),
+        in_specs=[pl.BlockSpec(memory_space=pltpu.HBM), VMEM, VMEM, VMEM],
+        out_specs=[pl.BlockSpec(memory_space=pltpu.HBM), VMEM, VMEM],
+        out_shape=[
+            pltpu.HBM((wanted, 2 * order, order), jnp.bfloat16),
+            jax.ShapeDtypeStruct((owned, 3 * wanted), jnp.bfloat16),
+            small,
         ],
-        out_specs=pl.BlockSpec((chunk, 2 * order, order), lambda i: (i, 0, 0)),
-        out_shape=jax.ShapeDtypeStruct((wanted, 2 * order, order), jnp.bfloat16),
-        compiler_params=pltpu.CompilerParams(vmem_limit_bytes=8 * MIB),
-    )(tiles.reshape(wanted, order, order), place, mine)
-
-    small = jax.ShapeDtypeStruct((owned, order), f32)
-    direction = pl.pallas_call(
-        begin_kernel,
-        in_specs=[VMEM] * 2,
-        out_specs=VMEM,
-        out_shape=small,
-        compiler_params=pltpu.CompilerParams(vmem_limit_bytes=8 * MIB),
-    )(rhs, held)
+        scratch_shapes=[
+            pltpu.VMEM((wanted, order, order), f32),
+            pltpu.VMEM((wanted, 2 * order, order), jnp.bfloat16),
+            pltpu.SemaphoreType.DMA((chunks,)),
+            pltpu.SemaphoreType.DMA((chunks,)),
+        ],
+        compiler_params=pltpu.CompilerParams(vmem_limit_bytes=16 * MIB),
+    )(pltpu.with_memory_space_constraint(tiles.reshape(wanted, order, order), pltpu.HBM), tile_row[0].T, rhs, mine)
 
     pick, send = pl.pallas_call(
         start_kernel,

time: 285 us -> 284 us (level)
  local copies, waits for them, and re-layouts: 5.73 us -> 2.08 us
    unnamed x13 -> x12, local copies, waits for them, and re-layouts: 5.56 us -> 2.08 us
where the time goes in v3:
time: 284 us; the launch traced here: 283 us
  blocking collectives  243 us (86%)
  Pallas kernels  20.7 us (7%)
  starting transfers between devices  11.5 us (4%)
  waiting for transfers between devices  4.81 us (2%)
    all_to_all x16, blocking collectives, per_device(): lax.all_to_all(send.reshape(devices, slots, order), BOTH, 0, 0, tiled=True)  243 us
    pallas_call x16, Pallas kernels, per_device(): pl.pallas_call(functools.partial(step_kernel, keep, gain, first, last), i...  16.1 us
    all_to_all x1, starting transfers between devices, per_device(): want = lax.all_to_all(asked[:, None], BOTH, 0, 0, tiled=True)[:, 0]  11.5 us
  transfers between devices with their start and end apart: 1, of which 1 were waited for; matrix products, arithmetic and copies ran while one was open for 0% of the time, Pallas kernels for 1%

profile of v3, /device:TPU:1, one launch (start us, length us, event | category | flops | bytes accessed | tf_op | source)
XLA Modules:
  0.0 283.1 jit_solution(10432573177038267516)
XLA Ops:
  0.6 0.0 copy-start.5
  0.6 0.7 copy-done.5
  1.3 0.7 shard_map.68
  2.0 11.5 %all-to-all-start = ((s32[128,1,128]{2,1,0:T(1,128)}), s32[128,1,128]{2,1,0:T(1,128)S(1)}, u32[]{:S(2)}, u32[]{:S(2)}) async-start(s32[128,1,128]{2,1,0:T(1,128)} %bitcast.3), calls=%async_computation | async-start | bytes 131072 | tf_op jit(solution)/shard_map/all_to_all | solution.py:149
  13.5 0.0 copy-start.2
  13.5 0.7 copy-done.2
  14.2 0.0 copy-start.4
  14.2 0.7 copy-done.4
  14.9 3.6 %shard_map.69 = (bf16[64,256,128]{2,1,0:T(8,128)(2,1)}, bf16[32,192]{1,0:T(8,128)(2,1)S(1)}, f32[32,128]{1,0:T(8,128)S(1)}) custom-call(f32[64,128,128]{2,1,0:T(8,128)} %bitcast.78, s32[4,16]{1,0:T(4,128)S(1)} %bitcast.76, f32[32,128]{1,0:T(8,128)S(1)} %copy-done.2, s32[1,128]{1,0:T(1,128)S(1)} %compare_select_fusion.mine_ref), custom_call_target="tpu_custom_call" | custom-call | tf_op jit(solution)/shard_map/pallas_call | solution.py:156
  18.6 4.8 %all-to-all-done = s32[128,1,128]{2,1,0:T(1,128)S(1)} async-done(((s32[128,1,128]{2,1,0:T(1,128)}), s32[128,1,128]{2,1,0:T(1,128)S(1)}, u32[]{:S(2)}, u32[]{:S(2)}) %all-to-all-start) | async-done | bytes 65568 | tf_op jit(solution)/shard_map/all_to_all | solution.py:149
  23.4 0.0 copy-start
  23.4 0.0 copy-start.1
  23.4 0.0 copy-start.3
  23.4 0.3 shard_map.70
  23.7 16.2 %all_to_all.85 = f32[128,4,128]{2,1,0:T(4,128)S(1)} all-to-all(f32[128,4,128]{2,1,0:T(4,128)S(1)} %bitcast.74), channel_id=1, replica_groups=mesh['row'=8,'col'=16] {'row','col'}, dimensions={0} | all-to-all | bytes 524288 | tf_op jit(solution)/shard_map/all_to_all | solution.py:190
  39.9 0.0 copy-done
  39.9 0.0 copy-done.1
  39.9 0.0 copy-done.3
  39.9 1.0 shard_map.71
  40.9 15.1 %all_to_all.86 = f32[128,4,128]{2,1,0:T(4,128)S(1)} all-to-all(f32[128,4,128]{2,1,0:T(4,128)S(1)} %bitcast.73), channel_id=1, replica_groups=mesh['row'=8,'col'=16] {'row','col'}, dimensions={0} | all-to-all | bytes 524288 | tf_op jit(solution)/shard_map/all_to_all | solution.py:190
  56.0 1.0 shard_map.72
  57.0 15.1 %all_to_all.87 = f32[128,4,128]{2,1,0:T(4,128)S(1)} all-to-all(f32[128,4,128]{2,1,0:T(4,128)S(1)} %bitcast.59), channel_id=1, replica_groups=mesh['row'=8,'col'=16] {'row','col'}, dimensions={0} | all-to-all | bytes 524288 | tf_op jit(solution)/shard_map/all_to_all | solution.py:190
  72.1 1.0 shard_map.73
  73.1 15.1 %all_to_all.88 = f32[128,4,128]{2,1,0:T(4,128)S(1)} all-to-all(f32[128,4,128]{2,1,0:T(4,128)S(1)} %bitcast.60), channel_id=1, replica_groups=mesh['row'=8,'col'=16] {'row','col'}, dimensions={0} | all-to-all | bytes 524288 | tf_op jit(solution)/shard_map/all_to_all | solution.py:190
  88.2 1.0 shard_map.74
  89.2 15.1 %all_to_all.89 = f32[128,4,128]{2,1,0:T(4,128)S(1)} all-to-all(f32[128,4,128]{2,1,0:T(4,128)S(1)} %bitcast.61), channel_id=1, replica_groups=mesh['row'=8,'col'=16] {'row','col'}, dimensions={0} | all-to-all | bytes 524288 | tf_op jit(solution)/shard_map/all_to_all | solution.py:190
  104.4 1.0 shard_map.75
  105.4 15.1 %all_to_all.90 = f32[128,4,128]{2,1,0:T(4,128)S(1)} all-to-all(f32[128,4,128]{2,1,0:T(4,128)S(1)} %bitcast.62), channel_id=1, replica_groups=mesh['row'=8,'col'=16] {'row','col'}, dimensions={0} | all-to-all | bytes 524288 | tf_op jit(solution)/shard_map/all_to_all | solution.py:190
  120.5 1.0 shard_map.76
  121.5 15.1 %all_to_all.91 = f32[128,4,128]{2,1,0:T(4,128)S(1)} all-to-all(f32[128,4,128]{2,1,0:T(4,128)S(1)} %bitcast.63), channel_id=1, replica_groups=mesh['row'=8,'col'=16] {'row','col'}, dimensions={0} | all-to-all | bytes 524288 | tf_op jit(solution)/shard_map/all_to_all | solution.py:190
  136.6 1.0 shard_map.77
  137.6 15.1 %all_to_all.92 = f32[128,4,128]{2,1,0:T(4,128)S(1)} all-to-all(f32[128,4,128]{2,1,0:T(4,128)S(1)} %bitcast.64), channel_id=1, replica_groups=mesh['row'=8,'col'=16] {'row','col'}, dimensions={0} | all-to-all | bytes 524288 | tf_op jit(solution)/shard_map/all_to_all | solution.py:190
  152.7 1.0 shard_map.78
  153.7 15.1 %all_to_all.93 = f32[128,4,128]{2,1,0:T(4,128)S(1)} all-to-all(f32[128,4,128]{2,1,0:T(4,128)S(1)} %bitcast.65), channel_id=1, replica_groups=mesh['row'=8,'col'=16] {'row','col'}, dimensions={0} | all-to-all | bytes 524288 | tf_op jit(solution)/shard_map/all_to_all | solution.py:190
  168.8 1.0 shard_map.79
  169.8 15.1 %all_to_all.94 = f32[128,4,128]{2,1,0:T(4,128)S(1)} all-to-all(f32[128,4,128]{2,1,0:T(4,128)S(1)} %bitcast.66), channel_id=1, replica_groups=mesh['row'=8,'col'=16] {'row','col'}, dimensions={0} | all-to-all | bytes 524288 | tf_op jit(solution)/shard_map/all_to_all | solution.py:190
  185.0 1.0 shard_map.80
  185.9 15.1 %all_to_all.95 = f32[128,4,128]{2,1,0:T(4,128)S(1)} all-to-all(f32[128,4,128]{2,1,0:T(4,128)S(1)} %bitcast.67), channel_id=1, replica_groups=mesh['row'=8,'col'=16] {'row','col'}, dimensions={0} | all-to-all | bytes 524288 | tf_op jit(solution)/shard_map/all_to_all | solution.py:190
  201.1 1.0 shard_map.81
  202.1 15.1 %all_to_all.96 = f32[128,4,128]{2,1,0:T(4,128)S(1)} all-to-all(f32[128,4,128]{2,1,0:T(4,128)S(1)} %bitcast.68), channel_id=1, replica_groups=mesh['row'=8,'col'=16] {'row','col'}, dimensions={0} | all-to-all | bytes 524288 | tf_op jit(solution)/shard_map/all_to_all | solution.py:190
  217.2 1.0 shard_map.82
  218.2 15.1 %all_to_all.97 = f32[128,4,128]{2,1,0:T(4,128)S(1)} all-to-all(f32[128,4,128]{2,1,0:T(4,128)S(1)} %bitcast.69), channel_id=1, replica_groups=mesh['row'=8,'col'=16] {'row','col'}, dimensions={0} | all-to-all | bytes 524288 | tf_op jit(solution)/shard_map/all_to_all | solution.py:190
  233.3 1.0 shard_map.83
  234.3 15.1 %all_to_all.98 = f32[128,4,128]{2,1,0:T(4,128)S(1)} all-to-all(f32[128,4,128]{2,1,0:T(4,128)S(1)} %bitcast.70), channel_id=1, replica_groups=mesh['row'=8,'col'=16] {'row','col'}, dimensions={0} | all-to-all | bytes 524288 | tf_op jit(solution)/shard_map/all_to_all | solution.py:190
  249.4 1.0 shard_map.84
  250.4 15.1 %all_to_all.99 = f32[128,4,128]{2,1,0:T(4,128)S(1)} all-to-all(f32[128,4,128]{2,1,0:T(4,128)S(1)} %bitcast.71), channel_id=1, replica_groups=mesh['row'=8,'col'=16] {'row','col'}, dimensions={0} | all-to-all | bytes 524288 | tf_op jit(solution)/shard_map/all_to_all | solution.py:190
  265.5 1.0 shard_map.85
  266.5 15.1 %all_to_all.100 = f32[128,4,128]{2,1,0:T(4,128)S(1)} all-to-all(f32[128,4,128]{2,1,0:T(4,128)S(1)} %bitcast.72), channel_id=1, replica_groups=mesh['row'=8,'col'=16] {'row','col'}, dimensions={0} | all-to-all | bytes 524288 | tf_op jit(solution)/shard_map/all_to_all | solution.py:190
  281.7 1.4 shard_map.86
  (1 shorter events, 0.0 us)
Async XLA Ops:
  0.6 0.7 copy-start.5
  2.0 21.4 %all-to-all-start = ((s32[128,1,128]{2,1,0:T(1,128)}), s32[128,1,128]{2,1,0:T(1,128)S(1)}, u32[]{:S(2)}, u32[]{:S(2)}) async-start(s32[128,1,128]{2,1,0:T(1,128)} %bitcast.3), calls=%async_computation | async-start | bytes 131072 | tf_op jit(solution)/shard_map/all_to_all | solution.py:149
  13.5 0.7 copy-start.2
  14.2 0.7 copy-start.4
  23.4 16.5 %copy-start = (bf16[64,256,128]{2,1,0:T(8,128)(2,1)S(1)}, bf16[64,256,128]{2,1,0:T(8,128)(2,1)}, u32[]{:S(2)}) copy-start(bf16[64,256,128]{2,1,0:T(8,128)(2,1)} %get-tuple-element.69.refs_1_) | copy-start | bytes 12582916
  23.4 16.5 %copy-start.1 = (f32[32,128]{1,0:T(8,128)S(1)}, f32[32,128]{1,0:T(8,128)}, u32[]{:S(2)}) copy-start(f32[32,128]{1,0:T(8,128)} %refs_4_.31) | copy-start | bytes 49156
  23.4 16.5 %copy-start.3 = (f32[32,128]{1,0:T(8,128)S(1)}, f32[32,128]{1,0:T(8,128)}, u32[]{:S(2)}) copy-start(f32[32,128]{1,0:T(8,128)} %refs_6_.1) | copy-start | bytes 49156

commit v4 on v3

--- a/solution.py
+++ b/solution.py
@@ -16,6 +16,10 @@
 BOTH = ("row", "col")
 VMEM = pl.BlockSpec(memory_space=pltpu.VMEM)
 MIB = 1 << 20
+
+
+def in_hbm(x):
+    return pltpu.with_memory_space_constraint(x, pltpu.HBM)
 
 
 def steps():
@@ -53,14 +57,17 @@
         ask_ref[first : first + groups] = rows
 
 
-def tile_kernel(tile_hbm, row_ref, rhs_ref, mine_ref, held_hbm, place_ref, direction_ref, tile_buf, held_buf, in_sem, out_sem):
+def tile_kernel(tile_hbm, row_hbm, rhs_hbm, mine_ref, held_hbm, place_ref, direction_ref, tile_buf, held_buf, row_ref, rhs_ref, in_sem, out_sem, row_sem, rhs_sem):
     chunks = in_sem.shape[0]
     size = tile_hbm.shape[0] // chunks
     order = tile_hbm.shape[-1]
     fetches = [pltpu.make_async_copy(tile_hbm.at[pl.ds(c * size, size)], tile_buf.at[pl.ds(c * size, size)], in_sem.at[c]) for c in range(chunks)]
     stores = [pltpu.make_async_copy(held_buf.at[pl.ds(c * size, size)], held_hbm.at[pl.ds(c * size, size)], out_sem.at[c]) for c in range(chunks)]
-    for fetch in fetches:
+    small = [pltpu.make_async_copy(row_hbm, row_ref, row_sem), pltpu.make_async_copy(rhs_hbm, rhs_ref, rhs_sem)]
+    for fetch in small + fetches:
         fetch.start()
+    for fetch in small:
+        fetch.wait()
     direction_ref[...] = rhs_ref[...] * (1.0 / centre)
     slots, groups = row_ref.shape
     owned, spread = place_ref.shape
@@ -155,7 +162,7 @@
     small = jax.ShapeDtypeStruct((owned, order), f32)
     held, place, direction = pl.pallas_call(
         tile_kernel,
-        in_specs=[pl.BlockSpec(memory_space=pltpu.HBM), VMEM, VMEM, VMEM],
+        in_specs=[pl.BlockSpec(memory_space=pltpu.HBM)] * 3 + [VMEM],
         out_specs=[pl.BlockSpec(memory_space=pltpu.HBM), VMEM, VMEM],
         out_shape=[
             pltpu.HBM((wanted, 2 * order, order), jnp.bfloat16),
@@ -165,11 +172,15 @@
         scratch_shapes=[
             pltpu.VMEM((wanted, order, order), f32),
             pltpu.VMEM((wanted, 2 * order, order), jnp.bfloat16),
+            pltpu.VMEM((slots, groups), jnp.int32),
+            pltpu.VMEM((owned, order), f32),
             pltpu.SemaphoreType.DMA((chunks,)),
             pltpu.SemaphoreType.DMA((chunks,)),
+            pltpu.SemaphoreType.DMA,
+            pltpu.SemaphoreType.DMA,
         ],
         compiler_params=pltpu.CompilerParams(vmem_limit_bytes=16 * MIB),
-    )(pltpu.with_memory_space_constraint(tiles.reshape(wanted, order, order), pltpu.HBM), tile_row[0].T, rhs, mine)
+    )(in_hbm(tiles.reshape(wanted, order, order)), in_hbm(tile_row[0].T), in_hbm(rhs), mine)
 
     pick, send = pl.pallas_call(
         start_kernel,

time: 284 us -> 283 us (level)
  transfers between devices with their start and end apart: 1 -> 1, of which waited for: 1 -> 1; matrix products, arithmetic and copies ran while one was open for 0% -> 0% of each run, Pallas kernels for 1% -> 2%
where the time goes in v4:
time: 283 us
  blocking collectives  243 us (86%)
  Pallas kernels  21.7 us (8%)
  starting transfers between devices  11.5 us (4%)
  waiting for transfers between devices  5.23 us (2%)
    all_to_all x16, blocking collectives, per_device(): lax.all_to_all(send.reshape(devices, slots, order), BOTH, 0, 0, tiled=True)  243 us
    pallas_call x16, Pallas kernels, per_device(): pl.pallas_call(functools.partial(step_kernel, keep, gain, first, last), i...  16.1 us
    all_to_all x1, starting transfers between devices, per_device(): want = lax.all_to_all(asked[:, None], BOTH, 0, 0, tiled=True)[:, 0]  11.5 us
  transfers between devices with their start and end apart: 1, of which 1 were waited for; matrix products, arithmetic and copies ran while one was open for 0% of the time, Pallas kernels for 2%

profile of v4, /device:TPU:1, one launch (start us, length us, event | category | flops | bytes accessed | tf_op | source)
XLA Modules:
  0.0 282.7 jit_solution(8844887277498554643)
XLA Ops:
  0.6 0.0 copy-start.3
  0.6 0.7 copy-done.3
  1.3 0.7 shard_map.68
  2.0 11.5 %all-to-all-start = ((s32[128,1,128]{2,1,0:T(1,128)}), s32[128,1,128]{2,1,0:T(1,128)S(1)}, u32[]{:S(2)}, u32[]{:S(2)}) async-start(s32[128,1,128]{2,1,0:T(1,128)} %bitcast.3), calls=%async_computation | async-start | bytes 131072 | tf_op jit(solution)/shard_map/all_to_all | solution.py:156
  13.5 4.6 %shard_map.69 = (bf16[64,256,128]{2,1,0:T(8,128)(2,1)}, bf16[32,192]{1,0:T(8,128)(2,1)S(1)}, f32[32,128]{1,0:T(8,128)S(1)}) custom-call(f32[64,128,128]{2,1,0:T(8,128)} %bitcast.77, s32[4,16]{1,0:T(4,128)} %bitcast.78, f32[32,128]{1,0:T(8,128)} %refs_6_.1, s32[1,128]{1,0:T(1,128)S(1)} %compare_select_fusion.mine_ref), custom_call_target="tpu_custom_call" | custom-call | tf_op jit(solution)/shard_map/pallas_call | solution.py:163
  18.1 5.2 %all-to-all-done = s32[128,1,128]{2,1,0:T(1,128)S(1)} async-done(((s32[128,1,128]{2,1,0:T(1,128)}), s32[128,1,128]{2,1,0:T(1,128)S(1)}, u32[]{:S(2)}, u32[]{:S(2)}) %all-to-all-start) | async-done | bytes 65568 | tf_op jit(solution)/shard_map/all_to_all | solution.py:156
  23.4 0.0 copy-start
  23.4 0.0 copy-start.1
  23.4 0.0 copy-start.2
  23.4 0.3 shard_map.70
  23.7 15.8 %all_to_all.85 = f32[128,4,128]{2,1,0:T(4,128)S(1)} all-to-all(f32[128,4,128]{2,1,0:T(4,128)S(1)} %bitcast.74), channel_id=1, replica_groups=mesh['row'=8,'col'=16] {'row','col'}, dimensions={0} | all-to-all | bytes 524288 | tf_op jit(solution)/shard_map/all_to_all | solution.py:201
  39.5 0.0 copy-done
  39.5 0.0 copy-done.1
  39.5 0.0 copy-done.2
  39.5 1.0 shard_map.71
  40.4 15.1 %all_to_all.86 = f32[128,4,128]{2,1,0:T(4,128)S(1)} all-to-all(f32[128,4,128]{2,1,0:T(4,128)S(1)} %bitcast.73), channel_id=1, replica_groups=mesh['row'=8,'col'=16] {'row','col'}, dimensions={0} | all-to-all | bytes 524288 | tf_op jit(solution)/shard_map/all_to_all | solution.py:201
  55.6 1.0 shard_map.72
  56.6 15.1 %all_to_all.87 = f32[128,4,128]{2,1,0:T(4,128)S(1)} all-to-all(f32[128,4,128]{2,1,0:T(4,128)S(1)} %bitcast.59), channel_id=1, replica_groups=mesh['row'=8,'col'=16] {'row','col'}, dimensions={0} | all-to-all | bytes 524288 | tf_op jit(solution)/shard_map/all_to_all | solution.py:201
  71.7 1.0 shard_map.73
  72.7 15.1 %all_to_all.88 = f32[128,4,128]{2,1,0:T(4,128)S(1)} all-to-all(f32[128,4,128]{2,1,0:T(4,128)S(1)} %bitcast.60), channel_id=1, replica_groups=mesh['row'=8,'col'=16] {'row','col'}, dimensions={0} | all-to-all | bytes 524288 | tf_op jit(solution)/shard_map/all_to_all | solution.py:201
  87.8 1.0 shard_map.74
  88.8 15.1 %all_to_all.89 = f32[128,4,128]{2,1,0:T(4,128)S(1)} all-to-all(f32[128,4,128]{2,1,0:T(4,128)S(1)} %bitcast.61), channel_id=1, replica_groups=mesh['row'=8,'col'=16] {'row','col'}, dimensions={0} | all-to-all | bytes 524288 | tf_op jit(solution)/shard_map/all_to_all | solution.py:201
  103.9 1.0 shard_map.75
  104.9 15.1 %all_to_all.90 = f32[128,4,128]{2,1,0:T(4,128)S(1)} all-to-all(f32[128,4,128]{2,1,0:T(4,128)S(1)} %bitcast.62), channel_id=1, replica_groups=mesh['row'=8,'col'=16] {'row','col'}, dimensions={0} | all-to-all | bytes 524288 | tf_op jit(solution)/shard_map/all_to_all | solution.py:201
  120.1 1.0 shard_map.76
  121.0 15.1 %all_to_all.91 = f32[128,4,128]{2,1,0:T(4,128)S(1)} all-to-all(f32[128,4,128]{2,1,0:T(4,128)S(1)} %bitcast.63), channel_id=1, replica_groups=mesh['row'=8,'col'=16] {'row','col'}, dimensions={0} | all-to-all | bytes 524288 | tf_op jit(solution)/shard_map/all_to_all | solution.py:201
  136.2 1.0 shard_map.77
  137.2 15.1 %all_to_all.92 = f32[128,4,128]{2,1,0:T(4,128)S(1)} all-to-all(f32[128,4,128]{2,1,0:T(4,128)S(1)} %bitcast.64), channel_id=1, replica_groups=mesh['row'=8,'col'=16] {'row','col'}, dimensions={0} | all-to-all | bytes 524288 | tf_op jit(solution)/shard_map/all_to_all | solution.py:201
  152.3 1.0 shard_map.78
  153.3 15.1 %all_to_all.93 = f32[128,4,128]{2,1,0:T(4,128)S(1)} all-to-all(f32[128,4,128]{2,1,0:T(4,128)S(1)} %bitcast.65), channel_id=1, replica_groups=mesh['row'=8,'col'=16] {'row','col'}, dimensions={0} | all-to-all | bytes 524288 | tf_op jit(solution)/shard_map/all_to_all | solution.py:201
  168.4 1.0 shard_map.79
  169.4 15.1 %all_to_all.94 = f32[128,4,128]{2,1,0:T(4,128)S(1)} all-to-all(f32[128,4,128]{2,1,0:T(4,128)S(1)} %bitcast.66), channel_id=1, replica_groups=mesh['row'=8,'col'=16] {'row','col'}, dimensions={0} | all-to-all | bytes 524288 | tf_op jit(solution)/shard_map/all_to_all | solution.py:201
  184.5 1.0 shard_map.80
  185.5 15.1 %all_to_all.95 = f32[128,4,128]{2,1,0:T(4,128)S(1)} all-to-all(f32[128,4,128]{2,1,0:T(4,128)S(1)} %bitcast.67), channel_id=1, replica_groups=mesh['row'=8,'col'=16] {'row','col'}, dimensions={0} | all-to-all | bytes 524288 | tf_op jit(solution)/shard_map/all_to_all | solution.py:201
  200.6 1.0 shard_map.81
  201.6 15.1 %all_to_all.96 = f32[128,4,128]{2,1,0:T(4,128)S(1)} all-to-all(f32[128,4,128]{2,1,0:T(4,128)S(1)} %bitcast.68), channel_id=1, replica_groups=mesh['row'=8,'col'=16] {'row','col'}, dimensions={0} | all-to-all | bytes 524288 | tf_op jit(solution)/shard_map/all_to_all | solution.py:201
  216.8 1.0 shard_map.82
  217.7 15.1 %all_to_all.97 = f32[128,4,128]{2,1,0:T(4,128)S(1)} all-to-all(f32[128,4,128]{2,1,0:T(4,128)S(1)} %bitcast.69), channel_id=1, replica_groups=mesh['row'=8,'col'=16] {'row','col'}, dimensions={0} | all-to-all | bytes 524288 | tf_op jit(solution)/shard_map/all_to_all | solution.py:201
  232.9 1.0 shard_map.83
  233.9 15.1 %all_to_all.98 = f32[128,4,128]{2,1,0:T(4,128)S(1)} all-to-all(f32[128,4,128]{2,1,0:T(4,128)S(1)} %bitcast.70), channel_id=1, replica_groups=mesh['row'=8,'col'=16] {'row','col'}, dimensions={0} | all-to-all | bytes 524288 | tf_op jit(solution)/shard_map/all_to_all | solution.py:201
  249.0 1.0 shard_map.84
  250.0 15.1 %all_to_all.99 = f32[128,4,128]{2,1,0:T(4,128)S(1)} all-to-all(f32[128,4,128]{2,1,0:T(4,128)S(1)} %bitcast.71), channel_id=1, replica_groups=mesh['row'=8,'col'=16] {'row','col'}, dimensions={0} | all-to-all | bytes 524288 | tf_op jit(solution)/shard_map/all_to_all | solution.py:201
  265.1 1.0 shard_map.85
  266.1 15.1 %all_to_all.100 = f32[128,4,128]{2,1,0:T(4,128)S(1)} all-to-all(f32[128,4,128]{2,1,0:T(4,128)S(1)} %bitcast.72), channel_id=1, replica_groups=mesh['row'=8,'col'=16] {'row','col'}, dimensions={0} | all-to-all | bytes 524288 | tf_op jit(solution)/shard_map/all_to_all | solution.py:201
  281.2 1.4 shard_map.86
  (1 shorter events, 0.0 us)
Async XLA Ops:
  0.6 0.7 copy-start.3
  2.0 21.3 %all-to-all-start = ((s32[128,1,128]{2,1,0:T(1,128)}), s32[128,1,128]{2,1,0:T(1,128)S(1)}, u32[]{:S(2)}, u32[]{:S(2)}) async-start(s32[128,1,128]{2,1,0:T(1,128)} %bitcast.3), calls=%async_computation | async-start | bytes 131072 | tf_op jit(solution)/shard_map/all_to_all | solution.py:156
  23.4 16.1 %copy-start = (bf16[64,256,128]{2,1,0:T(8,128)(2,1)S(1)}, bf16[64,256,128]{2,1,0:T(8,128)(2,1)}, u32[]{:S(2)}) copy-start(bf16[64,256,128]{2,1,0:T(8,128)(2,1)} %get-tuple-element.69.refs_1_) | copy-start | bytes 12582916
  23.4 16.1 %copy-start.1 = (f32[32,128]{1,0:T(8,128)S(1)}, f32[32,128]{1,0:T(8,128)}, u32[]{:S(2)}) copy-start(f32[32,128]{1,0:T(8,128)} %refs_4_.31) | copy-start | bytes 49156
  23.4 16.1 %copy-start.2 = (f32[32,128]{1,0:T(8,128)S(1)}, f32[32,128]{1,0:T(8,128)}, u32[]{:S(2)}) copy-start(f32[32,128]{1,0:T(8,128)} %refs_6_.1) | copy-start | bytes 49156

commit v5 on v4

--- a/solution.py
+++ b/solution.py
@@ -66,22 +66,6 @@
     small = [pltpu.make_async_copy(row_hbm, row_ref, row_sem), pltpu.make_async_copy(rhs_hbm, rhs_ref, rhs_sem)]
     for fetch in small + fetches:
         fetch.start()
-    for fetch in small:
-        fetch.wait()
-    direction_ref[...] = rhs_ref[...] * (1.0 / centre)
-    slots, groups = row_ref.shape
-    owned, spread = place_ref.shape
-    wanted = slots * groups
-    source = lax.broadcasted_iota(jnp.int32, (groups, spread), 0)
-    target = lax.broadcasted_iota(jnp.int32, (groups, spread), 1) % wanted
-    targets = jnp.zeros((8, spread), jnp.float32)
-    rows = row_ref[...].astype(jnp.float32)
-    for slot in range(slots):
-        expand = jnp.where(target == source * slots + slot, 1.0, 0.0).astype(jnp.bfloat16)
-        line = jnp.broadcast_to(rows[slot : slot + 1], (8, groups)).astype(jnp.bfloat16)
-        targets = targets + jnp.dot(line, expand, preferred_element_type=jnp.float32)
-    block = lax.broadcasted_iota(jnp.int32, (owned, spread), 0)
-    place_ref[...] = jnp.where(block == targets[:1].astype(jnp.int32), 1.0, 0.0).astype(jnp.bfloat16)
     for c in range(chunks):
         fetches[c].wait()
         for tile in range(c * size, (c + 1) * size):
@@ -90,6 +74,25 @@
             held_buf[tile, :order] = high
             held_buf[tile, order:] = (flipped - high.astype(jnp.float32)).astype(jnp.bfloat16)
         stores[c].start()
+    for fetch in small:
+        fetch.wait()
+    direction_ref[...] = rhs_ref[...] * (1.0 / centre)
+    slots, groups = row_ref.shape
+    wanted, owned, spread = place_ref.shape
+    source = lax.broadcasted_iota(jnp.int32, (groups, spread), 0)
+    target = lax.broadcasted_iota(jnp.int32, (groups, spread), 1)
+    targets = jnp.zeros((8, spread), jnp.float32)
+    rows = row_ref[...].astype(jnp.float32)
+    for slot in range(slots):
+        expand = jnp.where(target == source * slots + slot, 1.0, 0.0).astype(jnp.bfloat16)
+        line = jnp.broadcast_to(rows[slot : slot + 1], (8, groups)).astype(jnp.bfloat16)
+        targets = targets + jnp.dot(line, expand, preferred_element_type=jnp.float32)
+    targets = targets.astype(jnp.int32)
+    block = lax.broadcasted_iota(jnp.int32, (8, spread), 0)
+    for tile in range(wanted):
+        line = jnp.broadcast_to(targets[:, tile : tile + 1], (8, spread))
+        for first in range(0, owned, 8):
+            place_ref[tile, first : first + 8] = jnp.where(block + first == line, 1.0, 0.0)
     for store in stores:
         store.wait()
 
@@ -115,19 +118,15 @@
         vec = vec + got_ref[sender]
     high = vec.astype(jnp.bfloat16).astype(jnp.float32)
     low = vec - high
-    lane_row = lax.broadcasted_iota(jnp.int32, (8, order), 0)
-    products = []
+    off = jnp.zeros(direction_ref.shape, jnp.float32)
     for block in range(wanted // 8):
         rows = slice(8 * block, 8 * block + 8)
         left = jnp.concatenate([high[rows], low[rows]], axis=0).astype(jnp.bfloat16)
         left = jnp.concatenate([left, left], axis=1)
-        total = jnp.zeros((8, order), jnp.float32)
         for slot in range(8):
             out = jnp.dot(left, held_ref[8 * block + slot], preferred_element_type=jnp.float32)
-            total = jnp.where(lane_row == slot, out[:8] + out[8:], total)
-        products.append(total)
-    products = jnp.concatenate(products, axis=0)
-    off = jnp.dot(place_ref[...], jnp.concatenate(three_parts(products), axis=0), preferred_element_type=jnp.float32)
+            row = out[slot : slot + 1] + out[8 + slot : 9 + slot]
+            off = off + place_ref[8 * block + slot] * row
     direction = direction_ref[...]
     residual = residual_ref[...] - (diag_ref[...] * direction - off)
     out_refs[0][...] = direction if first else refs[7][...] + direction
@@ -166,7 +165,7 @@
         out_specs=[pl.BlockSpec(memory_space=pltpu.HBM), VMEM, VMEM],
         out_shape=[
             pltpu.HBM((wanted, 2 * order, order), jnp.bfloat16),
-            jax.ShapeDtypeStruct((owned, 3 * wanted), jnp.bfloat16),
+            jax.ShapeDtypeStruct((wanted, owned, order), f32),
             small,
         ],
         scratch_shapes=[

time: 283 us -> 281 us (level)
  Pallas kernels: 21.7 us -> 18.8 us
  transfers between devices with their start and end apart: 1 -> 1, of which waited for: 1 -> 1; matrix products, arithmetic and copies ran while one was open for 0% -> 0% of each run, Pallas kernels for 2% -> 1%
where the time goes in v5:
time: 281 us; the launch traced here: 280 us
  blocking collectives  242 us (86%)
  Pallas kernels  18.8 us (7%)
  starting transfers between devices  11.5 us (4%)
  waiting for transfers between devices  6.17 us (2%)
    all_to_all x16, blocking collectives, per_device(): lax.all_to_all(send.reshape(devices, slots, order), BOTH, 0, 0, tiled=True)  242 us
    pallas_call x16, Pallas kernels, per_device(): pl.pallas_call(functools.partial(step_kernel, keep, gain, first, last), i...  14.1 us
    all_to_all x1, starting transfers between devices, per_device(): want = lax.all_to_all(asked[:, None], BOTH, 0, 0, tiled=True)[:, 0]  11.5 us
    all_to_all x1, waiting for transfers between devices, per_device(): want = lax.all_to_all(asked[:, None], BOTH, 0, 0, tiled=True)[:, 0]  6.17 us
  transfers between devices with their start and end apart: 1, of which 1 were waited for; matrix products, arithmetic and copies ran while one was open for 0% of the time, Pallas kernels for 1%

profile of v5, /device:TPU:1, one launch (start us, length us, event | category | flops | bytes accessed | tf_op | source)
XLA Modules:
  0.0 280.3 jit_solution(9169530523041807962)
XLA Ops:
  0.6 0.0 copy-start.3
  0.6 0.7 copy-done.3
  1.3 0.7 shard_map.68
  2.0 11.5 %all-to-all-start = ((s32[128,1,128]{2,1,0:T(1,128)}), s32[128,1,128]{2,1,0:T(1,128)S(1)}, u32[]{:S(2)}, u32[]{:S(2)}) async-start(s32[128,1,128]{2,1,0:T(1,128)} %bitcast.3), calls=%async_computation | async-start | bytes 131072 | tf_op jit(solution)/shard_map/all_to_all | solution.py:155
  13.5 3.7 %shard_map.69 = (bf16[64,256,128]{2,1,0:T(8,128)(2,1)}, f32[64,32,128]{2,1,0:T(8,128)S(1)}, f32[32,128]{1,0:T(8,128)S(1)}) custom-call(f32[64,128,128]{2,1,0:T(8,128)} %bitcast.77, s32[4,16]{1,0:T(4,128)} %bitcast.78, f32[32,128]{1,0:T(8,128)} %refs_6_.1, s32[1,128]{1,0:T(1,128)S(1)} %compare_select_fusion.mine_ref), custom_call_target="tpu_custom_call" | custom-call | tf_op jit(solution)/shard_map/pallas_call | solution.py:162
  17.2 6.2 %all-to-all-done = s32[128,1,128]{2,1,0:T(1,128)S(1)} async-done(((s32[128,1,128]{2,1,0:T(1,128)}), s32[128,1,128]{2,1,0:T(1,128)S(1)}, u32[]{:S(2)}, u32[]{:S(2)}) %all-to-all-start) | async-done | bytes 65568 | tf_op jit(solution)/shard_map/all_to_all | solution.py:155
  23.4 0.0 copy-start
  23.4 0.0 copy-start.1
  23.4 0.0 copy-start.2
  23.4 0.3 shard_map.70
  23.7 15.3 %all_to_all.85 = f32[128,4,128]{2,1,0:T(4,128)S(1)} all-to-all(f32[128,4,128]{2,1,0:T(4,128)S(1)} %bitcast.74), channel_id=1, replica_groups=mesh['row'=8,'col'=16] {'row','col'}, dimensions={0} | all-to-all | bytes 524288 | tf_op jit(solution)/shard_map/all_to_all | solution.py:200
  39.0 0.0 copy-done
  39.0 0.0 copy-done.1
  39.0 0.0 copy-done.2
  39.0 0.9 shard_map.71
  39.9 15.1 %all_to_all.86 = f32[128,4,128]{2,1,0:T(4,128)S(1)} all-to-all(f32[128,4,128]{2,1,0:T(4,128)S(1)} %bitcast.73), channel_id=1, replica_groups=mesh['row'=8,'col'=16] {'row','col'}, dimensions={0} | all-to-all | bytes 524288 | tf_op jit(solution)/shard_map/all_to_all | solution.py:200
  55.0 0.9 shard_map.72
  55.9 15.1 %all_to_all.87 = f32[128,4,128]{2,1,0:T(4,128)S(1)} all-to-all(f32[128,4,128]{2,1,0:T(4,128)S(1)} %bitcast.59), channel_id=1, replica_groups=mesh['row'=8,'col'=16] {'row','col'}, dimensions={0} | all-to-all | bytes 524288 | tf_op jit(solution)/shard_map/all_to_all | solution.py:200
  71.0 0.9 shard_map.73
  71.9 15.1 %all_to_all.88 = f32[128,4,128]{2,1,0:T(4,128)S(1)} all-to-all(f32[128,4,128]{2,1,0:T(4,128)S(1)} %bitcast.60), channel_id=1, replica_groups=mesh['row'=8,'col'=16] {'row','col'}, dimensions={0} | all-to-all | bytes 524288 | tf_op jit(solution)/shard_map/all_to_all | solution.py:200
  87.0 0.9 shard_map.74
  87.9 15.1 %all_to_all.89 = f32[128,4,128]{2,1,0:T(4,128)S(1)} all-to-all(f32[128,4,128]{2,1,0:T(4,128)S(1)} %bitcast.61), channel_id=1, replica_groups=mesh['row'=8,'col'=16] {'row','col'}, dimensions={0} | all-to-all | bytes 524288 | tf_op jit(solution)/shard_map/all_to_all | solution.py:200
  103.0 0.9 shard_map.75
  103.9 15.1 %all_to_all.90 = f32[128,4,128]{2,1,0:T(4,128)S(1)} all-to-all(f32[128,4,128]{2,1,0:T(4,128)S(1)} %bitcast.62), channel_id=1, replica_groups=mesh['row'=8,'col'=16] {'row','col'}, dimensions={0} | all-to-all | bytes 524288 | tf_op jit(solution)/shard_map/all_to_all | solution.py:200
  119.0 0.9 shard_map.76
  119.9 15.1 %all_to_all.91 = f32[128,4,128]{2,1,0:T(4,128)S(1)} all-to-all(f32[128,4,128]{2,1,0:T(4,128)S(1)} %bitcast.63), channel_id=1, replica_groups=mesh['row'=8,'col'=16] {'row','col'}, dimensions={0} | all-to-all | bytes 524288 | tf_op jit(solution)/shard_map/all_to_all | solution.py:200
  135.0 0.9 shard_map.77
  135.9 15.1 %all_to_all.92 = f32[128,4,128]{2,1,0:T(4,128)S(1)} all-to-all(f32[128,4,128]{2,1,0:T(4,128)S(1)} %bitcast.64), channel_id=1, replica_groups=mesh['row'=8,'col'=16] {'row','col'}, dimensions={0} | all-to-all | bytes 524288 | tf_op jit(solution)/shard_map/all_to_all | solution.py:200
  151.0 0.9 shard_map.78
  151.9 15.1 %all_to_all.93 = f32[128,4,128]{2,1,0:T(4,128)S(1)} all-to-all(f32[128,4,128]{2,1,0:T(4,128)S(1)} %bitcast.65), channel_id=1, replica_groups=mesh['row'=8,'col'=16] {'row','col'}, dimensions={0} | all-to-all | bytes 524288 | tf_op jit(solution)/shard_map/all_to_all | solution.py:200
  167.0 0.9 shard_map.79
  167.9 15.1 %all_to_all.94 = f32[128,4,128]{2,1,0:T(4,128)S(1)} all-to-all(f32[128,4,128]{2,1,0:T(4,128)S(1)} %bitcast.66), channel_id=1, replica_groups=mesh['row'=8,'col'=16] {'row','col'}, dimensions={0} | all-to-all | bytes 524288 | tf_op jit(solution)/shard_map/all_to_all | solution.py:200
  183.0 0.9 shard_map.80
  183.9 15.1 %all_to_all.95 = f32[128,4,128]{2,1,0:T(4,128)S(1)} all-to-all(f32[128,4,128]{2,1,0:T(4,128)S(1)} %bitcast.67), channel_id=1, replica_groups=mesh['row'=8,'col'=16] {'row','col'}, dimensions={0} | all-to-all | bytes 524288 | tf_op jit(solution)/shard_map/all_to_all | solution.py:200
  199.0 0.9 shard_map.81
  199.9 15.1 %all_to_all.96 = f32[128,4,128]{2,1,0:T(4,128)S(1)} all-to-all(f32[128,4,128]{2,1,0:T(4,128)S(1)} %bitcast.68), channel_id=1, replica_groups=mesh['row'=8,'col'=16] {'row','col'}, dimensions={0} | all-to-all | bytes 524288 | tf_op jit(solution)/shard_map/all_to_all | solution.py:200
  215.0 0.9 shard_map.82
  215.8 15.1 %all_to_all.97 = f32[128,4,128]{2,1,0:T(4,128)S(1)} all-to-all(f32[128,4,128]{2,1,0:T(4,128)S(1)} %bitcast.69), channel_id=1, replica_groups=mesh['row'=8,'col'=16] {'row','col'}, dimensions={0} | all-to-all | bytes 524288 | tf_op jit(solution)/shard_map/all_to_all | solution.py:200
  231.0 0.9 shard_map.83
  231.8 15.1 %all_to_all.98 = f32[128,4,128]{2,1,0:T(4,128)S(1)} all-to-all(f32[128,4,128]{2,1,0:T(4,128)S(1)} %bitcast.70), channel_id=1, replica_groups=mesh['row'=8,'col'=16] {'row','col'}, dimensions={0} | all-to-all | bytes 524288 | tf_op jit(solution)/shard_map/all_to_all | solution.py:200
  247.0 0.9 shard_map.84
  247.8 15.1 %all_to_all.99 = f32[128,4,128]{2,1,0:T(4,128)S(1)} all-to-all(f32[128,4,128]{2,1,0:T(4,128)S(1)} %bitcast.71), channel_id=1, replica_groups=mesh['row'=8,'col'=16] {'row','col'}, dimensions={0} | all-to-all | bytes 524288 | tf_op jit(solution)/shard_map/all_to_all | solution.py:200
  263.0 0.9 shard_map.85
  263.8 15.1 %all_to_all.100 = f32[128,4,128]{2,1,0:T(4,128)S(1)} all-to-all(f32[128,4,128]{2,1,0:T(4,128)S(1)} %bitcast.72), channel_id=1, replica_groups=mesh['row'=8,'col'=16] {'row','col'}, dimensions={0} | all-to-all | bytes 524288 | tf_op jit(solution)/shard_map/all_to_all | solution.py:200
  279.0 1.3 shard_map.86
  (1 shorter events, 0.0 us)
Async XLA Ops:
  0.6 0.7 copy-start.3
  2.0 21.3 %all-to-all-start = ((s32[128,1,128]{2,1,0:T(1,128)}), s32[128,1,128]{2,1,0:T(1,128)S(1)}, u32[]{:S(2)}, u32[]{:S(2)}) async-start(s32[128,1,128]{2,1,0:T(1,128)} %bitcast.3), calls=%async_computation | async-start | bytes 131072 | tf_op jit(solution)/shard_map/all_to_all | solution.py:155
  23.4 15.7 %copy-start = (bf16[64,256,128]{2,1,0:T(8,128)(2,1)S(1)}, bf16[64,256,128]{2,1,0:T(8,128)(2,1)}, u32[]{:S(2)}) copy-start(bf16[64,256,128]{2,1,0:T(8,128)(2,1)} %get-tuple-element.69.refs_1_) | copy-start | bytes 12582916
  23.4 15.7 %copy-start.1 = (f32[32,128]{1,0:T(8,128)S(1)}, f32[32,128]{1,0:T(8,128)}, u32[]{:S(2)}) copy-start(f32[32,128]{1,0:T(8,128)} %refs_4_.31) | copy-start | bytes 49156
  23.4 15.7 %copy-start.2 = (f32[32,128]{1,0:T(8,128)S(1)}, f32[32,128]{1,0:T(8,128)}, u32[]{:S(2)}) copy-start(f32[32,128]{1,0:T(8,128)} %refs_6_.1) | copy-start | bytes 49156

commit v6 on v5

--- a/solution.py
+++ b/solution.py
@@ -33,18 +33,11 @@
     return pairs
 
 
-def three_parts(x):
-    high = x.astype(jnp.bfloat16)
-    rest = x - high.astype(jnp.float32)
-    middle = rest.astype(jnp.bfloat16)
-    low = (rest - middle.astype(jnp.float32)).astype(jnp.bfloat16)
-    return [high, middle, low]
-
-
 def to_send(pick, direction):
-    parts = three_parts(direction)
-    parts.append(jnp.zeros_like(parts[0]))
-    return jnp.dot(pick, jnp.concatenate(parts, axis=0), preferred_element_type=jnp.float32)
+    high = direction.astype(jnp.bfloat16)
+    low = (direction - high.astype(jnp.float32)).astype(jnp.bfloat16)
+    parts = jnp.concatenate([high, low], axis=0)
+    return jnp.dot(pick[:, : parts.shape[0]], parts, preferred_element_type=jnp.float32)
 
 
 def ask_kernel(col_ref, ask_ref):
@@ -155,7 +148,7 @@
     want = lax.all_to_all(asked[:, None], BOTH, 0, 0, tiled=True)[:, 0]
 
     lane = jnp.arange(order, dtype=jnp.int32)
-    mine = jnp.where(lane < 3 * owned, lax.axis_index("row") * owned + lane % owned, -1)[None, :]
+    mine = jnp.where(lane < 2 * owned, lax.axis_index("row") * owned + lane % owned, -1)[None, :]
 
     chunks = 8
     small = jax.ShapeDtypeStruct((owned, order), f32)

time: 281 us -> 281 us (level)
  no operation moved by 1% of the time
where the time goes in v6:
time: 281 us; the launch traced here: 280 us
  blocking collectives  242 us (86%)
  Pallas kernels  18.7 us (7%)
  starting transfers between devices  11.5 us (4%)
  waiting for transfers between devices  6.17 us (2%)
    all_to_all x16, blocking collectives, per_device(): lax.all_to_all(send.reshape(devices, slots, order), BOTH, 0, 0, tiled=True)  242 us
    pallas_call x16, Pallas kernels, per_device(): pl.pallas_call(functools.partial(step_kernel, keep, gain, first, last), i...  14 us
    all_to_all x1, starting transfers between devices, per_device(): want = lax.all_to_all(asked[:, None], BOTH, 0, 0, tiled=True)[:, 0]  11.5 us
    all_to_all x1, waiting for transfers between devices, per_device(): want = lax.all_to_all(asked[:, None], BOTH, 0, 0, tiled=True)[:, 0]  6.17 us
  transfers between devices with their start and end apart: 1, of which 1 were waited for; matrix products, arithmetic and copies ran while one was open for 0% of the time, Pallas kernels for 1%

profile of v6, /device:TPU:1, one launch (start us, length us, event | category | flops | bytes accessed | tf_op | source)
XLA Modules:
  0.0 280.2 jit_solution(10695683362658356330)
XLA Ops:
  0.6 0.0 copy-start.3
  0.6 0.7 copy-done.3
  1.3 0.7 shard_map.68
  2.0 11.5 %all-to-all-start = ((s32[128,1,128]{2,1,0:T(1,128)}), s32[128,1,128]{2,1,0:T(1,128)S(1)}, u32[]{:S(2)}, u32[]{:S(2)}) async-start(s32[128,1,128]{2,1,0:T(1,128)} %bitcast.3), calls=%async_computation | async-start | bytes 131072 | tf_op jit(solution)/shard_map/all_to_all | solution.py:148
  13.5 3.7 %shard_map.69 = (bf16[64,256,128]{2,1,0:T(8,128)(2,1)}, f32[64,32,128]{2,1,0:T(8,128)S(1)}, f32[32,128]{1,0:T(8,128)S(1)}) custom-call(f32[64,128,128]{2,1,0:T(8,128)} %bitcast.77, s32[4,16]{1,0:T(4,128)} %bitcast.78, f32[32,128]{1,0:T(8,128)} %refs_6_.1, s32[1,128]{1,0:T(1,128)S(1)} %compare_select_fusion.mine_ref), custom_call_target="tpu_custom_call" | custom-call | tf_op jit(solution)/shard_map/pallas_call | solution.py:155
  17.2 6.2 %all-to-all-done = s32[128,1,128]{2,1,0:T(1,128)S(1)} async-done(((s32[128,1,128]{2,1,0:T(1,128)}), s32[128,1,128]{2,1,0:T(1,128)S(1)}, u32[]{:S(2)}, u32[]{:S(2)}) %all-to-all-start) | async-done | bytes 65568 | tf_op jit(solution)/shard_map/all_to_all | solution.py:148
  23.4 0.0 copy-start
  23.4 0.0 copy-start.1
  23.4 0.0 copy-start.2
  23.4 0.3 shard_map.70
  23.7 15.3 %all_to_all.85 = f32[128,4,128]{2,1,0:T(4,128)S(1)} all-to-all(f32[128,4,128]{2,1,0:T(4,128)S(1)} %bitcast.74), channel_id=1, replica_groups=mesh['row'=8,'col'=16] {'row','col'}, dimensions={0} | all-to-all | bytes 524288 | tf_op jit(solution)/shard_map/all_to_all | solution.py:193
  39.0 0.0 copy-done
  39.0 0.0 copy-done.1
  39.0 0.0 copy-done.2
  39.0 0.9 shard_map.71
  39.9 15.1 %all_to_all.86 = f32[128,4,128]{2,1,0:T(4,128)S(1)} all-to-all(f32[128,4,128]{2,1,0:T(4,128)S(1)} %bitcast.73), channel_id=1, replica_groups=mesh['row'=8,'col'=16] {'row','col'}, dimensions={0} | all-to-all | bytes 524288 | tf_op jit(solution)/shard_map/all_to_all | solution.py:193
  55.0 0.8 shard_map.72
  55.9 15.1 %all_to_all.87 = f32[128,4,128]{2,1,0:T(4,128)S(1)} all-to-all(f32[128,4,128]{2,1,0:T(4,128)S(1)} %bitcast.59), channel_id=1, replica_groups=mesh['row'=8,'col'=16] {'row','col'}, dimensions={0} | all-to-all | bytes 524288 | tf_op jit(solution)/shard_map/all_to_all | solution.py:193
  71.0 0.8 shard_map.73
  71.9 15.1 %all_to_all.88 = f32[128,4,128]{2,1,0:T(4,128)S(1)} all-to-all(f32[128,4,128]{2,1,0:T(4,128)S(1)} %bitcast.60), channel_id=1, replica_groups=mesh['row'=8,'col'=16] {'row','col'}, dimensions={0} | all-to-all | bytes 524288 | tf_op jit(solution)/shard_map/all_to_all | solution.py:193
  87.0 0.8 shard_map.74
  87.9 15.1 %all_to_all.89 = f32[128,4,128]{2,1,0:T(4,128)S(1)} all-to-all(f32[128,4,128]{2,1,0:T(4,128)S(1)} %bitcast.61), channel_id=1, replica_groups=mesh['row'=8,'col'=16] {'row','col'}, dimensions={0} | all-to-all | bytes 524288 | tf_op jit(solution)/shard_map/all_to_all | solution.py:193
  103.0 0.8 shard_map.75
  103.9 15.1 %all_to_all.90 = f32[128,4,128]{2,1,0:T(4,128)S(1)} all-to-all(f32[128,4,128]{2,1,0:T(4,128)S(1)} %bitcast.62), channel_id=1, replica_groups=mesh['row'=8,'col'=16] {'row','col'}, dimensions={0} | all-to-all | bytes 524288 | tf_op jit(solution)/shard_map/all_to_all | solution.py:193
  119.0 0.8 shard_map.76
  119.9 15.1 %all_to_all.91 = f32[128,4,128]{2,1,0:T(4,128)S(1)} all-to-all(f32[128,4,128]{2,1,0:T(4,128)S(1)} %bitcast.63), channel_id=1, replica_groups=mesh['row'=8,'col'=16] {'row','col'}, dimensions={0} | all-to-all | bytes 524288 | tf_op jit(solution)/shard_map/all_to_all | solution.py:193
  135.0 0.8 shard_map.77
  135.8 15.1 %all_to_all.92 = f32[128,4,128]{2,1,0:T(4,128)S(1)} all-to-all(f32[128,4,128]{2,1,0:T(4,128)S(1)} %bitcast.64), channel_id=1, replica_groups=mesh['row'=8,'col'=16] {'row','col'}, dimensions={0} | all-to-all | bytes 524288 | tf_op jit(solution)/shard_map/all_to_all | solution.py:193
  151.0 0.8 shard_map.78
  151.8 15.1 %all_to_all.93 = f32[128,4,128]{2,1,0:T(4,128)S(1)} all-to-all(f32[128,4,128]{2,1,0:T(4,128)S(1)} %bitcast.65), channel_id=1, replica_groups=mesh['row'=8,'col'=16] {'row','col'}, dimensions={0} | all-to-all | bytes 524288 | tf_op jit(solution)/shard_map/all_to_all | solution.py:193
  167.0 0.8 shard_map.79
  167.8 15.1 %all_to_all.94 = f32[128,4,128]{2,1,0:T(4,128)S(1)} all-to-all(f32[128,4,128]{2,1,0:T(4,128)S(1)} %bitcast.66), channel_id=1, replica_groups=mesh['row'=8,'col'=16] {'row','col'}, dimensions={0} | all-to-all | bytes 524288 | tf_op jit(solution)/shard_map/all_to_all | solution.py:193
  183.0 0.8 shard_map.80
  183.8 15.1 %all_to_all.95 = f32[128,4,128]{2,1,0:T(4,128)S(1)} all-to-all(f32[128,4,128]{2,1,0:T(4,128)S(1)} %bitcast.67), channel_id=1, replica_groups=mesh['row'=8,'col'=16] {'row','col'}, dimensions={0} | all-to-all | bytes 524288 | tf_op jit(solution)/shard_map/all_to_all | solution.py:193
  199.0 0.8 shard_map.81
  199.8 15.1 %all_to_all.96 = f32[128,4,128]{2,1,0:T(4,128)S(1)} all-to-all(f32[128,4,128]{2,1,0:T(4,128)S(1)} %bitcast.68), channel_id=1, replica_groups=mesh['row'=8,'col'=16] {'row','col'}, dimensions={0} | all-to-all | bytes 524288 | tf_op jit(solution)/shard_map/all_to_all | solution.py:193
  214.9 0.8 shard_map.82
  215.8 15.1 %all_to_all.97 = f32[128,4,128]{2,1,0:T(4,128)S(1)} all-to-all(f32[128,4,128]{2,1,0:T(4,128)S(1)} %bitcast.69), channel_id=1, replica_groups=mesh['row'=8,'col'=16] {'row','col'}, dimensions={0} | all-to-all | bytes 524288 | tf_op jit(solution)/shard_map/all_to_all | solution.py:193
  230.9 0.8 shard_map.83
  231.8 15.1 %all_to_all.98 = f32[128,4,128]{2,1,0:T(4,128)S(1)} all-to-all(f32[128,4,128]{2,1,0:T(4,128)S(1)} %bitcast.70), channel_id=1, replica_groups=mesh['row'=8,'col'=16] {'row','col'}, dimensions={0} | all-to-all | bytes 524288 | tf_op jit(solution)/shard_map/all_to_all | solution.py:193
  246.9 0.8 shard_map.84
  247.8 15.1 %all_to_all.99 = f32[128,4,128]{2,1,0:T(4,128)S(1)} all-to-all(f32[128,4,128]{2,1,0:T(4,128)S(1)} %bitcast.71), channel_id=1, replica_groups=mesh['row'=8,'col'=16] {'row','col'}, dimensions={0} | all-to-all | bytes 524288 | tf_op jit(solution)/shard_map/all_to_all | solution.py:193
  262.9 0.8 shard_map.85
  263.8 15.1 %all_to_all.100 = f32[128,4,128]{2,1,0:T(4,128)S(1)} all-to-all(f32[128,4,128]{2,1,0:T(4,128)S(1)} %bitcast.72), channel_id=1, replica_groups=mesh['row'=8,'col'=16] {'row','col'}, dimensions={0} | all-to-all | bytes 524288 | tf_op jit(solution)/shard_map/all_to_all | solution.py:193
  278.9 1.3 shard_map.86
  (1 shorter events, 0.0 us)
Async XLA Ops:
  0.6 0.7 copy-start.3
  2.0 21.3 %all-to-all-start = ((s32[128,1,128]{2,1,0:T(1,128)}), s32[128,1,128]{2,1,0:T(1,128)S(1)}, u32[]{:S(2)}, u32[]{:S(2)}) async-start(s32[128,1,128]{2,1,0:T(1,128)} %bitcast.3), calls=%async_computation | async-start | bytes 131072 | tf_op jit(solution)/shard_map/all_to_all | solution.py:148
  23.4 15.7 %copy-start = (bf16[64,256,128]{2,1,0:T(8,128)(2,1)S(1)}, bf16[64,256,128]{2,1,0:T(8,128)(2,1)}, u32[]{:S(2)}) copy-start(bf16[64,256,128]{2,1,0:T(8,128)(2,1)} %get-tuple-element.69.refs_1_) | copy-start | bytes 12582916
  23.4 15.7 %copy-start.1 = (f32[32,128]{1,0:T(8,128)S(1)}, f32[32,128]{1,0:T(8,128)}, u32[]{:S(2)}) copy-start(f32[32,128]{1,0:T(8,128)} %refs_4_.31) | copy-start | bytes 49156
  23.4 15.7 %copy-start.2 = (f32[32,128]{1,0:T(8,128)S(1)}, f32[32,128]{1,0:T(8,128)}, u32[]{:S(2)}) copy-start(f32[32,128]{1,0:T(8,128)} %refs_6_.1) | copy-start | bytes 49156

commit v7 on v6

--- a/solution.py
+++ b/solution.py
@@ -16,6 +16,7 @@
 BOTH = ("row", "col")
 VMEM = pl.BlockSpec(memory_space=pltpu.VMEM)
 MIB = 1 << 20
+PLAIN = 1
 
 
 def in_hbm(x):
@@ -50,23 +51,33 @@
         ask_ref[first : first + groups] = rows
 
 
-def tile_kernel(tile_hbm, row_hbm, rhs_hbm, mine_ref, held_hbm, place_ref, direction_ref, tile_buf, held_buf, row_ref, rhs_ref, in_sem, out_sem, row_sem, rhs_sem):
+def tile_kernel(tile_hbm, row_hbm, rhs_hbm, mine_ref, held_hbm, plain_hbm, place_ref, direction_ref, tile_buf, held_buf, plain_buf, row_ref, rhs_ref, in_sem, out_sem, row_sem, rhs_sem):
     chunks = in_sem.shape[0]
     size = tile_hbm.shape[0] // chunks
     order = tile_hbm.shape[-1]
     fetches = [pltpu.make_async_copy(tile_hbm.at[pl.ds(c * size, size)], tile_buf.at[pl.ds(c * size, size)], in_sem.at[c]) for c in range(chunks)]
-    stores = [pltpu.make_async_copy(held_buf.at[pl.ds(c * size, size)], held_hbm.at[pl.ds(c * size, size)], out_sem.at[c]) for c in range(chunks)]
+    stores = []
+    for c in range(chunks):
+        held_part = pl.ds(c * (size - PLAIN), size - PLAIN)
+        plain_part = pl.ds(c * PLAIN, PLAIN)
+        stores.append(pltpu.make_async_copy(held_buf.at[held_part], held_hbm.at[held_part], out_sem.at[c]))
+        stores.append(pltpu.make_async_copy(plain_buf.at[plain_part], plain_hbm.at[plain_part], out_sem.at[chunks + c]))
     small = [pltpu.make_async_copy(row_hbm, row_ref, row_sem), pltpu.make_async_copy(rhs_hbm, rhs_ref, rhs_sem)]
     for fetch in small + fetches:
         fetch.start()
     for c in range(chunks):
         fetches[c].wait()
-        for tile in range(c * size, (c + 1) * size):
-            flipped = tile_buf[tile].T
-            high = flipped.astype(jnp.bfloat16)
-            held_buf[tile, :order] = high
-            held_buf[tile, order:] = (flipped - high.astype(jnp.float32)).astype(jnp.bfloat16)
-        stores[c].start()
+        for spot in range(size):
+            flipped = tile_buf[c * size + spot].T
+            if spot < PLAIN:
+                plain_buf[c * PLAIN + spot] = flipped
+            else:
+                tile = c * (size - PLAIN) + spot - PLAIN
+                high = flipped.astype(jnp.bfloat16)
+                held_buf[tile, :order] = high
+                held_buf[tile, order:] = (flipped - high.astype(jnp.float32)).astype(jnp.bfloat16)
+        stores[2 * c].start()
+        stores[2 * c + 1].start()
     for fetch in small:
         fetch.wait()
     direction_ref[...] = rhs_ref[...] * (1.0 / centre)
@@ -103,26 +114,34 @@
 
 
 def step_kernel(keep, gain, first, last, *refs):
-    got_ref, held_ref, place_ref, pick_ref, diag_ref, direction_ref, residual_ref = refs[:7]
-    out_refs = refs[7:] if first else refs[8:]
+    got_ref, held_ref, plain_ref, place_ref, pick_ref, diag_ref, direction_ref, residual_ref = refs[:8]
+    out_refs = refs[8:] if first else refs[9:]
     senders, wanted, order = got_ref.shape
     vec = got_ref[0]
     for sender in range(1, senders):
         vec = vec + got_ref[sender]
     high = vec.astype(jnp.bfloat16).astype(jnp.float32)
     low = vec - high
+    column = vec.T
     off = jnp.zeros(direction_ref.shape, jnp.float32)
     for block in range(wanted // 8):
         rows = slice(8 * block, 8 * block + 8)
         left = jnp.concatenate([high[rows], low[rows]], axis=0).astype(jnp.bfloat16)
         left = jnp.concatenate([left, left], axis=1)
         for slot in range(8):
-            out = jnp.dot(left, held_ref[8 * block + slot], preferred_element_type=jnp.float32)
-            row = out[slot : slot + 1] + out[8 + slot : 9 + slot]
+            if slot < PLAIN:
+                tile = 8 * block + slot
+                row = jnp.zeros((8, order), jnp.float32)
+                for part in range(0, order, 8):
+                    row = row + plain_ref[PLAIN * block + slot, part : part + 8] * column[part : part + 8, tile : tile + 1]
+                row = jnp.sum(row, axis=0, keepdims=True)
+            else:
+                out = jnp.dot(left, held_ref[(8 - PLAIN) * block + slot - PLAIN], preferred_element_type=jnp.float32)
+                row = out[slot : slot + 1] + out[8 + slot : 9 + slot]
             off = off + place_ref[8 * block + slot] * row
     direction = direction_ref[...]
     residual = residual_ref[...] - (diag_ref[...] * direction - off)
-    out_refs[0][...] = direction if first else refs[7][...] + direction
+    out_refs[0][...] = direction if first else refs[8][...] + direction
     out_refs[1][...] = residual
     if not last:
         direction = keep * direction + gain * residual
@@ -152,22 +171,26 @@
 
     chunks = 8
     small = jax.ShapeDtypeStruct((owned, order), f32)
-    held, place, direction = pl.pallas_call(
+    held_shape = ((8 - PLAIN) * chunks, 2 * order, order)
+    plain_shape = (PLAIN * chunks, order, order)
+    held, plain, place, direction = pl.pallas_call(
         tile_kernel,
         in_specs=[pl.BlockSpec(memory_space=pltpu.HBM)] * 3 + [VMEM],
-        out_specs=[pl.BlockSpec(memory_space=pltpu.HBM), VMEM, VMEM],
+        out_specs=[pl.BlockSpec(memory_space=pltpu.HBM)] * 2 + [VMEM, VMEM],
         out_shape=[
-            pltpu.HBM((wanted, 2 * order, order), jnp.bfloat16),
+            pltpu.HBM(held_shape, jnp.bfloat16),
+            pltpu.HBM(plain_shape, f32),
             jax.ShapeDtypeStruct((wanted, owned, order), f32),
             small,
         ],
         scratch_shapes=[
             pltpu.VMEM((wanted, order, order), f32),
-            pltpu.VMEM((wanted, 2 * order, order), jnp.bfloat16),
+            pltpu.VMEM(held_shape, jnp.bfloat16),
+            pltpu.VMEM(plain_shape, f32),
             pltpu.VMEM((slots, groups), jnp.int32),
             pltpu.VMEM((owned, order), f32),
             pltpu.SemaphoreType.DMA((chunks,)),
-            pltpu.SemaphoreType.DMA((chunks,)),
+            pltpu.SemaphoreType.DMA((2 * chunks,)),
             pltpu.SemaphoreType.DMA,
             pltpu.SemaphoreType.DMA,
         ],
@@ -193,11 +216,11 @@
         got = lax.all_to_all(send.reshape(devices, slots, order), BOTH, 0, 0, tiled=True)
         outs = pl.pallas_call(
             functools.partial(step_kernel, keep, gain, first, last),
-            in_specs=[VMEM] * (7 if first else 8),
+            in_specs=[VMEM] * (8 if first else 9),
             out_specs=[VMEM] * (2 if last else 4),
             out_shape=[small, small] if last else [small, small, small, jax.ShapeDtypeStruct((devices * slots, order), f32)],
             compiler_params=pltpu.CompilerParams(vmem_limit_bytes=16 * MIB),
-        )(got.reshape(senders, wanted, order), held, place, pick, diag_vals, direction, residual, *pressure)
+        )(got.reshape(senders, wanted, order), held, plain, place, pick, diag_vals, direction, residual, *pressure)
         pressure, residual = [outs[0]], outs[1]
         if not last:
             direction, send = outs[2:]

time: 281 us -> 280 us (level)
  no operation moved by 1% of the time
where the time goes in v7:
time: 280 us
  blocking collectives  242 us (86%)
  Pallas kernels  18.2 us (6%)
  starting transfers between devices  11.5 us (4%)
  waiting for transfers between devices  6.07 us (2%)
    all_to_all x16, blocking collectives, per_device(): lax.all_to_all(send.reshape(devices, slots, order), BOTH, 0, 0, tiled=True)  242 us
    pallas_call x16, Pallas kernels, per_device(): pl.pallas_call(functools.partial(step_kernel, keep, gain, first, last), i...  13.5 us
    all_to_all x1, starting transfers between devices, per_device(): want = lax.all_to_all(asked[:, None], BOTH, 0, 0, tiled=True)[:, 0]  11.5 us
    all_to_all x1, waiting for transfers between devices, per_device(): want = lax.all_to_all(asked[:, None], BOTH, 0, 0, tiled=True)[:, 0]  6.07 us
  transfers between devices with their start and end apart: 1, of which 1 were waited for; matrix products, arithmetic and copies ran while one was open for 0% of the time, Pallas kernels for 1%

profile of v7, /device:TPU:1, one launch (start us, length us, event | category | flops | bytes accessed | tf_op | source)
XLA Modules:
  0.0 279.6 jit_solution(12926317014345017690)
XLA Ops:
  0.6 0.0 copy-start.4
  0.6 0.7 copy-done.4
  1.3 0.7 shard_map.68
  2.0 11.5 %all-to-all-start = ((s32[128,1,128]{2,1,0:T(1,128)}), s32[128,1,128]{2,1,0:T(1,128)S(1)}, u32[]{:S(2)}, u32[]{:S(2)}) async-start(s32[128,1,128]{2,1,0:T(1,128)} %bitcast.3), calls=%async_computation | async-start | bytes 131072 | tf_op jit(solution)/shard_map/all_to_all | solution.py:167
  13.5 3.7 %shard_map.69 = (bf16[56,256,128]{2,1,0:T(8,128)(2,1)}, f32[8,128,128]{2,1,0:T(8,128)}, f32[64,32,128]{2,1,0:T(8,128)S(1)}, f32[32,128]{1,0:T(8,128)S(1)}) custom-call(f32[64,128,128]{2,1,0:T(8,128)} %bitcast.77, s32[4,16]{1,0:T(4,128)} %bitcast.78, f32[32,128]{1,0:T(8,128)} %refs_7_.1, s32[1,128]{1,0:T(1,128)S(1)} %compare_select_fusion.mine_ref), custom_call_target="tpu_custom_call" | custom-call | tf_op jit(solution)/shard_map/pallas_call | solution.py:176
  17.3 6.1 %all-to-all-done = s32[128,1,128]{2,1,0:T(1,128)S(1)} async-done(((s32[128,1,128]{2,1,0:T(1,128)}), s32[128,1,128]{2,1,0:T(1,128)S(1)}, u32[]{:S(2)}, u32[]{:S(2)}) %all-to-all-start) | async-done | bytes 65568 | tf_op jit(solution)/shard_map/all_to_all | solution.py:167
  23.3 0.0 copy-start
  23.3 0.0 copy-start.1
  23.3 0.0 copy-start.2
  23.3 0.0 copy-start.3
  23.3 0.3 shard_map.70
  23.7 15.4 %all_to_all.85 = f32[128,4,128]{2,1,0:T(4,128)S(1)} all-to-all(f32[128,4,128]{2,1,0:T(4,128)S(1)} %bitcast.74), channel_id=1, replica_groups=mesh['row'=8,'col'=16] {'row','col'}, dimensions={0} | all-to-all | bytes 524288 | tf_op jit(solution)/shard_map/all_to_all | solution.py:216
  39.0 0.0 copy-done
  39.0 0.0 copy-done.1
  39.0 0.0 copy-done.2
  39.0 0.0 copy-done.3
  39.1 0.8 shard_map.71
  39.9 15.1 %all_to_all.86 = f32[128,4,128]{2,1,0:T(4,128)S(1)} all-to-all(f32[128,4,128]{2,1,0:T(4,128)S(1)} %bitcast.73), channel_id=1, replica_groups=mesh['row'=8,'col'=16] {'row','col'}, dimensions={0} | all-to-all | bytes 524288 | tf_op jit(solution)/shard_map/all_to_all | solution.py:216
  55.0 0.8 shard_map.72
  55.8 15.1 %all_to_all.87 = f32[128,4,128]{2,1,0:T(4,128)S(1)} all-to-all(f32[128,4,128]{2,1,0:T(4,128)S(1)} %bitcast.59), channel_id=1, replica_groups=mesh['row'=8,'col'=16] {'row','col'}, dimensions={0} | all-to-all | bytes 524288 | tf_op jit(solution)/shard_map/all_to_all | solution.py:216
  71.0 0.8 shard_map.73
  71.8 15.1 %all_to_all.88 = f32[128,4,128]{2,1,0:T(4,128)S(1)} all-to-all(f32[128,4,128]{2,1,0:T(4,128)S(1)} %bitcast.60), channel_id=1, replica_groups=mesh['row'=8,'col'=16] {'row','col'}, dimensions={0} | all-to-all | bytes 524288 | tf_op jit(solution)/shard_map/all_to_all | solution.py:216
  86.9 0.8 shard_map.74
  87.7 15.1 %all_to_all.89 = f32[128,4,128]{2,1,0:T(4,128)S(1)} all-to-all(f32[128,4,128]{2,1,0:T(4,128)S(1)} %bitcast.61), channel_id=1, replica_groups=mesh['row'=8,'col'=16] {'row','col'}, dimensions={0} | all-to-all | bytes 524288 | tf_op jit(solution)/shard_map/all_to_all | solution.py:216
  102.9 0.8 shard_map.75
  103.7 15.1 %all_to_all.90 = f32[128,4,128]{2,1,0:T(4,128)S(1)} all-to-all(f32[128,4,128]{2,1,0:T(4,128)S(1)} %bitcast.62), channel_id=1, replica_groups=mesh['row'=8,'col'=16] {'row','col'}, dimensions={0} | all-to-all | bytes 524288 | tf_op jit(solution)/shard_map/all_to_all | solution.py:216
  118.8 0.8 shard_map.76
  119.7 15.1 %all_to_all.91 = f32[128,4,128]{2,1,0:T(4,128)S(1)} all-to-all(f32[128,4,128]{2,1,0:T(4,128)S(1)} %bitcast.63), channel_id=1, replica_groups=mesh['row'=8,'col'=16] {'row','col'}, dimensions={0} | all-to-all | bytes 524288 | tf_op jit(solution)/shard_map/all_to_all | solution.py:216
  134.8 0.8 shard_map.77
  135.6 15.1 %all_to_all.92 = f32[128,4,128]{2,1,0:T(4,128)S(1)} all-to-all(f32[128,4,128]{2,1,0:T(4,128)S(1)} %bitcast.64), channel_id=1, replica_groups=mesh['row'=8,'col'=16] {'row','col'}, dimensions={0} | all-to-all | bytes 524288 | tf_op jit(solution)/shard_map/all_to_all | solution.py:216
  150.7 0.8 shard_map.78
  151.6 15.1 %all_to_all.93 = f32[128,4,128]{2,1,0:T(4,128)S(1)} all-to-all(f32[128,4,128]{2,1,0:T(4,128)S(1)} %bitcast.65), channel_id=1, replica_groups=mesh['row'=8,'col'=16] {'row','col'}, dimensions={0} | all-to-all | bytes 524288 | tf_op jit(solution)/shard_map/all_to_all | solution.py:216
  166.7 0.8 shard_map.79
  167.5 15.1 %all_to_all.94 = f32[128,4,128]{2,1,0:T(4,128)S(1)} all-to-all(f32[128,4,128]{2,1,0:T(4,128)S(1)} %bitcast.66), channel_id=1, replica_groups=mesh['row'=8,'col'=16] {'row','col'}, dimensions={0} | all-to-all | bytes 524288 | tf_op jit(solution)/shard_map/all_to_all | solution.py:216
  182.7 0.8 shard_map.80
  183.5 15.1 %all_to_all.95 = f32[128,4,128]{2,1,0:T(4,128)S(1)} all-to-all(f32[128,4,128]{2,1,0:T(4,128)S(1)} %bitcast.67), channel_id=1, replica_groups=mesh['row'=8,'col'=16] {'row','col'}, dimensions={0} | all-to-all | bytes 524288 | tf_op jit(solution)/shard_map/all_to_all | solution.py:216
  198.6 0.8 shard_map.81
  199.4 15.1 %all_to_all.96 = f32[128,4,128]{2,1,0:T(4,128)S(1)} all-to-all(f32[128,4,128]{2,1,0:T(4,128)S(1)} %bitcast.68), channel_id=1, replica_groups=mesh['row'=8,'col'=16] {'row','col'}, dimensions={0} | all-to-all | bytes 524288 | tf_op jit(solution)/shard_map/all_to_all | solution.py:216
  214.6 0.8 shard_map.82
  215.4 15.1 %all_to_all.97 = f32[128,4,128]{2,1,0:T(4,128)S(1)} all-to-all(f32[128,4,128]{2,1,0:T(4,128)S(1)} %bitcast.69), channel_id=1, replica_groups=mesh['row'=8,'col'=16] {'row','col'}, dimensions={0} | all-to-all | bytes 524288 | tf_op jit(solution)/shard_map/all_to_all | solution.py:216
  230.5 0.8 shard_map.83
  231.3 15.1 %all_to_all.98 = f32[128,4,128]{2,1,0:T(4,128)S(1)} all-to-all(f32[128,4,128]{2,1,0:T(4,128)S(1)} %bitcast.70), channel_id=1, replica_groups=mesh['row'=8,'col'=16] {'row','col'}, dimensions={0} | all-to-all | bytes 524288 | tf_op jit(solution)/shard_map/all_to_all | solution.py:216
  246.5 0.8 shard_map.84
  247.3 15.1 %all_to_all.99 = f32[128,4,128]{2,1,0:T(4,128)S(1)} all-to-all(f32[128,4,128]{2,1,0:T(4,128)S(1)} %bitcast.71), channel_id=1, replica_groups=mesh['row'=8,'col'=16] {'row','col'}, dimensions={0} | all-to-all | bytes 524288 | tf_op jit(solution)/shard_map/all_to_all | solution.py:216
  262.4 0.8 shard_map.85
  263.3 15.1 %all_to_all.100 = f32[128,4,128]{2,1,0:T(4,128)S(1)} all-to-all(f32[128,4,128]{2,1,0:T(4,128)S(1)} %bitcast.72), channel_id=1, replica_groups=mesh['row'=8,'col'=16] {'row','col'}, dimensions={0} | all-to-all | bytes 524288 | tf_op jit(solution)/shard_map/all_to_all | solution.py:216
  278.4 1.3 shard_map.86
  (1 shorter events, 0.0 us)
Async XLA Ops:
  0.6 0.7 copy-start.4
  2.0 21.3 %all-to-all-start = ((s32[128,1,128]{2,1,0:T(1,128)}), s32[128,1,128]{2,1,0:T(1,128)S(1)}, u32[]{:S(2)}, u32[]{:S(2)}) async-start(s32[128,1,128]{2,1,0:T(1,128)} %bitcast.3), calls=%async_computation | async-start | bytes 131072 | tf_op jit(solution)/shard_map/all_to_all | solution.py:167
  23.3 15.7 %copy-start = (bf16[56,256,128]{2,1,0:T(8,128)(2,1)S(1)}, bf16[56,256,128]{2,1,0:T(8,128)(2,1)}, u32[]{:S(2)}) copy-start(bf16[56,256,128]{2,1,0:T(8,128)(2,1)} %get-tuple-element.70.refs_1_) | copy-start | bytes 11010052
  23.3 15.7 %copy-start.1 = (f32[8,128,128]{2,1,0:T(8,128)S(1)}, f32[8,128,128]{2,1,0:T(8,128)}, u32[]{:S(2)}) copy-start(f32[8,128,128]{2,1,0:T(8,128)} %get-tuple-element.71.refs_2_) | copy-start | bytes 1572868
  23.3 15.7 %copy-start.2 = (f32[32,128]{1,0:T(8,128)S(1)}, f32[32,128]{1,0:T(8,128)}, u32[]{:S(2)}) copy-start(f32[32,128]{1,0:T(8,128)} %refs_5_.31) | copy-start | bytes 49156
  23.3 15.7 %copy-start.3 = (f32[32,128]{1,0:T(8,128)S(1)}, f32[32,128]{1,0:T(8,128)}, u32[]{:S(2)}) copy-start(f32[32,128]{1,0:T(8,128)} %refs_7_.1) | copy-start | bytes 49156

commit v8 on v7

--- a/solution.py
+++ b/solution.py
@@ -113,9 +113,9 @@
     send_ref[...] = to_send(pick, direction_ref[...])
 
 
-def step_kernel(keep, gain, first, last, *refs):
+def step_kernel(keep, gain, last, *refs):
     got_ref, held_ref, plain_ref, place_ref, pick_ref, diag_ref, direction_ref, residual_ref = refs[:8]
-    out_refs = refs[8:] if first else refs[9:]
+    out_refs = refs[8:] if last else refs[9:]
     senders, wanted, order = got_ref.shape
     vec = got_ref[0]
     for sender in range(1, senders):
@@ -141,12 +141,12 @@
             off = off + place_ref[8 * block + slot] * row
     direction = direction_ref[...]
     residual = residual_ref[...] - (diag_ref[...] * direction - off)
-    out_refs[0][...] = direction if first else refs[8][...] + direction
-    out_refs[1][...] = residual
+    out_refs[0][...] = residual
     if not last:
         direction = keep * direction + gain * residual
-        out_refs[2][...] = direction
-        out_refs[3][...] = to_send(pick_ref[...], direction)
+        out_refs[1][...] = direction
+        out_refs[2][...] = to_send(pick_ref[...], direction)
+        out_refs[3][...] = refs[8][...] + direction
 
 
 def per_device(rhs, diag_vals, tiles, tile_row, tile_col):
@@ -210,21 +210,21 @@
         compiler_params=pltpu.CompilerParams(vmem_limit_bytes=16 * MIB),
     )(want, mine, direction)
 
-    pressure, residual = [], rhs
+    pressure, residual = direction, rhs
     for index, (keep, gain) in enumerate(steps()):
-        first, last = index == 0, index == ITERS - 1
+        last = index == ITERS - 1
         got = lax.all_to_all(send.reshape(devices, slots, order), BOTH, 0, 0, tiled=True)
         outs = pl.pallas_call(
-            functools.partial(step_kernel, keep, gain, first, last),
-            in_specs=[VMEM] * (8 if first else 9),
-            out_specs=[VMEM] * (2 if last else 4),
-            out_shape=[small, small] if last else [small, small, small, jax.ShapeDtypeStruct((devices * slots, order), f32)],
+            functools.partial(step_kernel, keep, gain, last),
+            in_specs=[VMEM] * (8 if last else 9),
+            out_specs=[VMEM] * (1 if last else 4),
+            out_shape=[small] if last else [small, small, jax.ShapeDtypeStruct((devices * slots, order), f32), small],
             compiler_params=pltpu.CompilerParams(vmem_limit_bytes=16 * MIB),
-        )(got.reshape(senders, wanted, order), held, plain, place, pick, diag_vals, direction, residual, *pressure)
-        pressure, residual = [outs[0]], outs[1]
+        )(got.reshape(senders, wanted, order), held, plain, place, pick, diag_vals, direction, residual, *([] if last else [pressure]))
+        residual = outs[0]
         if not last:
-            direction, send = outs[2:]
-    return (pressure[0], residual)
+            direction, send, pressure = outs[1:]
+    return (pressure, residual)
 
 
 def solution(mesh):

time: 280 us -> 281 us (level)
  no operation moved by 1% of the time
where the time goes in v8:
time: 281 us; the launch traced here: 280 us
  blocking collectives  242 us (86%)
  Pallas kernels  18.7 us (7%)
  starting transfers between devices  11.5 us (4%)
  waiting for transfers between devices  6.07 us (2%)
    all_to_all x16, blocking collectives, per_device(): lax.all_to_all(send.reshape(devices, slots, order), BOTH, 0, 0, tiled=True)  242 us
    pallas_call x16, Pallas kernels, per_device(): pl.pallas_call(functools.partial(step_kernel, keep, gain, last), in_specs...  13.9 us
    all_to_all x1, starting transfers between devices, per_device(): want = lax.all_to_all(asked[:, None], BOTH, 0, 0, tiled=True)[:, 0]  11.5 us
    all_to_all x1, waiting for transfers between devices, per_device(): want = lax.all_to_all(asked[:, None], BOTH, 0, 0, tiled=True)[:, 0]  6.07 us
  transfers between devices with their start and end apart: 1, of which 1 were waited for; matrix products, arithmetic and copies ran while one was open for 0% of the time, Pallas kernels for 1%

profile of v8, /device:TPU:1, one launch (start us, length us, event | category | flops | bytes accessed | tf_op | source)
XLA Modules:
  0.0 280.1 jit_solution(3165686911584591517)
XLA Ops:
  0.6 0.0 copy-start.4
  0.6 0.7 copy-done.4
  1.3 0.7 shard_map.68
  2.0 11.5 %all-to-all-start = ((s32[128,1,128]{2,1,0:T(1,128)}), s32[128,1,128]{2,1,0:T(1,128)S(1)}, u32[]{:S(2)}, u32[]{:S(2)}) async-start(s32[128,1,128]{2,1,0:T(1,128)} %bitcast.3), calls=%async_computation | async-start | bytes 131072 | tf_op jit(solution)/shard_map/all_to_all | solution.py:167
  13.5 3.7 %shard_map.69 = (bf16[56,256,128]{2,1,0:T(8,128)(2,1)}, f32[8,128,128]{2,1,0:T(8,128)}, f32[64,32,128]{2,1,0:T(8,128)S(1)}, f32[32,128]{1,0:T(8,128)S(1)}) custom-call(f32[64,128,128]{2,1,0:T(8,128)} %bitcast.77, s32[4,16]{1,0:T(4,128)} %bitcast.78, f32[32,128]{1,0:T(8,128)} %refs_7_.1, s32[1,128]{1,0:T(1,128)S(1)} %compare_select_fusion.mine_ref), custom_call_target="tpu_custom_call" | custom-call | tf_op jit(solution)/shard_map/pallas_call | solution.py:176
  17.3 6.1 %all-to-all-done = s32[128,1,128]{2,1,0:T(1,128)S(1)} async-done(((s32[128,1,128]{2,1,0:T(1,128)}), s32[128,1,128]{2,1,0:T(1,128)S(1)}, u32[]{:S(2)}, u32[]{:S(2)}) %all-to-all-start) | async-done | bytes 65568 | tf_op jit(solution)/shard_map/all_to_all | solution.py:167
  23.3 0.0 copy-start
  23.3 0.0 copy-start.1
  23.3 0.0 copy-start.2
  23.3 0.0 copy-start.3
  23.3 0.3 shard_map.70
  23.7 15.4 %all_to_all.85 = f32[128,4,128]{2,1,0:T(4,128)S(1)} all-to-all(f32[128,4,128]{2,1,0:T(4,128)S(1)} %bitcast.74), channel_id=1, replica_groups=mesh['row'=8,'col'=16] {'row','col'}, dimensions={0} | all-to-all | bytes 524288 | tf_op jit(solution)/shard_map/all_to_all | solution.py:216
  39.0 0.0 copy-done
  39.0 0.0 copy-done.1
  39.0 0.0 copy-done.2
  39.0 0.0 copy-done.3
  39.1 0.8 shard_map.71
  39.9 15.1 %all_to_all.86 = f32[128,4,128]{2,1,0:T(4,128)S(1)} all-to-all(f32[128,4,128]{2,1,0:T(4,128)S(1)} %bitcast.73), channel_id=1, replica_groups=mesh['row'=8,'col'=16] {'row','col'}, dimensions={0} | all-to-all | bytes 524288 | tf_op jit(solution)/shard_map/all_to_all | solution.py:216
  55.0 0.8 shard_map.72
  55.8 15.1 %all_to_all.87 = f32[128,4,128]{2,1,0:T(4,128)S(1)} all-to-all(f32[128,4,128]{2,1,0:T(4,128)S(1)} %bitcast.59), channel_id=1, replica_groups=mesh['row'=8,'col'=16] {'row','col'}, dimensions={0} | all-to-all | bytes 524288 | tf_op jit(solution)/shard_map/all_to_all | solution.py:216
  71.0 0.8 shard_map.73
  71.8 15.1 %all_to_all.88 = f32[128,4,128]{2,1,0:T(4,128)S(1)} all-to-all(f32[128,4,128]{2,1,0:T(4,128)S(1)} %bitcast.60), channel_id=1, replica_groups=mesh['row'=8,'col'=16] {'row','col'}, dimensions={0} | all-to-all | bytes 524288 | tf_op jit(solution)/shard_map/all_to_all | solution.py:216
  86.9 0.8 shard_map.74
  87.7 15.1 %all_to_all.89 = f32[128,4,128]{2,1,0:T(4,128)S(1)} all-to-all(f32[128,4,128]{2,1,0:T(4,128)S(1)} %bitcast.61), channel_id=1, replica_groups=mesh['row'=8,'col'=16] {'row','col'}, dimensions={0} | all-to-all | bytes 524288 | tf_op jit(solution)/shard_map/all_to_all | solution.py:216
  102.9 0.8 shard_map.75
  103.7 15.1 %all_to_all.90 = f32[128,4,128]{2,1,0:T(4,128)S(1)} all-to-all(f32[128,4,128]{2,1,0:T(4,128)S(1)} %bitcast.62), channel_id=1, replica_groups=mesh['row'=8,'col'=16] {'row','col'}, dimensions={0} | all-to-all | bytes 524288 | tf_op jit(solution)/shard_map/all_to_all | solution.py:216
  118.8 0.8 shard_map.76
  119.7 15.1 %all_to_all.91 = f32[128,4,128]{2,1,0:T(4,128)S(1)} all-to-all(f32[128,4,128]{2,1,0:T(4,128)S(1)} %bitcast.63), channel_id=1, replica_groups=mesh['row'=8,'col'=16] {'row','col'}, dimensions={0} | all-to-all | bytes 524288 | tf_op jit(solution)/shard_map/all_to_all | solution.py:216
  134.8 0.8 shard_map.77
  135.6 15.1 %all_to_all.92 = f32[128,4,128]{2,1,0:T(4,128)S(1)} all-to-all(f32[128,4,128]{2,1,0:T(4,128)S(1)} %bitcast.64), channel_id=1, replica_groups=mesh['row'=8,'col'=16] {'row','col'}, dimensions={0} | all-to-all | bytes 524288 | tf_op jit(solution)/shard_map/all_to_all | solution.py:216
  150.7 0.8 shard_map.78
  151.6 15.1 %all_to_all.93 = f32[128,4,128]{2,1,0:T(4,128)S(1)} all-to-all(f32[128,4,128]{2,1,0:T(4,128)S(1)} %bitcast.65), channel_id=1, replica_groups=mesh['row'=8,'col'=16] {'row','col'}, dimensions={0} | all-to-all | bytes 524288 | tf_op jit(solution)/shard_map/all_to_all | solution.py:216
  166.7 0.8 shard_map.79
  167.5 15.1 %all_to_all.94 = f32[128,4,128]{2,1,0:T(4,128)S(1)} all-to-all(f32[128,4,128]{2,1,0:T(4,128)S(1)} %bitcast.66), channel_id=1, replica_groups=mesh['row'=8,'col'=16] {'row','col'}, dimensions={0} | all-to-all | bytes 524288 | tf_op jit(solution)/shard_map/all_to_all | solution.py:216
  182.7 0.8 shard_map.80
  183.5 15.1 %all_to_all.95 = f32[128,4,128]{2,1,0:T(4,128)S(1)} all-to-all(f32[128,4,128]{2,1,0:T(4,128)S(1)} %bitcast.67), channel_id=1, replica_groups=mesh['row'=8,'col'=16] {'row','col'}, dimensions={0} | all-to-all | bytes 524288 | tf_op jit(solution)/shard_map/all_to_all | solution.py:216
  198.6 0.8 shard_map.81
  199.4 15.1 %all_to_all.96 = f32[128,4,128]{2,1,0:T(4,128)S(1)} all-to-all(f32[128,4,128]{2,1,0:T(4,128)S(1)} %bitcast.68), channel_id=1, replica_groups=mesh['row'=8,'col'=16] {'row','col'}, dimensions={0} | all-to-all | bytes 524288 | tf_op jit(solution)/shard_map/all_to_all | solution.py:216
  214.6 0.8 shard_map.82
  215.4 15.1 %all_to_all.97 = f32[128,4,128]{2,1,0:T(4,128)S(1)} all-to-all(f32[128,4,128]{2,1,0:T(4,128)S(1)} %bitcast.69), channel_id=1, replica_groups=mesh['row'=8,'col'=16] {'row','col'}, dimensions={0} | all-to-all | bytes 524288 | tf_op jit(solution)/shard_map/all_to_all | solution.py:216
  230.5 0.8 shard_map.83
  231.3 15.1 %all_to_all.98 = f32[128,4,128]{2,1,0:T(4,128)S(1)} all-to-all(f32[128,4,128]{2,1,0:T(4,128)S(1)} %bitcast.70), channel_id=1, replica_groups=mesh['row'=8,'col'=16] {'row','col'}, dimensions={0} | all-to-all | bytes 524288 | tf_op jit(solution)/shard_map/all_to_all | solution.py:216
  246.5 0.8 shard_map.84
  247.3 15.1 %all_to_all.99 = f32[128,4,128]{2,1,0:T(4,128)S(1)} all-to-all(f32[128,4,128]{2,1,0:T(4,128)S(1)} %bitcast.71), channel_id=1, replica_groups=mesh['row'=8,'col'=16] {'row','col'}, dimensions={0} | all-to-all | bytes 524288 | tf_op jit(solution)/shard_map/all_to_all | solution.py:216
  262.4 1.3 shard_map.85
  263.7 15.1 %all_to_all.100 = f32[128,4,128]{2,1,0:T(4,128)S(1)} all-to-all(f32[128,4,128]{2,1,0:T(4,128)S(1)} %bitcast.72), channel_id=1, replica_groups=mesh['row'=8,'col'=16] {'row','col'}, dimensions={0} | all-to-all | bytes 524288 | tf_op jit(solution)/shard_map/all_to_all | solution.py:216
  278.8 1.3 shard_map.86
  (1 shorter events, 0.0 us)
Async XLA Ops:
  0.6 0.7 copy-start.4
  2.0 21.3 %all-to-all-start = ((s32[128,1,128]{2,1,0:T(1,128)}), s32[128,1,128]{2,1,0:T(1,128)S(1)}, u32[]{:S(2)}, u32[]{:S(2)}) async-start(s32[128,1,128]{2,1,0:T(1,128)} %bitcast.3), calls=%async_computation | async-start | bytes 131072 | tf_op jit(solution)/shard_map/all_to_all | solution.py:167
  23.3 15.7 %copy-start = (bf16[56,256,128]{2,1,0:T(8,128)(2,1)S(1)}, bf16[56,256,128]{2,1,0:T(8,128)(2,1)}, u32[]{:S(2)}) copy-start(bf16[56,256,128]{2,1,0:T(8,128)(2,1)} %get-tuple-element.70.refs_1_) | copy-start | bytes 11010052
  23.3 15.7 %copy-start.1 = (f32[8,128,128]{2,1,0:T(8,128)S(1)}, f32[8,128,128]{2,1,0:T(8,128)}, u32[]{:S(2)}) copy-start(f32[8,128,128]{2,1,0:T(8,128)} %get-tuple-element.71.refs_2_) | copy-start | bytes 1572868
  23.3 15.7 %copy-start.2 = (f32[32,128]{1,0:T(8,128)S(1)}, f32[32,128]{1,0:T(8,128)}, u32[]{:S(2)}) copy-start(f32[32,128]{1,0:T(8,128)} %refs_5_.31) | copy-start | bytes 49156
  23.3 15.7 %copy-start.3 = (f32[32,128]{1,0:T(8,128)S(1)}, f32[32,128]{1,0:T(8,128)}, u32[]{:S(2)}) copy-start(f32[32,128]{1,0:T(8,128)} %refs_7_.1) | copy-start | bytes 49156

commit v9 on v7

--- a/solution.py
+++ b/solution.py
@@ -69,10 +69,10 @@
         fetches[c].wait()
         for spot in range(size):
             flipped = tile_buf[c * size + spot].T
-            if spot < PLAIN:
-                plain_buf[c * PLAIN + spot] = flipped
+            if spot >= size - PLAIN:
+                plain_buf[c * PLAIN + spot - (size - PLAIN)] = flipped
             else:
-                tile = c * (size - PLAIN) + spot - PLAIN
+                tile = c * (size - PLAIN) + spot
                 high = flipped.astype(jnp.bfloat16)
                 held_buf[tile, :order] = high
                 held_buf[tile, order:] = (flipped - high.astype(jnp.float32)).astype(jnp.bfloat16)
@@ -129,14 +129,14 @@
         left = jnp.concatenate([high[rows], low[rows]], axis=0).astype(jnp.bfloat16)
         left = jnp.concatenate([left, left], axis=1)
         for slot in range(8):
-            if slot < PLAIN:
+            if slot >= 8 - PLAIN:
                 tile = 8 * block + slot
                 row = jnp.zeros((8, order), jnp.float32)
                 for part in range(0, order, 8):
-                    row = row + plain_ref[PLAIN * block + slot, part : part + 8] * column[part : part + 8, tile : tile + 1]
+                    row = row + plain_ref[PLAIN * block + slot - (8 - PLAIN), part : part + 8] * column[part : part + 8, tile : tile + 1]
                 row = jnp.sum(row, axis=0, keepdims=True)
             else:
-                out = jnp.dot(left, held_ref[(8 - PLAIN) * block + slot - PLAIN], preferred_element_type=jnp.float32)
+                out = jnp.dot(left, held_ref[(8 - PLAIN) * block + slot], preferred_element_type=jnp.float32)
                 row = out[slot : slot + 1] + out[8 + slot : 9 + slot]
             off = off + place_ref[8 * block + slot] * row
     direction = direction_ref[...]

time: 280 us -> 280 us (level)
  no operation moved by 1% of the time
where the time goes in v9:
time: 280 us
  blocking collectives  242 us (86%)
  Pallas kernels  18.2 us (6%)
  starting transfers between devices  11.5 us (4%)
  waiting for transfers between devices  6.08 us (2%)
    all_to_all x16, blocking collectives, per_device(): lax.all_to_all(send.reshape(devices, slots, order), BOTH, 0, 0, tiled=True)  242 us
    pallas_call x16, Pallas kernels, per_device(): pl.pallas_call(functools.partial(step_kernel, keep, gain, first, last), i...  13.5 us
    all_to_all x1, starting transfers between devices, per_device(): want = lax.all_to_all(asked[:, None], BOTH, 0, 0, tiled=True)[:, 0]  11.5 us
    all_to_all x1, waiting for transfers between devices, per_device(): want = lax.all_to_all(asked[:, None], BOTH, 0, 0, tiled=True)[:, 0]  6.08 us
  transfers between devices with their start and end apart: 1, of which 1 were waited for; matrix products, arithmetic and copies ran while one was open for 0% of the time, Pallas kernels for 1%

profile of v9, /device:TPU:1, one launch (start us, length us, event | category | flops | bytes accessed | tf_op | source)
XLA Modules:
  0.0 279.7 jit_solution(4965033979534719561)
XLA Ops:
  0.6 0.0 copy-start.4
  0.6 0.7 copy-done.4
  1.3 0.7 shard_map.68
  2.0 11.5 %all-to-all-start = ((s32[128,1,128]{2,1,0:T(1,128)}), s32[128,1,128]{2,1,0:T(1,128)S(1)}, u32[]{:S(2)}, u32[]{:S(2)}) async-start(s32[128,1,128]{2,1,0:T(1,128)} %bitcast.3), calls=%async_computation | async-start | bytes 131072 | tf_op jit(solution)/shard_map/all_to_all | solution.py:167
  13.5 3.7 %shard_map.69 = (bf16[56,256,128]{2,1,0:T(8,128)(2,1)}, f32[8,128,128]{2,1,0:T(8,128)}, f32[64,32,128]{2,1,0:T(8,128)S(1)}, f32[32,128]{1,0:T(8,128)S(1)}) custom-call(f32[64,128,128]{2,1,0:T(8,128)} %bitcast.77, s32[4,16]{1,0:T(4,128)} %bitcast.78, f32[32,128]{1,0:T(8,128)} %refs_7_.1, s32[1,128]{1,0:T(1,128)S(1)} %compare_select_fusion.mine_ref), custom_call_target="tpu_custom_call" | custom-call | tf_op jit(solution)/shard_map/pallas_call | solution.py:176
  17.3 6.1 %all-to-all-done = s32[128,1,128]{2,1,0:T(1,128)S(1)} async-done(((s32[128,1,128]{2,1,0:T(1,128)}), s32[128,1,128]{2,1,0:T(1,128)S(1)}, u32[]{:S(2)}, u32[]{:S(2)}) %all-to-all-start) | async-done | bytes 65568 | tf_op jit(solution)/shard_map/all_to_all | solution.py:167
  23.3 0.0 copy-start
  23.3 0.0 copy-start.1
  23.3 0.0 copy-start.2
  23.3 0.0 copy-start.3
  23.3 0.3 shard_map.70
  23.7 15.4 %all_to_all.85 = f32[128,4,128]{2,1,0:T(4,128)S(1)} all-to-all(f32[128,4,128]{2,1,0:T(4,128)S(1)} %bitcast.74), channel_id=1, replica_groups=mesh['row'=8,'col'=16] {'row','col'}, dimensions={0} | all-to-all | bytes 524288 | tf_op jit(solution)/shard_map/all_to_all | solution.py:216
  39.0 0.0 copy-done
  39.0 0.0 copy-done.1
  39.0 0.0 copy-done.2
  39.0 0.0 copy-done.3
  39.1 0.8 shard_map.71
  39.9 15.1 %all_to_all.86 = f32[128,4,128]{2,1,0:T(4,128)S(1)} all-to-all(f32[128,4,128]{2,1,0:T(4,128)S(1)} %bitcast.73), channel_id=1, replica_groups=mesh['row'=8,'col'=16] {'row','col'}, dimensions={0} | all-to-all | bytes 524288 | tf_op jit(solution)/shard_map/all_to_all | solution.py:216
  55.0 0.8 shard_map.72
  55.8 15.1 %all_to_all.87 = f32[128,4,128]{2,1,0:T(4,128)S(1)} all-to-all(f32[128,4,128]{2,1,0:T(4,128)S(1)} %bitcast.59), channel_id=1, replica_groups=mesh['row'=8,'col'=16] {'row','col'}, dimensions={0} | all-to-all | bytes 524288 | tf_op jit(solution)/shard_map/all_to_all | solution.py:216
  71.0 0.8 shard_map.73
  71.8 15.1 %all_to_all.88 = f32[128,4,128]{2,1,0:T(4,128)S(1)} all-to-all(f32[128,4,128]{2,1,0:T(4,128)S(1)} %bitcast.60), channel_id=1, replica_groups=mesh['row'=8,'col'=16] {'row','col'}, dimensions={0} | all-to-all | bytes 524288 | tf_op jit(solution)/shard_map/all_to_all | solution.py:216
  86.9 0.8 shard_map.74
  87.8 15.1 %all_to_all.89 = f32[128,4,128]{2,1,0:T(4,128)S(1)} all-to-all(f32[128,4,128]{2,1,0:T(4,128)S(1)} %bitcast.61), channel_id=1, replica_groups=mesh['row'=8,'col'=16] {'row','col'}, dimensions={0} | all-to-all | bytes 524288 | tf_op jit(solution)/shard_map/all_to_all | solution.py:216
  102.9 0.8 shard_map.75
  103.7 15.1 %all_to_all.90 = f32[128,4,128]{2,1,0:T(4,128)S(1)} all-to-all(f32[128,4,128]{2,1,0:T(4,128)S(1)} %bitcast.62), channel_id=1, replica_groups=mesh['row'=8,'col'=16] {'row','col'}, dimensions={0} | all-to-all | bytes 524288 | tf_op jit(solution)/shard_map/all_to_all | solution.py:216
  118.8 0.8 shard_map.76
  119.7 15.1 %all_to_all.91 = f32[128,4,128]{2,1,0:T(4,128)S(1)} all-to-all(f32[128,4,128]{2,1,0:T(4,128)S(1)} %bitcast.63), channel_id=1, replica_groups=mesh['row'=8,'col'=16] {'row','col'}, dimensions={0} | all-to-all | bytes 524288 | tf_op jit(solution)/shard_map/all_to_all | solution.py:216
  134.8 0.8 shard_map.77
  135.6 15.1 %all_to_all.92 = f32[128,4,128]{2,1,0:T(4,128)S(1)} all-to-all(f32[128,4,128]{2,1,0:T(4,128)S(1)} %bitcast.64), channel_id=1, replica_groups=mesh['row'=8,'col'=16] {'row','col'}, dimensions={0} | all-to-all | bytes 524288 | tf_op jit(solution)/shard_map/all_to_all | solution.py:216
  150.8 0.8 shard_map.78
  151.6 15.1 %all_to_all.93 = f32[128,4,128]{2,1,0:T(4,128)S(1)} all-to-all(f32[128,4,128]{2,1,0:T(4,128)S(1)} %bitcast.65), channel_id=1, replica_groups=mesh['row'=8,'col'=16] {'row','col'}, dimensions={0} | all-to-all | bytes 524288 | tf_op jit(solution)/shard_map/all_to_all | solution.py:216
  166.7 0.8 shard_map.79
  167.5 15.1 %all_to_all.94 = f32[128,4,128]{2,1,0:T(4,128)S(1)} all-to-all(f32[128,4,128]{2,1,0:T(4,128)S(1)} %bitcast.66), channel_id=1, replica_groups=mesh['row'=8,'col'=16] {'row','col'}, dimensions={0} | all-to-all | bytes 524288 | tf_op jit(solution)/shard_map/all_to_all | solution.py:216
  182.7 0.8 shard_map.80
  183.5 15.1 %all_to_all.95 = f32[128,4,128]{2,1,0:T(4,128)S(1)} all-to-all(f32[128,4,128]{2,1,0:T(4,128)S(1)} %bitcast.67), channel_id=1, replica_groups=mesh['row'=8,'col'=16] {'row','col'}, dimensions={0} | all-to-all | bytes 524288 | tf_op jit(solution)/shard_map/all_to_all | solution.py:216
  198.6 0.8 shard_map.81
  199.4 15.1 %all_to_all.96 = f32[128,4,128]{2,1,0:T(4,128)S(1)} all-to-all(f32[128,4,128]{2,1,0:T(4,128)S(1)} %bitcast.68), channel_id=1, replica_groups=mesh['row'=8,'col'=16] {'row','col'}, dimensions={0} | all-to-all | bytes 524288 | tf_op jit(solution)/shard_map/all_to_all | solution.py:216
  214.6 0.8 shard_map.82
  215.4 15.1 %all_to_all.97 = f32[128,4,128]{2,1,0:T(4,128)S(1)} all-to-all(f32[128,4,128]{2,1,0:T(4,128)S(1)} %bitcast.69), channel_id=1, replica_groups=mesh['row'=8,'col'=16] {'row','col'}, dimensions={0} | all-to-all | bytes 524288 | tf_op jit(solution)/shard_map/all_to_all | solution.py:216
  230.5 0.8 shard_map.83
  231.4 15.1 %all_to_all.98 = f32[128,4,128]{2,1,0:T(4,128)S(1)} all-to-all(f32[128,4,128]{2,1,0:T(4,128)S(1)} %bitcast.70), channel_id=1, replica_groups=mesh['row'=8,'col'=16] {'row','col'}, dimensions={0} | all-to-all | bytes 524288 | tf_op jit(solution)/shard_map/all_to_all | solution.py:216
  246.5 0.8 shard_map.84
  247.3 15.1 %all_to_all.99 = f32[128,4,128]{2,1,0:T(4,128)S(1)} all-to-all(f32[128,4,128]{2,1,0:T(4,128)S(1)} %bitcast.71), channel_id=1, replica_groups=mesh['row'=8,'col'=16] {'row','col'}, dimensions={0} | all-to-all | bytes 524288 | tf_op jit(solution)/shard_map/all_to_all | solution.py:216
  262.4 0.8 shard_map.85
  263.3 15.1 %all_to_all.100 = f32[128,4,128]{2,1,0:T(4,128)S(1)} all-to-all(f32[128,4,128]{2,1,0:T(4,128)S(1)} %bitcast.72), channel_id=1, replica_groups=mesh['row'=8,'col'=16] {'row','col'}, dimensions={0} | all-to-all | bytes 524288 | tf_op jit(solution)/shard_map/all_to_all | solution.py:216
  278.4 1.3 shard_map.86
  (1 shorter events, 0.0 us)
Async XLA Ops:
  0.6 0.7 copy-start.4
  2.0 21.3 %all-to-all-start = ((s32[128,1,128]{2,1,0:T(1,128)}), s32[128,1,128]{2,1,0:T(1,128)S(1)}, u32[]{:S(2)}, u32[]{:S(2)}) async-start(s32[128,1,128]{2,1,0:T(1,128)} %bitcast.3), calls=%async_computation | async-start | bytes 131072 | tf_op jit(solution)/shard_map/all_to_all | solution.py:167
  23.3 15.7 %copy-start = (bf16[56,256,128]{2,1,0:T(8,128)(2,1)S(1)}, bf16[56,256,128]{2,1,0:T(8,128)(2,1)}, u32[]{:S(2)}) copy-start(bf16[56,256,128]{2,1,0:T(8,128)(2,1)} %get-tuple-element.70.refs_1_) | copy-start | bytes 11010052
  23.3 15.7 %copy-start.1 = (f32[8,128,128]{2,1,0:T(8,128)S(1)}, f32[8,128,128]{2,1,0:T(8,128)}, u32[]{:S(2)}) copy-start(f32[8,128,128]{2,1,0:T(8,128)} %get-tuple-element.71.refs_2_) | copy-start | bytes 1572868
  23.3 15.7 %copy-start.2 = (f32[32,128]{1,0:T(8,128)S(1)}, f32[32,128]{1,0:T(8,128)}, u32[]{:S(2)}) copy-start(f32[32,128]{1,0:T(8,128)} %refs_5_.31) | copy-start | bytes 49156
  23.3 15.7 %copy-start.3 = (f32[32,128]{1,0:T(8,128)S(1)}, f32[32,128]{1,0:T(8,128)}, u32[]{:S(2)}) copy-start(f32[32,128]{1,0:T(8,128)} %refs_7_.1) | copy-start | bytes 49156
